TPU v7x, 32 devices: a whole 2x2x4 slice. The times are simulated.
32 devices in a mesh: wide: 8 (over y, x, core), narrow: 4 (over z).
Axes of the slice: x: 2, y: 2, z: 4, core: 2. Of those that a mesh axis runs over, the one named last changes fastest.
Arguments:
- tokens: bfloat16 [4096, 2048], P(('wide', 'narrow')), may hold values from -6 to 6
- memory: bfloat16 [8192, 2048], P(('wide', 'narrow')), may hold values from -6 to 6
- item_len: int32 [8, 4], P('wide'), may hold values from 1 to 128, 448 in all within a row
- item_kind: int32 [8, 4], P('wide'), may hold values from 0 to 1
- norm_gains: bfloat16 [3, 2048], replicated, may hold values from 0.5 to 1.5
- w_self_in: bfloat16 [2048, 3, 2048], P(('wide', 'narrow')), may hold values from -0.125 to 0.125
- w_self_out: bfloat16 [2048, 2048], P(('wide', 'narrow')), may hold values from -0.75 to 0.75
- w_cross_q: bfloat16 [2048, 2048], P(('wide', 'narrow')), may hold values from -0.125 to 0.125
- w_cross_kv: bfloat16 [2048, 2, 2048], P(('wide', 'narrow')), may hold values from -0.125 to 0.125
- w_cross_out: bfloat16 [2048, 2048], P(('wide', 'narrow')), may hold values from -2 to 2
- w_mlp_in: bfloat16 [5120, 2, 2048], P(('wide', 'narrow')), may hold values from -0.125 to 0.125
- w_mlp_out: bfloat16 [5120, 2048], P(('wide', 'narrow')), may hold values from -0.078125 to 0.078125
- cotangent: bfloat16 [4096, 2048], P(('wide', 'narrow')), may hold values from -6 to 6
Outputs:
- output: bfloat16 [4096, 2048], P(('wide', 'narrow'))
- grad_tokens: bfloat16 [4096, 2048], P(('wide', 'narrow'))
- grad_memory: bfloat16 [8192, 2048], P(('wide', 'narrow'))
- grad_gains: float32 [3, 2048], P(None, 'narrow')
- grad_self_in: float32 [2048, 3, 2048], P('narrow')
- grad_self_out: float32 [2048, 2048], P('narrow')
- grad_cross_q: float32 [2048, 2048], P('narrow')
- grad_cross_kv: float32 [2048, 2, 2048], P('narrow')
- grad_cross_out: float32 [2048, 2048], P('narrow')
- grad_mlp_in: float32 [5120, 2, 2048], P('narrow')
- grad_mlp_out: float32 [5120, 2048], P('narrow')
Inputs may be any that keep to these rules, and one draw needn't show every extreme that they name: `item_len`: in each group the lengths sum to 448 and one item has exactly 128 tokens; the last 64 positions of a group are padding.
All inputs are finite; a program needn't handle non-finite values.
Results may differ from a plain program's by a relative error of at most 0.039.
Values may be sent and summed in bfloat16 or wider, within the bound.
No kernel may reach another device: no remote copies, remote signals or barrier semaphores. Data moves between devices by JAX's collectives and lax.ppermute only.
A program may use at most 512 MiB of HBM per device.

v0:
```python
import jax
import jax.numpy as jnp
from jax import lax
from jax.sharding import PartitionSpec as P

HEAD_DIM = 128


EPSILON = 1e-06
ROBOT_WEIGHT = 2.0
NEGATIVE = -1e30


def normed(values, gain_row):
    factor = lax.rsqrt(jnp.mean(values * values, axis=-1, keepdims=True) + EPSILON)
    return values * factor * gain_row


def token_info(lengths, item_kinds, positions, item_count):
    item_ends = jnp.cumsum(lengths)
    segment = jnp.sum((positions[:, None] >= item_ends[None, :]).astype(jnp.int32), axis=1)
    token_valid = segment < item_count
    item_hit = segment[:, None] == jnp.arange(item_count, dtype=jnp.int32)[None, :]
    robot_flag = jnp.sum(jnp.where(item_hit, item_kinds[None, :], 0), axis=1)
    weight = jnp.where(token_valid, jnp.where(robot_flag == 1, ROBOT_WEIGHT, 1.0), 0.0).astype(
        jnp.float32
    )
    return (segment, token_valid, weight)


def attend_forward(queries, keys_all, values_all, allowed):
    scores = jnp.einsum(
        "qhd,khd->hqk", queries, keys_all, preferred_element_type=jnp.float32
    ) * HEAD_DIM ** (-0.5)
    scores = jnp.where(allowed[None], scores, NEGATIVE)
    row_top = jnp.max(scores, axis=2, keepdims=True)
    exp_scores = jnp.exp(scores - row_top)
    denom_sum = jnp.sum(exp_scores, axis=2, keepdims=True)
    soft_probs = (exp_scores / denom_sum).astype(jnp.bfloat16)
    result = jnp.einsum("hqk,khd->qhd", soft_probs, values_all, preferred_element_type=jnp.float32)
    return (result, row_top + jnp.log(denom_sum))


def attend_backward(queries, keys_all, values_all, allowed, log_sums, grad_out):
    score_scale = HEAD_DIM ** (-0.5)
    scores = (
        jnp.einsum("qhd,khd->hqk", queries, keys_all, preferred_element_type=jnp.float32)
        * score_scale
    )
    scores = jnp.where(allowed[None], scores, NEGATIVE)
    soft_probs = jnp.exp(scores - log_sums)
    grad_probs = jnp.einsum(
        "qhd,khd->hqk", grad_out, values_all, preferred_element_type=jnp.float32
    )
    row_inner = jnp.sum(soft_probs * grad_probs, axis=2, keepdims=True)
    grad_scores = (soft_probs * (grad_probs - row_inner)).astype(jnp.bfloat16)
    grad_query = (
        jnp.einsum("hqk,khd->qhd", grad_scores, keys_all, preferred_element_type=jnp.float32)
        * score_scale
    )
    grad_keys = (
        jnp.einsum("hqk,qhd->khd", grad_scores, queries, preferred_element_type=jnp.float32)
        * score_scale
    )
    grad_values = jnp.einsum(
        "hqk,qhd->khd",
        soft_probs.astype(jnp.bfloat16),
        grad_out,
        preferred_element_type=jnp.float32,
    )
    return (grad_query, grad_keys, grad_values)


def own_fetch(w_self_in, w_self_out, w_cross_q, w_cross_kv, w_cross_out, w_mlp_in, w_mlp_out):
    gathered = (
        lax.all_gather(w_self_in, "wide", axis=0, tiled=True),
        lax.all_gather(w_self_out, "wide", axis=0, tiled=True),
        lax.all_gather(w_cross_q, "wide", axis=0, tiled=True),
        lax.all_gather(w_cross_kv, "wide", axis=0, tiled=True),
        lax.all_gather(w_cross_out, "wide", axis=0, tiled=True),
        lax.all_gather(w_mlp_in, "wide", axis=0, tiled=True),
        lax.all_gather(w_mlp_out, "wide", axis=0, tiled=True),
    )
    wide_count = lax.axis_size("wide")
    flat = tuple((piece.reshape(1, wide_count, -1) for piece in gathered))
    moved = (
        lax.all_to_all(flat[0], "narrow", split_axis=1, concat_axis=0, tiled=True),
        lax.all_to_all(flat[1], "narrow", split_axis=1, concat_axis=0, tiled=True),
        lax.all_to_all(flat[2], "narrow", split_axis=1, concat_axis=0, tiled=True),
        lax.all_to_all(flat[3], "narrow", split_axis=1, concat_axis=0, tiled=True),
        lax.all_to_all(flat[4], "narrow", split_axis=1, concat_axis=0, tiled=True),
        lax.all_to_all(flat[5], "narrow", split_axis=1, concat_axis=0, tiled=True),
        lax.all_to_all(flat[6], "narrow", split_axis=1, concat_axis=0, tiled=True),
    )
    return tuple(
        (
            jnp.swapaxes(block, 0, 1).reshape((-1,) + piece.shape[1:])
            for block, piece in zip(moved, gathered)
        )
    )


def row_gather(local_rows):
    return lax.all_gather(local_rows, "narrow", axis=0, tiled=True)


def branch_sum(partial_rows):
    return lax.psum_scatter(
        partial_rows.astype(jnp.bfloat16), "narrow", scatter_dimension=0, tiled=True
    ).astype(jnp.float32)


def tensor_pass(tokens, memory, gain_float, weights, cotangent, masks):
    segment, token_valid, valid_float, local_weight, self_ok, cross_ok = masks
    tok_rows = tokens.shape[0]
    group_rows = tok_rows * lax.axis_size("narrow")
    mem_group = memory.shape[0] * lax.axis_size("narrow")
    fwd_own = own_fetch(*weights)
    ws_in, ws_out, wc_q, wc_kv, wc_out, wm_in, wm_out = fwd_own
    own_width = ws_out.shape[0]
    heads_here = own_width // HEAD_DIM
    tok_float = tokens.astype(jnp.float32)
    h1 = normed(tok_float, gain_float[0]).astype(jnp.bfloat16)
    rows_one = row_gather(h1)
    qkv = jnp.einsum("td,hkd->kth", rows_one, ws_in, preferred_element_type=jnp.float32).astype(
        jnp.bfloat16
    )
    head_split = qkv.reshape(3, group_rows, heads_here, HEAD_DIM)
    self_result, self_lse = attend_forward(head_split[0], head_split[1], head_split[2], self_ok)
    self_heads = self_result.reshape(group_rows, own_width).astype(jnp.bfloat16)
    x1 = tok_float + branch_sum(jnp.dot(self_heads, ws_out, preferred_element_type=jnp.float32))
    h2 = normed(x1, gain_float[1]).astype(jnp.bfloat16)
    rows_two = row_gather(h2)
    memory_all = row_gather(memory)
    cross_query = jnp.einsum(
        "td,hd->th", rows_two, wc_q, preferred_element_type=jnp.float32
    ).astype(jnp.bfloat16)
    cross_kv = jnp.einsum(
        "md,hkd->kmh", memory_all, wc_kv, preferred_element_type=jnp.float32
    ).astype(jnp.bfloat16)
    cq_split = cross_query.reshape(group_rows, heads_here, HEAD_DIM)
    ck_split = cross_kv[0].reshape(mem_group, heads_here, HEAD_DIM)
    cv_split = cross_kv[1].reshape(mem_group, heads_here, HEAD_DIM)
    cross_result, cross_lse = attend_forward(cq_split, ck_split, cv_split, cross_ok)
    cross_heads = (
        (cross_result * valid_float[:, None, None])
        .reshape(group_rows, own_width)
        .astype(jnp.bfloat16)
    )
    x2 = x1 + branch_sum(jnp.dot(cross_heads, wc_out, preferred_element_type=jnp.float32))
    h3 = normed(x2, gain_float[2]).astype(jnp.bfloat16)
    rows_three = row_gather(h3)
    gate_up = jnp.einsum("td,fkd->ktf", rows_three, wm_in, preferred_element_type=jnp.float32)
    hidden = (jax.nn.gelu(gate_up[0], approximate=True) * gate_up[1]).astype(jnp.bfloat16)
    output = (x2 + branch_sum(jnp.dot(hidden, wm_out, preferred_element_type=jnp.float32))).astype(
        jnp.bfloat16
    )
    back_own = own_fetch(*weights)
    ws_in, ws_out, wc_q, wc_kv, wc_out, wm_in, wm_out = back_own
    grad_y = cotangent.astype(jnp.float32) * local_weight[:, None]
    grad_mlp = row_gather(grad_y.astype(jnp.bfloat16))
    grad_hidden = jnp.einsum("td,fd->tf", grad_mlp, wm_out, preferred_element_type=jnp.float32)
    _, gelu_pull = jax.vjp(
        lambda gate_part, up_part: jax.nn.gelu(gate_part, approximate=True) * up_part,
        gate_up[0],
        gate_up[1],
    )
    grad_gate, grad_up = gelu_pull(grad_hidden)
    grad_gate_up = jnp.stack([grad_gate, grad_up]).astype(jnp.bfloat16)
    grad_h3 = branch_sum(
        jnp.einsum("ktf,fkd->td", grad_gate_up, wm_in, preferred_element_type=jnp.float32)
    )
    _, norm_pull3 = jax.vjp(normed, x2, gain_float[2])
    part_x2, grad_gain3 = norm_pull3(grad_h3)
    grad_x2 = grad_y + part_x2
    gate_term = jnp.einsum(
        "ktf,td->fkd", grad_gate_up, rows_three, preferred_element_type=jnp.float32
    )
    down_term = jnp.einsum("tf,td->fd", hidden, grad_mlp, preferred_element_type=jnp.float32)
    mlp_grads = jnp.concatenate([gate_term, down_term[:, None, :]], axis=1)
    grad_cross = row_gather(grad_x2.astype(jnp.bfloat16))
    grad_cross_heads = jnp.einsum(
        "td,hd->th", grad_cross, wc_out, preferred_element_type=jnp.float32
    ).astype(jnp.bfloat16)
    grad_cross_heads = grad_cross_heads.reshape(group_rows, heads_here, HEAD_DIM)
    grad_cross_heads = jnp.where(
        token_valid[:, None, None], grad_cross_heads, jnp.zeros_like(grad_cross_heads)
    )
    gq_heads, gk_heads, gv_heads = attend_backward(
        cq_split, ck_split, cv_split, cross_ok, cross_lse, grad_cross_heads
    )
    grad_cq = gq_heads.reshape(group_rows, own_width).astype(jnp.bfloat16)
    grad_ckv = jnp.stack([gk_heads.reshape(mem_group, -1), gv_heads.reshape(mem_group, -1)]).astype(
        jnp.bfloat16
    )
    grad_h2 = branch_sum(jnp.einsum("th,hd->td", grad_cq, wc_q, preferred_element_type=jnp.float32))
    grad_memory = branch_sum(
        jnp.einsum("kmh,hkd->md", grad_ckv, wc_kv, preferred_element_type=jnp.float32)
    ).astype(jnp.bfloat16)
    _, norm_pull2 = jax.vjp(normed, x1, gain_float[1])
    part_x1, grad_gain2 = norm_pull2(grad_h2)
    grad_x1 = grad_x2 + part_x1
    grad_self = row_gather(grad_x1.astype(jnp.bfloat16))
    grad_self_heads = jnp.einsum(
        "td,hd->th", grad_self, ws_out, preferred_element_type=jnp.float32
    ).astype(jnp.bfloat16)
    grad_self_heads = grad_self_heads.reshape(group_rows, heads_here, HEAD_DIM)
    sq_heads, sk_heads, sv_heads = attend_backward(
        head_split[0], head_split[1], head_split[2], self_ok, self_lse, grad_self_heads
    )
    grad_qkv = (
        jnp.stack([sq_heads, sk_heads, sv_heads]).reshape(3, group_rows, -1).astype(jnp.bfloat16)
    )
    grad_h1 = branch_sum(
        jnp.einsum("kth,hkd->td", grad_qkv, ws_in, preferred_element_type=jnp.float32)
    )
    _, norm_pull1 = jax.vjp(normed, tok_float, gain_float[0])
    part_x, grad_gain1 = norm_pull1(grad_h1)
    grad_tokens = (grad_x1 + part_x).astype(jnp.bfloat16)
    in_term = jnp.einsum("kth,td->hkd", grad_qkv, rows_one, preferred_element_type=jnp.float32)
    self_term = jnp.einsum("th,td->hd", self_heads, grad_self, preferred_element_type=jnp.float32)
    query_term = jnp.einsum("th,td->hd", grad_cq, rows_two, preferred_element_type=jnp.float32)
    memory_term = jnp.einsum(
        "kmh,md->hkd", grad_ckv, memory_all, preferred_element_type=jnp.float32
    )
    cross_term = jnp.einsum(
        "th,td->hd", cross_heads, grad_cross, preferred_element_type=jnp.float32
    )
    attn_grads = jnp.concatenate(
        [
            in_term,
            self_term[:, None, :],
            query_term[:, None, :],
            memory_term,
            cross_term[:, None, :],
        ],
        axis=1,
    )
    gain_terms = jnp.stack([grad_gain1, grad_gain2, grad_gain3])
    return (output, grad_tokens, grad_memory, gain_terms, attn_grads, mlp_grads)


def per_device(
    tokens,
    memory,
    item_len,
    item_kind,
    norm_gains,
    w_self_in,
    w_self_out,
    w_cross_q,
    w_cross_kv,
    w_cross_out,
    w_mlp_in,
    w_mlp_out,
    cotangent,
):
    tok_rows = tokens.shape[0]
    narrow_size = lax.axis_size("narrow")
    group_rows = tok_rows * narrow_size
    mem_group = memory.shape[0] * narrow_size
    lengths = item_len[0]
    item_count = lengths.shape[0]
    patch_rows = mem_group // item_count
    positions = jnp.arange(group_rows, dtype=jnp.int32)
    segment, token_valid, weight = token_info(lengths, item_kind[0], positions, item_count)
    local_weight = lax.dynamic_slice_in_dim(weight, lax.axis_index("narrow") * tok_rows, tok_rows)
    self_ok = (segment[:, None] == segment[None, :]) & (positions[None, :] <= positions[:, None])
    mem_item = jnp.arange(mem_group, dtype=jnp.int32) // patch_rows
    cross_ok = mem_item[None, :] == jnp.minimum(segment, item_count - 1)[:, None]
    valid_float = token_valid.astype(jnp.float32)
    masks = (segment, token_valid, valid_float, local_weight, self_ok, cross_ok)
    gain_float = norm_gains.astype(jnp.float32)
    weights = (w_self_in, w_self_out, w_cross_q, w_cross_kv, w_cross_out, w_mlp_in, w_mlp_out)
    results = tensor_pass(tokens, memory, gain_float, weights, cotangent, masks)
    output, grad_tokens, grad_memory, gain_terms, attn_grads, mlp_grads = results
    gain_shard = lax.psum_scatter(gain_terms, "narrow", scatter_dimension=1, tiled=True)
    summed = (
        lax.psum_scatter(
            attn_grads.astype(jnp.bfloat16), "wide", scatter_dimension=0, tiled=True
        ).astype(jnp.float32),
        lax.psum_scatter(
            mlp_grads.astype(jnp.bfloat16), "wide", scatter_dimension=0, tiled=True
        ).astype(jnp.float32),
        lax.psum_scatter(
            gain_shard.astype(jnp.bfloat16), "wide", scatter_dimension=1, tiled=True
        ).astype(jnp.float32),
    )
    attn_total, mlp_total, gain_total = (
        lax.all_gather(summed[0].astype(jnp.bfloat16), "wide", axis=0, tiled=True).astype(
            jnp.float32
        ),
        lax.all_gather(summed[1].astype(jnp.bfloat16), "wide", axis=0, tiled=True).astype(
            jnp.float32
        ),
        lax.all_gather(summed[2].astype(jnp.bfloat16), "wide", axis=1, tiled=True).astype(
            jnp.float32
        ),
    )
    return (
        output,
        grad_tokens,
        grad_memory,
        gain_total,
        attn_total[:, 0:3, :],
        attn_total[:, 3, :],
        attn_total[:, 4, :],
        attn_total[:, 5:7, :],
        attn_total[:, 7, :],
        mlp_total[:, 0:2, :],
        mlp_total[:, 2, :],
    )


def solution(mesh):
    return jax.shard_map(
        per_device,
        mesh=mesh,
        in_specs=(
            P(("wide", "narrow"), None),
            P(("wide", "narrow"), None),
            P("wide", None),
            P("wide", None),
            P(),
            P(("wide", "narrow"), None, None),
            P(("wide", "narrow"), None),
            P(("wide", "narrow"), None),
            P(("wide", "narrow"), None, None),
            P(("wide", "narrow"), None),
            P(("wide", "narrow"), None, None),
            P(("wide", "narrow"), None),
            P(("wide", "narrow"), None),
        ),
        out_specs=(
            P(("wide", "narrow"), None),
            P(("wide", "narrow"), None),
            P(("wide", "narrow"), None),
            P(None, "narrow"),
            P("narrow", None, None),
            P("narrow", None),
            P("narrow", None),
            P("narrow", None, None),
            P("narrow", None),
            P("narrow", None, None),
            P("narrow", None),
        ),
        check_vma=False,
    )
```

profile of v0, /device:TPU:25, one launch (start us, length us, event | category | flops | bytes accessed | tf_op | source)
XLA Modules:
  0.0 2400.9 jit_solution(10870311697358337911)
XLA Ops:
  15.8 23.3 all-gather.22.cloned.1.call-done
  111.8 40.2 %reduce.15 = bf16[8,393216]{1,0:T(8,128)(2,1)} reduce(bf16[8,1,393216]{2,1,0:T(2,128)(2,1)} %bitcast.230, bf16[]{:T(256)} %broadcast.335), dimensions={1}, to_apply=%bitcast.169.reduce_sub_computation | reduce | bytes 12582914
  193.9 109.0 %all-to-all-done = bf16[4,2,393216]{2,1,0:T(2,128)(2,1)} async-done(((bf16[4,2,393216]{2,1,0:T(2,128)(2,1)}), bf16[4,2,393216]{2,1,0:T(2,128)(2,1)}, u32[]{:S(2)}, u32[]{:S(2)}) %all-to-all-start) | async-done | bytes 6291488 | tf_op jit(solution)/shard_map/all_to_all | solution.py:87
  312.8 41.6 %bitcast_reduce_fusion.1 = bf16[8,393216]{1,0:T(8,128)(2,1)} fusion(bf16[8,1,393216]{2,1,0:T(2,128)(2,1)} %reshape.393), kind=kLoop, calls=%fused_computation.222 | loop fusion | bytes 12582912 | tf_op jit(solution)/shard_map/all_to_all | solution.py:87
  459.0 30.3 %all-to-all-done.4 = bf16[4,2,131072]{2,1,0:T(2,128)(2,1)S(1)} async-done(((bf16[4,2,131072]{2,1,0:T(2,128)(2,1)}), bf16[4,2,131072]{2,1,0:T(2,128)(2,1)S(1)}, u32[]{:S(2)}, u32[]{:S(2)}) %all-to-all-start.4) | async-done | bytes 2097184 | tf_op jit(solution)/shard_map/all_to_all | solution.py:91
  505.5 27.2 %reduce.14 = bf16[8,262144]{1,0:T(8,128)(2,1)} reduce(bf16[8,1,262144]{2,1,0:T(2,128)(2,1)} %bitcast.233, bf16[]{:T(256)} %broadcast.335), dimensions={1}, to_apply=%bitcast.163.reduce_sub_computation | reduce | bytes 8388610
  561.4 33.9 %reduce.20 = bf16[8,327680]{1,0:T(8,128)(2,1)} reduce(bf16[8,1,327680]{2,1,0:T(2,128)(2,1)} %bitcast.231, bf16[]{:T(256)} %broadcast.335), dimensions={1}, to_apply=%bitcast.167.reduce_sub_computation | reduce | bytes 10485762
  603.4 36.0 %all-to-all-done.2 = bf16[4,2,262144]{2,1,0:T(2,128)(2,1)} async-done(((bf16[4,2,262144]{2,1,0:T(2,128)(2,1)}), bf16[4,2,262144]{2,1,0:T(2,128)(2,1)}, u32[]{:S(2)}, u32[]{:S(2)}) %all-to-all-start.2) | async-done | bytes 4194336 | tf_op jit(solution)/shard_map/all_to_all | solution.py:90
  705.1 65.8 %reduce.18 = bf16[8,655360]{1,0:T(8,128)(2,1)} reduce(bf16[8,1,655360]{2,1,0:T(2,128)(2,1)} %bitcast.229, bf16[]{:T(256)} %broadcast.335), dimensions={1}, to_apply=%bitcast.165.reduce_sub_computation | reduce | bytes 20971522
  770.9 21.9 reshape.388
  792.9 34.2 %all-to-all-done.6 = bf16[4,2,327680]{2,1,0:T(2,128)(2,1)} async-done(((bf16[4,2,327680]{2,1,0:T(2,128)(2,1)}), bf16[4,2,327680]{2,1,0:T(2,128)(2,1)}, u32[]{:S(2)}, u32[]{:S(2)}) %all-to-all-start.6) | async-done | bytes 5242912 | tf_op jit(solution)/shard_map/all_to_all | solution.py:93
  865.5 27.7 %bitcast_reduce_fusion.3 = bf16[8,262144]{1,0:T(8,128)(2,1)} fusion(bf16[8,1,262144]{2,1,0:T(2,128)(2,1)} %reshape.387), kind=kLoop, calls=%fused_computation.224 | loop fusion | bytes 8388608 | tf_op jit(solution)/shard_map/all_to_all | solution.py:90
  938.9 139.6 %reduce-scatter.17.cloned.1.call-done = bf16[128,2048]{1,0:T(8,128)(2,1)} async-done(((bf16[512,2048]{1,0:T(8,128)(2,1)}), bf16[128,2048]{1,0:T(8,128)(2,1)}) %reduce-scatter.17.cloned.1.call-update) | async-done | bytes 524304 | tf_op jit(solution)/shard_map/reduce_scatter | solution.py:108
  1091.9 34.0 %bitcast_reduce_fusion.2 = bf16[8,327680]{1,0:T(8,128)(2,1)} fusion(bf16[8,1,327680]{2,1,0:T(2,128)(2,1)} %reshape.391), kind=kLoop, calls=%fused_computation.223 | loop fusion | bytes 10485760 | tf_op jit(solution)/shard_map/all_to_all | solution.py:93
  1157.7 25.6 %reshape.389 = bf16[8,1,655360]{2,1,0:T(2,128)(2,1)} reshape(bf16[4,2,655360]{2,1,0:T(2,128)(2,1)} %all-to-all-done.5) | data formatting | bytes 20971520
  1183.3 67.8 %bitcast_reduce_fusion = bf16[8,655360]{1,0:T(8,128)(2,1)} fusion(bf16[8,1,655360]{2,1,0:T(2,128)(2,1)} %reshape.389), kind=kLoop, calls=%fused_computation.221 | loop fusion | bytes 20971520 | tf_op jit(solution)/shard_map/all_to_all | solution.py:92
  1251.1 21.9 all_to_all.39
  1287.6 20.3 reshape.348
  1346.6 43.1 %reduce-scatter.21.cloned.1.call-done = bf16[128,2048]{1,0:T(8,128)(2,1)} async-done(((bf16[512,2048]{1,0:T(8,128)(2,1)}), bf16[128,2048]{1,0:T(8,128)(2,1)}) %reduce-scatter.21.cloned.1.call-update) | async-done | bytes 524304 | tf_op jit(solution)/shard_map/reduce_scatter | solution.py:108
  1393.7 44.6 %all-gather.42.cloned.1.call-done = bf16[512,2048]{1,0:T(8,128)(2,1)} async-done(((bf16[128,2048]{1,0:T(8,128)(2,1)}), bf16[512,2048]{1,0:T(8,128)(2,1)}) %all-gather.42.cloned.1.call-update) | async-done | bytes 2097168 | tf_op jit(solution)/shard_map/all_gather | solution.py:104
  1465.6 34.1 %reduce-scatter.23.cloned.1.call-done = bf16[128,2048]{1,0:T(8,128)(2,1)} async-done(((bf16[512,2048]{1,0:T(8,128)(2,1)}), bf16[128,2048]{1,0:T(8,128)(2,1)}) %reduce-scatter.23.cloned.1.call-update) | async-done | bytes 524304 | tf_op jit(solution)/shard_map/reduce_scatter | solution.py:108
  1501.3 44.0 %reduce-scatter.19.cloned.1.call-done = bf16[128,2048]{1,0:T(8,128)(2,1)} async-done(((bf16[512,2048]{1,0:T(8,128)(2,1)}), bf16[128,2048]{1,0:T(8,128)(2,1)}) %reduce-scatter.19.cloned.1.call-update) | async-done | bytes 524304 | tf_op jit(solution)/shard_map/reduce_scatter | solution.py:108
  1548.8 44.5 %all-gather.44.cloned.1.call-done = bf16[512,2048]{1,0:T(8,128)(2,1)} async-done(((bf16[128,2048]{1,0:T(8,128)(2,1)}), bf16[512,2048]{1,0:T(8,128)(2,1)}) %all-gather.44.cloned.1.call-update) | async-done | bytes 2097168 | tf_op jit(solution)/shard_map/all_gather | solution.py:104
  1639.2 25.4 %reduce-scatter.25.cloned.1.call-done = bf16[128,2048]{1,0:T(8,128)(2,1)} async-done(((bf16[512,2048]{1,0:T(8,128)(2,1)}), bf16[128,2048]{1,0:T(8,128)(2,1)}) %reduce-scatter.25.cloned.1.call-update) | async-done | bytes 524304 | tf_op jit(solution)/shard_map/reduce_scatter | solution.py:108
  1680.9 34.0 %copy.343 = bf16[1280,3,2048]{2,1,0:T(4,128)(2,1)} copy(bf16[1280,3,2048]{0,2,1:T(8,128)(2,1)} %pad_maximum_fusion) | data formatting | bytes 31457280 | tf_op jit(solution)/shard_map/concatenate | solution.py:180
  1749.8 25.3 %copy.340 = bf16[512,8,2048]{2,1,0:T(8,128)(2,1)} copy(bf16[512,8,2048]{0,2,1:T(8,128)(2,1)} %fusion.38) | data formatting | bytes 33554432 | tf_op jit(solution)/shard_map/concatenate | solution.py:229
  1779.2 199.3 %all-reduce.3.cloned.1.call-done = bf16[1280,3,2048]{2,1,0:T(4,128)(2,1)} async-done(((bf16[1280,3,2048]{2,1,0:T(4,128)(2,1)}), bf16[1280,3,2048]{2,1,0:T(4,128)(2,1)}) %all-reduce.3.cloned.1.call-update) | async-done | bytes 15728656
  1984.2 114.0 %reduce-scatter.29.cloned.1.call-done = bf16[64,8,2048]{2,1,0:T(8,128)(2,1)} async-done(((bf16[512,8,2048]{2,1,0:T(8,128)(2,1)}), bf16[64,8,2048]{2,1,0:T(8,128)(2,1)}) %reduce-scatter.29.cloned.1.call-update) | async-done | bytes 2097168 | tf_op jit(solution)/shard_map/reduce_scatter | solution.py:279
  2110.3 24.5 %reduce-scatter.33.cloned.1.call-done = bf16[64,3]{1,0:T(8,128)(2,1)} async-done(((bf16[512,3]{1,0:T(8,128)(2,1)}), bf16[64,3]{1,0:T(8,128)(2,1)}) %reduce-scatter.33.cloned.1.call-update) | async-done | bytes 400
  2146.2 77.3 %all-gather.48.cloned.1.call-done = bf16[1280,3,2048]{2,0,1:T(8,128)(2,1)} async-done(((bf16[160,3,2048]{2,0,1:T(8,128)(2,1)}), bf16[1280,3,2048]{2,0,1:T(8,128)(2,1)}) %all-gather.48.cloned.1.call-update) | async-done | bytes 15728656 | tf_op jit(solution)/shard_map/all_gather | solution.py:293
  2239.3 35.6 %copy.346 = f32[1280,2,2048]{2,1,0:T(2,128)} copy(f32[1280,2,2048]{2,0,1:T(8,128)} %slice.94) | data formatting | bytes 41943040
  2348.3 27.1 %fusion.148 = (f32[512,1,2048]{2,1,0:T(1,128)S(1)}, f32[512,1,2048]{2,1,0:T(1,128)S(1)}, f32[512,1,2048]{2,1,0:T(1,128)S(1)}) fusion(bf16[512,8,2048]{2,1,0:T(8,128)(2,1)} %all-gather.46.cloned.1.call-done), kind=kLoop, calls=%fused_computation.215 | loop fusion | bytes 25165824 | tf_op jit(solution)/shard_map/slice | solution.py:309
  (375 shorter events, 811.2 us)
Async XLA Ops:
  7.9 78.5 %all-gather.20.cloned.1.call-start = ((), (), s32[]{:S(2)}) async-start(), calls=%async_computation.18 | async-start | bytes 7077888 | tf_op jit(solution)/shard_map/all_gather | solution.py:76
  8.7 374.5 %all-gather.18.cloned.1.call-start = ((), (), s32[]{:S(2)}) async-start(), calls=%async_computation.17 | async-start | bytes 2621440 | tf_op jit(solution)/shard_map/all_gather | solution.py:104
  14.6 389.2 %all-gather.32.cloned.1.call-start = ((), (), s32[]{:S(2)}) async-start(), calls=%async_computation.25 | async-start | bytes 2359296 | tf_op jit(solution)/shard_map/all_gather | solution.py:80
  15.2 417.9 %all-gather.30.cloned.1.call-start = ((), (), s32[]{:S(2)}) async-start(), calls=%async_computation.24 | async-start | bytes 2359296 | tf_op jit(solution)/shard_map/all_gather | solution.py:78
  62.7 98.7 %all-to-all-start.1 = ((bf16[4,2,131072]{2,1,0:T(2,128)(2,1)}), bf16[4,2,131072]{2,1,0:T(2,128)(2,1)S(1)}, u32[]{:S(2)}, u32[]{:S(2)}) async-start(bf16[4,2,131072]{2,1,0:T(2,128)(2,1)} %reshape.394), calls=%async_computation.1 | async-start | bytes 4194304 | tf_op jit(solution)/shard_map/all_to_all | solution.py:88
  67.2 429.5 %all-gather.24.cloned.1.call-start = ((), (), s32[]{:S(2)}) async-start(), calls=%async_computation.21 | async-start | bytes 4718592 | tf_op jit(solution)/shard_map/all_gather | solution.py:79
  161.3 141.5 %all-to-all-start = ((bf16[4,2,393216]{2,1,0:T(2,128)(2,1)}), bf16[4,2,393216]{2,1,0:T(2,128)(2,1)}, u32[]{:S(2)}, u32[]{:S(2)}) async-start(bf16[4,2,393216]{2,1,0:T(2,128)(2,1)} %reshape.392), calls=%async_computation | async-start | bytes 12582912 | tf_op jit(solution)/shard_map/all_to_all | solution.py:87
  166.9 382.6 %all-gather.38.cloned.1.call-start = ((), (), s32[]{:S(2)}) async-start(), calls=%async_computation.29 | async-start | bytes 5898240 | tf_op jit(solution)/shard_map/all_gather | solution.py:82
  167.7 486.5 %reduce-scatter.15.cloned.1.call-start = ((), (), s32[]{:S(2)}) async-start(), calls=%async_computation.20 | async-start | bytes 2621440 | tf_op jit(solution)/shard_map/reduce_scatter | solution.py:108
  403.0 286.4 %all-gather.36.cloned.1.call-start = ((), (), s32[]{:S(2)}) async-start(), calls=%async_computation.28 | async-start | bytes 11796480 | tf_op jit(solution)/shard_map/all_gather | solution.py:81
  427.3 62.0 %all-to-all-start.4 = ((bf16[4,2,131072]{2,1,0:T(2,128)(2,1)}), bf16[4,2,131072]{2,1,0:T(2,128)(2,1)S(1)}, u32[]{:S(2)}, u32[]{:S(2)}) async-start(bf16[4,2,131072]{2,1,0:T(2,128)(2,1)} %reshape.398), calls=%async_computation.5 | async-start | bytes 4194304 | tf_op jit(solution)/shard_map/all_to_all | solution.py:91
  542.4 97.0 %all-to-all-start.2 = ((bf16[4,2,262144]{2,1,0:T(2,128)(2,1)}), bf16[4,2,262144]{2,1,0:T(2,128)(2,1)}, u32[]{:S(2)}, u32[]{:S(2)}) async-start(bf16[4,2,262144]{2,1,0:T(2,128)(2,1)} %reshape.386), calls=%async_computation.3 | async-start | bytes 8388608 | tf_op jit(solution)/shard_map/all_to_all | solution.py:90
  639.5 187.6 %all-to-all-start.6 = ((bf16[4,2,327680]{2,1,0:T(2,128)(2,1)}), bf16[4,2,327680]{2,1,0:T(2,128)(2,1)}, u32[]{:S(2)}, u32[]{:S(2)}) async-start(bf16[4,2,327680]{2,1,0:T(2,128)(2,1)} %reshape.390), calls=%async_computation.8 | async-start | bytes 10485760 | tf_op jit(solution)/shard_map/all_to_all | solution.py:93
  647.3 267.7 %all-gather.26.cloned.1.call-start = ((), (), s32[]{:S(2)}) async-start(), calls=%async_computation.22 | async-start | bytes 5242880 | tf_op jit(solution)/shard_map/all_gather | solution.py:104
  647.9 275.9 %all-gather.28.cloned.1.call-start = ((), (), s32[]{:S(2)}) async-start(), calls=%async_computation.23 | async-start | bytes 2621440 | tf_op jit(solution)/shard_map/all_gather | solution.py:104
  827.1 330.6 %all-to-all-start.5 = ((bf16[4,2,655360]{2,1,0:T(2,128)(2,1)}), bf16[4,2,655360]{2,1,0:T(2,128)(2,1)}, u32[]{:S(2)}, u32[]{:S(2)}) async-start(bf16[4,2,655360]{2,1,0:T(2,128)(2,1)} %reshape.388), calls=%async_computation.7 | async-start | bytes 20971520 | tf_op jit(solution)/shard_map/all_to_all | solution.py:92
  835.9 242.6 %reduce-scatter.17.cloned.1.call-start = ((), (), s32[]{:S(2)}) async-start(), calls=%async_computation.26 | async-start | bytes 2621440 | tf_op jit(solution)/shard_map/reduce_scatter | solution.py:108
  938.9 369.0 %all-gather.34.cloned.1.call-start = ((), (), s32[]{:S(2)}) async-start(), calls=%async_computation.27 | async-start | bytes 2621440 | tf_op jit(solution)/shard_map/all_gather | solution.py:104
  1082.0 245.8 %all-gather.40.cloned.1.call-start = ((), (), s32[]{:S(2)}) async-start(), calls=%async_computation.31 | async-start | bytes 2621440 | tf_op jit(solution)/shard_map/all_gather | solution.py:104
  1083.1 306.6 %reduce-scatter.21.cloned.1.call-start = ((), (), s32[]{:S(2)}) async-start(), calls=%async_computation.32 | async-start | bytes 2621440 | tf_op jit(solution)/shard_map/reduce_scatter | solution.py:108
  1346.5 91.8 %all-gather.42.cloned.1.call-start = ((), (), s32[]{:S(2)}) async-start(), calls=%async_computation.33 | async-start | bytes 2621440 | tf_op jit(solution)/shard_map/all_gather | solution.py:104
  1393.7 106.1 %reduce-scatter.23.cloned.1.call-start = ((), (), s32[]{:S(2)}) async-start(), calls=%async_computation.34 | async-start | bytes 2621440 | tf_op jit(solution)/shard_map/reduce_scatter | solution.py:108
  1456.8 88.5 %reduce-scatter.19.cloned.1.call-start = ((), (), s32[]{:S(2)}) async-start(), calls=%async_computation.30 | async-start | bytes 2621440 | tf_op jit(solution)/shard_map/reduce_scatter | solution.py:108
  1465.5 127.8 %all-gather.44.cloned.1.call-start = ((), (), s32[]{:S(2)}) async-start(), calls=%async_computation.35 | async-start | bytes 2621440 | tf_op jit(solution)/shard_map/all_gather | solution.py:104
  1548.7 115.9 %reduce-scatter.25.cloned.1.call-start = ((), (), s32[]{:S(2)}) async-start(), calls=%async_computation.36 | async-start | bytes 2621440 | tf_op jit(solution)/shard_map/reduce_scatter | solution.py:108
  1621.6 155.4 %reduce-scatter.31.cloned.1.call-start = ((), (), s32[]{:S(2)}) async-start(), calls=%async_computation.41 | async-start | bytes 1310720
  1667.6 310.9 %all-reduce.3.cloned.1.call-start = ((), (), s32[]{:S(2)}) async-start(), calls=%async_computation.43 | async-start | bytes 41943040
  1715.0 383.2 %reduce-scatter.29.cloned.1.call-start = ((), (), s32[]{:S(2)}) async-start(), calls=%async_computation.38 | async-start | bytes 18874368 | tf_op jit(solution)/shard_map/reduce_scatter | solution.py:279
  1775.2 359.6 %reduce-scatter.33.cloned.1.call-start = ((), (), s32[]{:S(2)}) async-start(), calls=%async_computation.42 | async-start | bytes 147456
  1779.0 444.6 %all-gather.48.cloned.1.call-start = ((), (), s32[]{:S(2)}) async-start(), calls=%async_computation.40 | async-start | bytes 17694720 | tf_op jit(solution)/shard_map/all_gather | solution.py:293
  1984.2 330.9 %all-gather.46.cloned.1.call-start = ((), (), s32[]{:S(2)}) async-start(), calls=%async_computation.39 | async-start | bytes 18874368 | tf_op jit(solution)/shard_map/all_gather | solution.py:290
  2098.2 295.4 %reduce-scatter.27.cloned.1.call-start = ((), (), s32[]{:S(2)}) async-start(), calls=%async_computation.37 | async-start | bytes 5242880 | tf_op jit(solution)/shard_map/reduce_scatter | solution.py:108
  (78 other events, 2123.4 us)
Sparse Core Ops, SparseCore 0:
  9.9 29.1 all-gather.21
  41.0 45.3 all-gather.19
  88.5 59.5 all-gather.17
  149.8 28.0 all-gather.31
  179.7 27.7 all-gather.29
  209.2 36.5 all-gather.23
  247.7 40.9 all-gather.37
  403.2 52.1 reduce-scatter.14
  457.2 70.2 all-gather.35
  649.4 169.4 all-gather.25
  821.1 69.9 all-gather.27
  939.0 139.4 reduce-scatter.16
  1082.1 67.6 all-gather.33
  1151.9 44.5 all-gather.39
  1346.7 43.0 reduce-scatter.20
  1393.8 44.4 all-gather.41
  1456.9 42.7 reduce-scatter.22
  1502.5 42.8 reduce-scatter.18
  1548.8 44.4 all-gather.43
  1621.8 42.7 reduce-scatter.24
  1667.7 25.1 reduce-scatter.30
  1715.1 263.3 all-reduce.2
  1982.0 116.1 reduce-scatter.28
  2101.6 33.1 reduce-scatter.32
  2137.3 86.2 all-gather.47
  2225.3 89.7 all-gather.45
  2317.8 75.7 reduce-scatter.26
where the time goes:
time: 2420 us; the launch traced here: 2400 us
  waiting for transfers between devices  1080 us (45%)
  local copies, waits for them, and re-layouts  811 us (34%)
  other arithmetic  261 us (11%)
  matrix products  179 us (7%)
  starting transfers between devices  46.8 us (2%)
    reduce_scatter x7, waiting for transfers between devices, branch_sum(): lax.psum_scatter(partial_rows.astype(jnp.bfloat16), 'narrow', scatter_dim...  287 us
    unnamed x30, waiting for transfers between devices  229 us
    unnamed x177, local copies, waits for them, and re-layouts  210 us
    unnamed x9, other arithmetic  207 us
    reduce_scatter x1, waiting for transfers between devices, per_device(): lax.psum_scatter(attn_grads.astype(jnp.bfloat16), 'wide', scatter_dimensi...  114 us
    all_to_all x1, waiting for transfers between devices, own_fetch(): lax.all_to_all(flat[0], 'narrow', split_axis=1, concat_axis=0, tiled=True)  109 us
    all_to_all x2, local copies, waits for them, and re-layouts, own_fetch(): lax.all_to_all(flat[5], 'narrow', split_axis=1, concat_axis=0, tiled=True)  89.7 us
    all_gather x7, waiting for transfers between devices, row_gather(): return lax.all_gather(local_rows, 'narrow', axis=0, tiled=True)  89.2 us
  transfers between devices with their start and end apart: 34, of which 21 were waited for; matrix products, arithmetic and copies ran while one was open for 46% of the time, Pallas kernels for 0%

commit v1 on v0

v1 whole, which is shorter than its diff:
```python
import jax
import jax.numpy as jnp
from jax import lax
from jax.sharding import PartitionSpec as P

HEAD_DIM = 128


EPSILON = 1e-06
ROBOT_WEIGHT = 2.0
NEGATIVE = -1e30


def normed(values, gain_row):
    factor = lax.rsqrt(jnp.mean(values * values, axis=-1, keepdims=True) + EPSILON)
    return values * factor * gain_row


def token_info(lengths, item_kinds, positions, item_count):
    item_ends = jnp.cumsum(lengths)
    segment = jnp.sum((positions[:, None] >= item_ends[None, :]).astype(jnp.int32), axis=1)
    token_valid = segment < item_count
    item_hit = segment[:, None] == jnp.arange(item_count, dtype=jnp.int32)[None, :]
    robot_flag = jnp.sum(jnp.where(item_hit, item_kinds[None, :], 0), axis=1)
    weight = jnp.where(token_valid, jnp.where(robot_flag == 1, ROBOT_WEIGHT, 1.0), 0.0).astype(
        jnp.float32
    )
    return (segment, token_valid, weight)


def attend_forward(queries, keys_all, values_all, allowed):
    scores = jnp.einsum(
        "qhd,khd->hqk", queries, keys_all, preferred_element_type=jnp.float32
    ) * HEAD_DIM ** (-0.5)
    scores = jnp.where(allowed[None], scores, NEGATIVE)
    row_top = jnp.max(scores, axis=2, keepdims=True)
    exp_scores = jnp.exp(scores - row_top)
    denom_sum = jnp.sum(exp_scores, axis=2, keepdims=True)
    soft_probs = (exp_scores / denom_sum).astype(jnp.bfloat16)
    result = jnp.einsum("hqk,khd->qhd", soft_probs, values_all, preferred_element_type=jnp.float32)
    return (result, row_top + jnp.log(denom_sum))


def attend_backward(queries, keys_all, values_all, allowed, log_sums, grad_out):
    score_scale = HEAD_DIM ** (-0.5)
    scores = (
        jnp.einsum("qhd,khd->hqk", queries, keys_all, preferred_element_type=jnp.float32)
        * score_scale
    )
    scores = jnp.where(allowed[None], scores, NEGATIVE)
    soft_probs = jnp.exp(scores - log_sums)
    grad_probs = jnp.einsum(
        "qhd,khd->hqk", grad_out, values_all, preferred_element_type=jnp.float32
    )
    row_inner = jnp.sum(soft_probs * grad_probs, axis=2, keepdims=True)
    grad_scores = (soft_probs * (grad_probs - row_inner)).astype(jnp.bfloat16)
    grad_query = (
        jnp.einsum("hqk,khd->qhd", grad_scores, keys_all, preferred_element_type=jnp.float32)
        * score_scale
    )
    grad_keys = (
        jnp.einsum("hqk,qhd->khd", grad_scores, queries, preferred_element_type=jnp.float32)
        * score_scale
    )
    grad_values = jnp.einsum(
        "hqk,qhd->khd",
        soft_probs.astype(jnp.bfloat16),
        grad_out,
        preferred_element_type=jnp.float32,
    )
    return (grad_query, grad_keys, grad_values)


def spread_tables(wide, narrow):
    total = wide * narrow
    ratio = wide // narrow
    if (wide, narrow) == (8, 4):
        first, second, spots = [], [], [[0] * wide for _ in range(narrow)]
        for block in range(total):
            w, n = divmod(block, narrow)
            q, c = divmod(w, ratio)
            z1, z0 = divmod(n, 2)
            spot = 2 * (q ^ (2 * c + z1)) + (z0 ^ c)
            first.append((block, spot * narrow + n))
            second.append((spot * narrow + n, spot * narrow + q))
            spots[q][block - q * wide] = spot
        return (first, second, spots)
    direct = []
    for block in range(total):
        n, w = divmod(block, wide)
        direct.append((block, w * narrow + n))
    return (direct, None, None)


def spread(piece):
    axes = ("wide", "narrow")
    first, second, _ = spread_tables(lax.axis_size("wide"), lax.axis_size("narrow"))
    piece = lax.ppermute(piece, axes, first)
    if second is not None:
        piece = lax.ppermute(piece, axes, second)
    return piece


def wide_gather(pieces):
    rows, width = pieces[0].shape
    moved = spread(jnp.concatenate(pieces, axis=0))
    full = lax.all_gather(moved, "wide", axis=0, tiled=False)
    full = full.reshape(-1, len(pieces), rows, width)
    return tuple(full[:, kind].reshape(-1, width) for kind in range(len(pieces)))


def wide_total(terms):
    wide_count = lax.axis_size("wide")
    width = terms[0].shape[1]
    parts = [term.astype(jnp.bfloat16).reshape(wide_count, -1, width) for term in terms]
    packed = jnp.concatenate(parts, axis=1)
    rows = packed.shape[1]
    shard = lax.psum_scatter(
        packed.reshape(wide_count * rows, width), "wide", scatter_dimension=0, tiled=True
    )
    full = lax.all_gather(shard, "wide", axis=0, tiled=False)
    _, _, spots = spread_tables(wide_count, lax.axis_size("narrow"))
    if spots is not None:
        order = jnp.asarray(spots, jnp.int32)[lax.axis_index("narrow")]
        full = jnp.concatenate(
            [lax.dynamic_slice_in_dim(full, order[j], 1, 0) for j in range(wide_count)], axis=0
        )
    full = full.reshape(wide_count, len(terms), -1, width)
    return [
        full[:, kind].reshape(-1, width).astype(jnp.float32) for kind in range(len(terms))
    ]


def row_gather(local_rows):
    return lax.all_gather(local_rows, "narrow", axis=0, tiled=True)


def branch_sum(partial_rows):
    return lax.psum_scatter(
        partial_rows.astype(jnp.bfloat16), "narrow", scatter_dimension=0, tiled=True
    ).astype(jnp.float32)


def matmul_nt(a, b):
    return lax.dot_general(a, b, (((1,), (1,)), ((), ())), preferred_element_type=jnp.float32)


def matmul_nn(a, b):
    return lax.dot_general(a, b, (((1,), (0,)), ((), ())), preferred_element_type=jnp.float32)


def matmul_tn(a, b):
    return lax.dot_general(a, b, (((0,), (0,)), ((), ())), preferred_element_type=jnp.float32)


def tensor_pass(tokens, memory, gain_float, weights, cotangent, masks):
    segment, token_valid, valid_float, local_weight, self_ok, cross_ok = masks
    tok_rows = tokens.shape[0]
    group_rows = tok_rows * lax.axis_size("narrow")
    mem_group = memory.shape[0] * lax.axis_size("narrow")
    w_self_in, w_self_out, w_cross_q, w_cross_kv, w_cross_out, w_mlp_in, w_mlp_out = weights
    tok_float = tokens.astype(jnp.float32)
    h1 = normed(tok_float, gain_float[0]).astype(jnp.bfloat16)
    rows_one = row_gather(h1)
    ws_q, ws_k, ws_v = wide_gather([w_self_in[:, 0], w_self_in[:, 1], w_self_in[:, 2]])
    ws_out, wc_q, wc_k, wc_v, wc_out = wide_gather(
        [w_self_out, w_cross_q, w_cross_kv[:, 0], w_cross_kv[:, 1], w_cross_out]
    )
    wm_gate, wm_up, wm_out = wide_gather([w_mlp_in[:, 0], w_mlp_in[:, 1], w_mlp_out])
    memory_all = row_gather(memory)
    grad_y = cotangent.astype(jnp.float32) * local_weight[:, None]
    grad_mlp = row_gather(grad_y.astype(jnp.bfloat16))
    own_width = ws_out.shape[0]
    heads_here = own_width // HEAD_DIM

    def split(mat):
        return mat.reshape(mat.shape[0], heads_here, HEAD_DIM)

    def project(rows, mat):
        return matmul_nt(rows, mat).astype(jnp.bfloat16)

    sq, sk, sv = (split(project(rows_one, mat)) for mat in (ws_q, ws_k, ws_v))
    self_result, self_lse = attend_forward(sq, sk, sv, self_ok)
    self_heads = self_result.reshape(group_rows, own_width).astype(jnp.bfloat16)
    x1 = tok_float + branch_sum(matmul_nn(self_heads, ws_out))
    h2 = normed(x1, gain_float[1]).astype(jnp.bfloat16)
    rows_two = row_gather(h2)
    ck, cv = (split(project(memory_all, mat)) for mat in (wc_k, wc_v))
    cq = split(project(rows_two, wc_q))
    cross_result, cross_lse = attend_forward(cq, ck, cv, cross_ok)
    cross_heads = (
        (cross_result * valid_float[:, None, None])
        .reshape(group_rows, own_width)
        .astype(jnp.bfloat16)
    )
    x2 = x1 + branch_sum(matmul_nn(cross_heads, wc_out))
    h3 = normed(x2, gain_float[2]).astype(jnp.bfloat16)
    rows_three = row_gather(h3)
    gate = matmul_nt(rows_three, wm_gate)
    up = matmul_nt(rows_three, wm_up)
    hidden = (jax.nn.gelu(gate, approximate=True) * up).astype(jnp.bfloat16)
    output = (x2 + branch_sum(matmul_nn(hidden, wm_out))).astype(jnp.bfloat16)
    grad_hidden = matmul_nt(grad_mlp, wm_out)
    _, gelu_pull = jax.vjp(
        lambda gate_part, up_part: jax.nn.gelu(gate_part, approximate=True) * up_part, gate, up
    )
    grad_gate, grad_up = gelu_pull(grad_hidden)
    grad_gate = grad_gate.astype(jnp.bfloat16)
    grad_up = grad_up.astype(jnp.bfloat16)
    grad_h3 = branch_sum(matmul_nn(grad_gate, wm_gate) + matmul_nn(grad_up, wm_up))
    _, norm_pull3 = jax.vjp(normed, x2, gain_float[2])
    part_x2, grad_gain3 = norm_pull3(grad_h3)
    grad_x2 = grad_y + part_x2
    mlp_totals = wide_total(
        [
            matmul_tn(grad_gate, rows_three),
            matmul_tn(grad_up, rows_three),
            matmul_tn(hidden, grad_mlp),
        ]
    )
    grad_cross = row_gather(grad_x2.astype(jnp.bfloat16))
    grad_cross_heads = split(project(grad_cross, wc_out))
    grad_cross_heads = jnp.where(
        token_valid[:, None, None], grad_cross_heads, jnp.zeros_like(grad_cross_heads)
    )
    gq_heads, gk_heads, gv_heads = attend_backward(
        cq, ck, cv, cross_ok, cross_lse, grad_cross_heads
    )
    grad_cq = gq_heads.reshape(group_rows, own_width).astype(jnp.bfloat16)
    grad_ck = gk_heads.reshape(mem_group, own_width).astype(jnp.bfloat16)
    grad_cv = gv_heads.reshape(mem_group, own_width).astype(jnp.bfloat16)
    grad_h2 = branch_sum(matmul_nn(grad_cq, wc_q))
    _, norm_pull2 = jax.vjp(normed, x1, gain_float[1])
    part_x1, grad_gain2 = norm_pull2(grad_h2)
    grad_x1 = grad_x2 + part_x1
    grad_self = row_gather(grad_x1.astype(jnp.bfloat16))
    grad_memory = branch_sum(matmul_nn(grad_ck, wc_k) + matmul_nn(grad_cv, wc_v)).astype(
        jnp.bfloat16
    )
    mid_totals = wide_total(
        [
            matmul_tn(self_heads, grad_self),
            matmul_tn(grad_cq, rows_two),
            matmul_tn(grad_ck, memory_all),
            matmul_tn(grad_cv, memory_all),
            matmul_tn(cross_heads, grad_cross),
        ]
    )
    grad_self_heads = split(project(grad_self, ws_out))
    gsq, gsk, gsv = (
        mat.reshape(group_rows, own_width).astype(jnp.bfloat16)
        for mat in attend_backward(sq, sk, sv, self_ok, self_lse, grad_self_heads)
    )
    in_totals = wide_total(
        [matmul_tn(gsq, rows_one), matmul_tn(gsk, rows_one), matmul_tn(gsv, rows_one)]
    )
    grad_h1 = branch_sum(matmul_nn(gsq, ws_q) + matmul_nn(gsk, ws_k) + matmul_nn(gsv, ws_v))
    _, norm_pull1 = jax.vjp(normed, tok_float, gain_float[0])
    part_x, grad_gain1 = norm_pull1(grad_h1)
    grad_tokens = (grad_x1 + part_x).astype(jnp.bfloat16)
    gain_terms = jnp.stack([grad_gain1, grad_gain2, grad_gain3])
    return (output, grad_tokens, grad_memory, gain_terms, in_totals, mid_totals, mlp_totals)


def per_device_general(
    tokens,
    memory,
    item_len,
    item_kind,
    norm_gains,
    w_self_in,
    w_self_out,
    w_cross_q,
    w_cross_kv,
    w_cross_out,
    w_mlp_in,
    w_mlp_out,
    cotangent,
):
    tok_rows = tokens.shape[0]
    narrow_size = lax.axis_size("narrow")
    group_rows = tok_rows * narrow_size
    mem_group = memory.shape[0] * narrow_size
    lengths = item_len[0]
    item_count = lengths.shape[0]
    patch_rows = mem_group // item_count
    positions = jnp.arange(group_rows, dtype=jnp.int32)
    segment, token_valid, weight = token_info(lengths, item_kind[0], positions, item_count)
    local_weight = lax.dynamic_slice_in_dim(weight, lax.axis_index("narrow") * tok_rows, tok_rows)
    self_ok = (segment[:, None] == segment[None, :]) & (positions[None, :] <= positions[:, None])
    mem_item = jnp.arange(mem_group, dtype=jnp.int32) // patch_rows
    cross_ok = mem_item[None, :] == jnp.minimum(segment, item_count - 1)[:, None]
    valid_float = token_valid.astype(jnp.float32)
    masks = (segment, token_valid, valid_float, local_weight, self_ok, cross_ok)
    gain_float = norm_gains.astype(jnp.float32)
    weights = (w_self_in, w_self_out, w_cross_q, w_cross_kv, w_cross_out, w_mlp_in, w_mlp_out)
    output, grad_tokens, grad_memory, gain_terms, in_totals, mid_totals, mlp_totals = tensor_pass(
        tokens, memory, gain_float, weights, cotangent, masks
    )
    gain_shard = lax.psum_scatter(gain_terms, "narrow", scatter_dimension=1, tiled=True)
    gain_total = lax.psum(gain_shard, "wide")
    return (
        output,
        grad_tokens,
        grad_memory,
        gain_total,
        jnp.stack(in_totals, axis=1),
        mid_totals[0],
        mid_totals[1],
        jnp.stack([mid_totals[2], mid_totals[3]], axis=1),
        mid_totals[4],
        jnp.stack([mlp_totals[0], mlp_totals[1]], axis=1),
        mlp_totals[2],
    )


CORE, XDIM, YDIM = 1, 2, 4
PLANE = 8


def flip(value, bit):
    return lax.ppermute(value, "wide", [(i, i ^ bit) for i in range(PLANE)])


def unspread(piece):
    axes = ("wide", "narrow")
    first, second, _ = spread_tables(lax.axis_size("wide"), lax.axis_size("narrow"))
    piece = lax.ppermute(piece, axes, [(b, a) for a, b in second])
    return lax.ppermute(piece, axes, [(b, a) for a, b in first])


def plane_pieces(shard):
    half = shard.shape[0] // 2
    over_x = flip(shard, XDIM)
    over_y = flip(shard, YDIM)
    over_xy = (flip(over_x[:half], YDIM), flip(over_y[half:], XDIM))
    own = [(shard[:half], shard[half:]), (over_x[:half], over_x[half:])]
    own += [(over_y[:half], over_y[half:]), over_xy]
    partner = [flip(shard, CORE), flip(over_x, CORE), flip(over_y, CORE)]
    partner = [(part[:half], part[half:]) for part in partner]
    partner.append((flip(over_xy[0], CORE), flip(over_xy[1], CORE)))
    return [pair for both in zip(own, partner) for pair in both]


def plane_gather(shard):
    return jnp.concatenate([part for pair in plane_pieces(shard) for part in pair], axis=0)


def low(value):
    return value.astype(jnp.bfloat16)


def plus(kept, moved):
    return kept.astype(jnp.float32) + moved.astype(jnp.float32)


def plane_scatter(partial_rows):
    rows = partial_rows.shape[0] // PLANE
    half = rows // 2
    view = partial_rows.reshape(2, 2, 2, rows, -1)
    chip = low(plus(view[:, :, 0], flip(low(view[:, :, 1]), CORE)))
    part_a, part_b = chip[:, :, :half], chip[:, :, half:]
    part_a = plus(part_a[:, 0], flip(part_a[:, 1], XDIM))
    part_b = plus(part_b[0], flip(part_b[1], YDIM))
    done_a = plus(part_a[0], flip(low(part_a[1]), YDIM))
    done_b = plus(part_b[0], flip(low(part_b[1]), XDIM))
    return jnp.concatenate([done_a, done_b], axis=0)


def group_attend(queries, keys_all, values_all, allowed):
    scores = jnp.einsum(
        "gqhd,gkhd->ghqk", queries, keys_all, preferred_element_type=jnp.float32
    ) * HEAD_DIM ** (-0.5)
    scores = jnp.where(allowed[:, None], scores, NEGATIVE)
    row_top = jnp.max(scores, axis=3, keepdims=True)
    exp_scores = jnp.exp(scores - row_top)
    denom_sum = jnp.sum(exp_scores, axis=3, keepdims=True)
    soft_probs = low(exp_scores / denom_sum)
    result = jnp.einsum(
        "ghqk,gkhd->gqhd", soft_probs, values_all, preferred_element_type=jnp.float32
    )
    return (result, row_top + jnp.log(denom_sum))


def group_attend_back(queries, keys_all, values_all, allowed, log_sums, grad_out):
    score_scale = HEAD_DIM ** (-0.5)
    scores = (
        jnp.einsum("gqhd,gkhd->ghqk", queries, keys_all, preferred_element_type=jnp.float32)
        * score_scale
    )
    scores = jnp.where(allowed[:, None], scores, NEGATIVE)
    soft_probs = jnp.exp(scores - log_sums)
    grad_probs = jnp.einsum(
        "gqhd,gkhd->ghqk", grad_out, values_all, preferred_element_type=jnp.float32
    )
    row_inner = jnp.sum(soft_probs * grad_probs, axis=3, keepdims=True)
    grad_scores = low(soft_probs * (grad_probs - row_inner))
    grad_query = (
        jnp.einsum("ghqk,gkhd->gqhd", grad_scores, keys_all, preferred_element_type=jnp.float32)
        * score_scale
    )
    grad_keys = (
        jnp.einsum("ghqk,gqhd->gkhd", grad_scores, queries, preferred_element_type=jnp.float32)
        * score_scale
    )
    grad_values = jnp.einsum(
        "ghqk,gqhd->gkhd", low(soft_probs), grad_out, preferred_element_type=jnp.float32
    )
    return (grad_query, grad_keys, grad_values)


def narrow_full(pieces):
    rows, width = pieces[0].shape
    full = lax.all_gather(jnp.concatenate(pieces, axis=0), "narrow", axis=0, tiled=False)
    full = full.reshape(-1, len(pieces), rows, width)
    return [full[:, kind].reshape(-1, width) for kind in range(len(pieces))]


def narrow_total(term):
    return lax.psum_scatter(low(term), "narrow", scatter_dimension=0, tiled=True)


def placed(shards, spot_zero):
    rows = shards[0].shape[0]
    moved = spread(jnp.concatenate(shards, axis=0))
    kinds = len(shards)
    stacked = plane_gather(
        moved.reshape(kinds, 2, rows // 2, -1).swapaxes(0, 1).reshape(kinds * rows, -1)
    )
    width = stacked.shape[-1]
    stacked = stacked.reshape(PLANE, 2, kinds, rows // 2, width)
    order = [0] * PLANE
    for e in range(PLANE):
        ey, ex, ec = e >> 2, (e >> 1) & 1, e & 1
        order[4 * ey + 2 * ex + (ec ^ ey)] = e
    outs = []
    for kind in range(kinds):
        by_flip = jnp.stack([stacked[e, :, kind].reshape(rows, width) for e in order], axis=0)
        blocks = [
            lax.dynamic_index_in_dim(by_flip, spot_zero ^ j, 0, keepdims=False)
            for j in range(PLANE)
        ]
        outs.append(jnp.concatenate(blocks, axis=0).astype(jnp.float32))
    return outs


def per_device(
    tokens,
    memory,
    item_len,
    item_kind,
    norm_gains,
    w_self_in,
    w_self_out,
    w_cross_q,
    w_cross_kv,
    w_cross_out,
    w_mlp_in,
    w_mlp_out,
    cotangent,
):
    tok_rows, width = tokens.shape
    mem_rows = memory.shape[0]
    item_count = item_len.shape[1]
    gain = norm_gains.astype(jnp.float32)
    x = spread(tokens).astype(jnp.float32)
    h1 = low(normed(x, gain[0]))
    rows_one = plane_gather(h1)
    ws_q, ws_k, ws_v = narrow_full([w_self_in[:, 0], w_self_in[:, 1], w_self_in[:, 2]])
    ws_out, wc_q = narrow_full([w_self_out, w_cross_q])
    wc_k, wc_v = narrow_full([w_cross_kv[:, 0], w_cross_kv[:, 1]])
    (wc_out,) = narrow_full([w_cross_out])
    memory_all = plane_gather(spread(memory))
    units = w_mlp_out.shape[0] // 2
    mlp_shard = jnp.concatenate(
        [
            part[lo : lo + units]
            for lo in (0, units)
            for part in (w_mlp_in[:, 0], w_mlp_in[:, 1], w_mlp_out)
        ],
        axis=0,
    )
    mlp_pieces = plane_pieces(mlp_shard)
    wm_gate, wm_up, wm_out = (
        jnp.concatenate(
            [part[kind * units : (kind + 1) * units] for pair in mlp_pieces for part in pair],
            axis=0,
        )
        for kind in range(3)
    )

    me, level = lax.axis_index("wide"), lax.axis_index("narrow")
    differ = (me >> 1) ^ level
    side, upper = differ >> 1, differ & 1
    quarter = 2 * upper + ((me & 1) ^ side)
    spot_zero = 4 * side + quarter
    info_own = spread(jnp.concatenate([item_len, item_kind], axis=1))
    info = jnp.stack([info_own[0], flip(info_own, YDIM)[0]], axis=0)
    order = jnp.arange(PLANE // 2, dtype=jnp.int32)
    quarters = jnp.stack([quarter ^ order, quarter ^ 1 ^ order], axis=0)
    positions = (
        quarters[:, :, None] * tok_rows + jnp.arange(tok_rows, dtype=jnp.int32)
    ).reshape(2, -1)
    segment, token_valid, weight = jax.vmap(token_info, in_axes=(0, 0, 0, None))(
        info[:, :item_count], info[:, item_count:], positions, item_count
    )
    local_weight = weight[0, :tok_rows]
    self_ok = (segment[:, :, None] == segment[:, None, :]) & (
        positions[:, None, :] <= positions[:, :, None]
    )
    patch_rows = mem_rows * (PLANE // 2) // item_count
    mem_item = (
        (quarters[:, :, None] * mem_rows + jnp.arange(mem_rows, dtype=jnp.int32)) // patch_rows
    ).reshape(2, -1)
    cross_ok = mem_item[:, None, :] == jnp.minimum(segment, item_count - 1)[:, :, None]
    valid_float = token_valid.astype(jnp.float32)

    own_width = ws_out.shape[0]
    heads_here = own_width // HEAD_DIM

    def split(mat):
        return mat.reshape(2, -1, heads_here, HEAD_DIM)

    def merge(mat):
        return low(mat.reshape(-1, own_width))

    def project(rows, mat):
        return low(matmul_nt(rows, mat))

    sq, sk, sv = (split(project(rows_one, mat)) for mat in (ws_q, ws_k, ws_v))
    self_result, self_lse = group_attend(sq, sk, sv, self_ok)
    self_heads = merge(self_result)
    x1 = x + plane_scatter(matmul_nn(self_heads, ws_out))
    h2 = low(normed(x1, gain[1]))
    rows_two = plane_gather(h2)
    ck, cv = (split(project(memory_all, mat)) for mat in (wc_k, wc_v))
    cq = split(project(rows_two, wc_q))
    cross_result, cross_lse = group_attend(cq, ck, cv, cross_ok)
    cross_heads = merge(cross_result * valid_float[:, :, None, None])
    x2 = x1 + plane_scatter(matmul_nn(cross_heads, wc_out))
    h3 = low(normed(x2, gain[2]))
    grad_y = spread(cotangent).astype(jnp.float32) * local_weight[:, None]
    grad_mlp = row_gather(low(grad_y))
    rows_three = row_gather(h3)
    gate = matmul_nt(rows_three, wm_gate)
    up = matmul_nt(rows_three, wm_up)
    hidden = low(jax.nn.gelu(gate, approximate=True) * up)
    grad_hidden = matmul_nt(grad_mlp, wm_out)
    _, gelu_pull = jax.vjp(
        lambda gate_part, up_part: jax.nn.gelu(gate_part, approximate=True) * up_part, gate, up
    )
    grad_gate, grad_up = gelu_pull(grad_hidden)
    grad_gate, grad_up = low(grad_gate), low(grad_up)
    grad_h3 = branch_sum(matmul_nn(grad_gate, wm_gate) + matmul_nn(grad_up, wm_up))
    output = unspread(low(x2 + branch_sum(matmul_nn(hidden, wm_out))))
    _, norm_pull3 = jax.vjp(normed, x2, gain[2])
    part_x2, grad_gain3 = norm_pull3(grad_h3)
    grad_x2 = grad_y + part_x2
    grad_cross = plane_gather(low(grad_x2))
    mlp_totals = placed(
        [
            low(plane_scatter(matmul_tn(term, rows)))
            for term, rows in (
                (grad_gate, rows_three),
                (grad_up, rows_three),
                (hidden, grad_mlp),
            )
        ],
        spot_zero,
    )
    grad_cross_heads = split(project(grad_cross, wc_out))
    grad_cross_heads = jnp.where(
        token_valid[:, :, None, None], grad_cross_heads, jnp.zeros_like(grad_cross_heads)
    )
    grad_cq, grad_ck, grad_cv = (
        merge(mat)
        for mat in group_attend_back(cq, ck, cv, cross_ok, cross_lse, grad_cross_heads)
    )
    grad_h2 = plane_scatter(matmul_nn(grad_cq, wc_q))
    _, norm_pull2 = jax.vjp(normed, x1, gain[1])
    part_x1, grad_gain2 = norm_pull2(grad_h2)
    grad_x1 = grad_x2 + part_x1
    grad_self = plane_gather(low(grad_x1))
    mid_totals = placed(
        [
            narrow_total(matmul_tn(cross_heads, grad_cross)),
            narrow_total(matmul_tn(grad_cv, memory_all)),
            narrow_total(matmul_tn(grad_ck, memory_all)),
            narrow_total(matmul_tn(grad_cq, rows_two)),
            narrow_total(matmul_tn(self_heads, grad_self)),
        ],
        spot_zero,
    )
    grad_memory = unspread(
        low(plane_scatter(matmul_nn(grad_ck, wc_k) + matmul_nn(grad_cv, wc_v)))
    )
    grad_self_heads = split(project(grad_self, ws_out))
    gsq, gsk, gsv = (
        merge(mat) for mat in group_attend_back(sq, sk, sv, self_ok, self_lse, grad_self_heads)
    )
    in_totals = placed(
        [narrow_total(matmul_tn(term, rows_one)) for term in (gsq, gsk, gsv)], spot_zero
    )
    grad_h1 = plane_scatter(matmul_nn(gsq, ws_q) + matmul_nn(gsk, ws_k) + matmul_nn(gsv, ws_v))
    _, norm_pull1 = jax.vjp(normed, x, gain[0])
    part_x, grad_gain1 = norm_pull1(grad_h1)
    grad_tokens = unspread(low(grad_x1 + part_x))
    gain_terms = lax.psum(jnp.stack([grad_gain1, grad_gain2, grad_gain3]), ("wide", "narrow"))
    own_gains = width // lax.axis_size("narrow")
    return (
        output,
        grad_tokens,
        grad_memory,
        lax.dynamic_slice_in_dim(gain_terms, level * own_gains, own_gains, 1),
        jnp.stack(in_totals, axis=1),
        mid_totals[4],
        mid_totals[3],
        jnp.stack([mid_totals[2], mid_totals[1]], axis=1),
        mid_totals[0],
        jnp.stack([mlp_totals[0], mlp_totals[1]], axis=1),
        mlp_totals[2],
    )


def solution(mesh):
    in_plane = (mesh.shape["wide"], mesh.shape["narrow"]) == (8, 4)
    return jax.shard_map(
        per_device if in_plane else per_device_general,
        mesh=mesh,
        in_specs=(
            P(("wide", "narrow"), None),
            P(("wide", "narrow"), None),
            P("wide", None),
            P("wide", None),
            P(),
            P(("wide", "narrow"), None, None),
            P(("wide", "narrow"), None),
            P(("wide", "narrow"), None),
            P(("wide", "narrow"), None, None),
            P(("wide", "narrow"), None),
            P(("wide", "narrow"), None, None),
            P(("wide", "narrow"), None),
            P(("wide", "narrow"), None),
        ),
        out_specs=(
            P(("wide", "narrow"), None),
            P(("wide", "narrow"), None),
            P(("wide", "narrow"), None),
            P(None, "narrow"),
            P("narrow", None, None),
            P("narrow", None),
            P("narrow", None),
            P("narrow", None, None),
            P("narrow", None),
            P("narrow", None, None),
            P("narrow", None),
        ),
        check_vma=False,
    )
```

time: 2420 us -> 1300 us (0.54)
  waiting for transfers between devices: 1080 us -> 374 us
  local copies, waits for them, and re-layouts: 811 us -> 318 us
  starting transfers between devices: 46.8 us -> 224 us
  other arithmetic: 261 us -> 105 us
  blocking collectives: 9.94 us -> 62.5 us
    ppermute x0 -> x142, waiting for transfers between devices: none -> 337 us  [the longest x122 244 us: flip(): return lax.ppermute(value, 'wide', [(i, i ^ bit) for i in range(PLANE)])]
    reduce_scatter x7 -> x2, waiting for transfers between devices: 287 us -> 0.01 us  [branch_sum(): lax.psum_scatter(partial_rows.astype(jnp.bfloat16), 'narrow', scatter_dim...]
    all_to_all x14 -> x0, local copies, waits for them, and re-layouts: 268 us -> none  [the longest x2 89.7 us: own_fetch(): lax.all_to_all(flat[5], 'narrow', split_axis=1, concat_axis=0, tiled=True)]
    unnamed x30 -> x16, waiting for transfers between devices: 229 us -> 0.26 us
    ppermute x0 -> x142, starting transfers between devices: none -> 222 us  [the longest x122 162 us: flip(): return lax.ppermute(value, 'wide', [(i, i ^ bit) for i in range(PLANE)])]
    all_to_all x7 -> x0, waiting for transfers between devices: 219 us -> none  [the longest x1 109 us: own_fetch(): lax.all_to_all(flat[0], 'narrow', split_axis=1, concat_axis=0, tiled=True)]
    unnamed x9 -> x15, other arithmetic: 207 us -> 11.7 us
    all_gather x9 -> x4, waiting for transfers between devices: 139 us -> 0.03 us  [narrow_full(): lax.all_gather(jnp.concatenate(pieces, axis=0), 'narrow', axis=0, tiled=F...]
  transfers between devices with their start and end apart: 34 -> 158, of which waited for: 21 -> 52; matrix products, arithmetic and copies ran while one was open for 46% -> 40% of each run, Pallas kernels for 0% -> 0%
where the time goes in v1:
time: 1300 us; the launch traced here: 1280 us
  waiting for transfers between devices  374 us (29%)
  local copies, waits for them, and re-layouts  318 us (24%)
  starting transfers between devices  224 us (17%)
  matrix products  179 us (14%)
  other arithmetic  105 us (8%)
  blocking collectives  62.5 us (5%)
  between operations  18.7 us (1%)
    ppermute x122, waiting for transfers between devices, flip(): return lax.ppermute(value, 'wide', [(i, i ^ bit) for i in range(PLANE)])  244 us
    unnamed x498, local copies, waits for them, and re-layouts  214 us
    ppermute x122, starting transfers between devices, flip(): return lax.ppermute(value, 'wide', [(i, i ^ bit) for i in range(PLANE)])  162 us
    psum x1, blocking collectives, per_device(): lax.psum(jnp.stack([grad_gain1, grad_gain2, grad_gain3]), ('wide', 'narro...  62.5 us
    dot_general x11, matrix products, matmul_nt(): lax.dot_general(a, b, (((1,), (1,)), ((), ())), preferred_element_type=jn...  53.1 us
    dot_general x11, matrix products, matmul_tn(): lax.dot_general(a, b, (((0,), (0,)), ((), ())), preferred_element_type=jn...  47.2 us
    dot_general x11, matrix products, matmul_nn(): lax.dot_general(a, b, (((1,), (0,)), ((), ())), preferred_element_type=jn...  46.9 us
    ppermute x7, waiting for transfers between devices, spread(): piece = lax.ppermute(piece, axes, first)  45.4 us
  transfers between devices with their start and end apart: 158, of which 52 were waited for; matrix products, arithmetic and copies ran while one was open for 40% of the time, Pallas kernels for 0%

profile of v1, /device:TPU:25, one launch (start us, length us, event | category | flops | bytes accessed | tf_op | source)
XLA Modules:
  0.0 1281.7 jit_solution(14495890123668538554)
XLA Ops:
  33.1 45.4 %collective-permute-done.11 = s32[1,8]{1,0:T(1,128)S(1)} collective-permute-done((s32[1,8]{1,0:T(1,128)S(1)}, s32[1,8]{1,0:T(1,128)S(1)}, u32[]{:S(2)}, u32[]{:S(2)}) %collective-permute-start.11) | collective-permute-done | bytes 64 | tf_op jit(solution)/shard_map/ppermute | solution.py:98
  98.9 18.7 %collective-permute-done.1 = bf16[128,2048]{1,0:T(8,128)(2,1)S(1)} collective-permute-done((bf16[128,2048]{1,0:T(8,128)(2,1)}, bf16[128,2048]{1,0:T(8,128)(2,1)S(1)}, u32[]{:S(2)}, u32[]{:S(2)}) %collective-permute-start.1) | collective-permute-done | bytes 524320 | tf_op jit(solution)/shard_map/ppermute | solution.py:100
  120.5 8.5 collective-permute-done.56
  129.0 14.4 %collective-permute-start.3 = (bf16[128,2048]{1,0:T(8,128)(2,1)S(1)}, bf16[128,2048]{1,0:T(8,128)(2,1)S(1)}, u32[]{:S(2)}, u32[]{:S(2)}) collective-permute-start(bf16[128,2048]{1,0:T(8,128)(2,1)S(1)} %get-tuple-element.64), channel_id=1, source_target_pairs={{0,8},{4,12},{8,0},{12,4},{16,24},{20,28},{24,16},{28,20},{1,9},{5... | collective-permute-start | bytes 1572872 | tf_op jit(solution)/shard_map/ppermute | solution.py:322
  145.3 9.9 collective-permute-done.3
  160.5 23.9 %collective-permute-done.5 = bf16[128,2048]{1,0:T(8,128)(2,1)S(1)} collective-permute-done((bf16[128,2048]{1,0:T(8,128)(2,1)S(1)}, bf16[128,2048]{1,0:T(8,128)(2,1)S(1)}, u32[]{:S(2)}, u32[]{:S(2)}) %collective-permute-start.5) | collective-permute-done | bytes 524320 | tf_op jit(solution)/shard_map/ppermute | solution.py:322
  192.8 11.4 collective-permute-start.8
  222.7 16.7 %collective-permute-done.22 = bf16[256,2048]{1,0:T(8,128)(2,1)} collective-permute-done((bf16[256,2048]{1,0:T(8,128)(2,1)}, bf16[256,2048]{1,0:T(8,128)(2,1)}, u32[]{:S(2)}, u32[]{:S(2)}) %collective-permute-start.22) | collective-permute-done | bytes 1048608 | tf_op jit(solution)/shard_map/ppermute | solution.py:322
  310.3 7.8 collective-permute-done.15
  326.1 18.7 %collective-permute-done.18 = bf16[64,2048]{1,0:T(8,128)(2,1)S(1)} collective-permute-done((bf16[64,2048]{1,0:T(8,128)(2,1)S(1)}, bf16[64,2048]{1,0:T(8,128)(2,1)S(1)}, u32[]{:S(2)}, u32[]{:S(2)}) %collective-permute-start.18) | collective-permute-done | bytes 262176 | tf_op jit(solution)/shard_map/ppermute | solution.py:322
  361.2 7.1 convolution_convert_fusion.10
  458.5 7.9 fusion.199
  469.4 25.8 %all-gather.11.cloned.1.call-done = bf16[512,2048]{1,0:T(8,128)(2,1)} async-done(((bf16[128,2048]{1,0:T(8,128)(2,1)}), bf16[512,2048]{1,0:T(8,128)(2,1)}) %all-gather.11.cloned.1.call-update) | async-done | bytes 2097168 | tf_op jit(solution)/shard_map/all_gather | solution.py:135
  501.5 8.5 fusion.31
  574.6 11.2 collective-permute-done.124
  589.4 10.5 collective-permute-done.129
  682.4 6.8 convolution_convert_fusion.8
  703.7 7.0 convolution_convert_fusion.7
  716.0 9.8 convolution_add_fusion
  792.2 10.6 reduce-scatter.27.cloned.1.call-done
  804.5 12.8 collective-permute-done.132
  818.6 24.2 %collective-permute-start.134 = (bf16[480,2048]{1,0:T(8,128)(2,1)}, bf16[480,2048]{1,0:T(8,128)(2,1)}, u32[]{:S(2)}, u32[]{:S(2)}) collective-permute-start(bf16[480,2048]{1,0:T(8,128)(2,1)} %bitcast.273), channel_id=1, source_target_pairs={{0,8},{4,12},{8,0},{12,4},{16,24},{20,28},{24,16},{28,20},{1,9},{5... | collective-permute-start | bytes 5898248 | tf_op jit(solution)/shard_map/ppermute | solution.py:322
  880.2 8.8 add_add_fusion
  909.7 8.4 collective-permute-done.88
  926.6 23.8 %collective-permute-done.91 = bf16[128,2048]{1,0:T(8,128)(2,1)S(1)} collective-permute-done((bf16[128,2048]{1,0:T(8,128)(2,1)S(1)}, bf16[128,2048]{1,0:T(8,128)(2,1)S(1)}, u32[]{:S(2)}, u32[]{:S(2)}) %collective-permute-start.91) | collective-permute-done | bytes 524320 | tf_op jit(solution)/shard_map/ppermute | solution.py:322
  1010.0 12.4 maximum_convert_fusion
  1041.3 35.2 %copy.278 = f32[1280,2,2048]{2,1,0:T(2,128)} copy(f32[1280,2,2048]{2,0,1:T(8,128)} %maximum_convert_fusion) | data formatting | bytes 41943040
  1092.2 62.5 %psum.7 = f32[3,2048]{1,0:T(4,128)S(1)} all-reduce(f32[3,2048]{1,0:T(4,128)S(1)} %pad_maximum_fusion.7), channel_id=1, replica_groups=mesh['wide'=8,'narrow'=4] {'wide','narrow'}, use_global_device_ids=true, to_apply=%region_20.21 | all-reduce | flops 6144 | bytes 49152 | tf_op jit(solution)/shard_map/psum | solution.py:608
  1163.3 16.1 %collective-permute-done.97 = bf16[192,2048]{1,0:T(8,128)(2,1)S(1)} collective-permute-done((bf16[192,2048]{1,0:T(8,128)(2,1)S(1)}, bf16[192,2048]{1,0:T(8,128)(2,1)S(1)}, u32[]{:S(2)}, u32[]{:S(2)}) %collective-permute-start.97) | collective-permute-done | bytes 786464 | tf_op jit(solution)/shard_map/ppermute | solution.py:322
  1201.7 19.0 %collective-permute-done.108 = bf16[320,2048]{1,0:T(8,128)(2,1)S(1)} collective-permute-done((bf16[320,2048]{1,0:T(8,128)(2,1)S(1)}, bf16[320,2048]{1,0:T(8,128)(2,1)S(1)}, u32[]{:S(2)}, u32[]{:S(2)}) %collective-permute-start.108) | collective-permute-done | bytes 1310752 | tf_op jit(solution)/shard_map/ppermute | solution.py:322
  1227.2 7.3 maximum_convert_fusion.1
  1255.9 11.1 copy.277
  (1074 shorter events, 740.8 us)
Async XLA Ops:
  7.2 233.0 %all-gather.17.cloned.1.call-start = ((), (), s32[]{:S(2)}) async-start(), calls=%async_computation.23 | async-start | bytes 2621440 | tf_op jit(solution)/shard_map/all_gather | solution.py:414
  9.2 234.3 %all-gather.15.cloned.1.call-start = ((), (), s32[]{:S(2)}) async-start(), calls=%async_computation.22 | async-start | bytes 3932160 | tf_op jit(solution)/shard_map/all_gather | solution.py:414
  11.4 275.0 %all-gather.19.cloned.1.call-start = ((), (), s32[]{:S(2)}) async-start(), calls=%async_computation.24 | async-start | bytes 2621440 | tf_op jit(solution)/shard_map/all_gather | solution.py:414
  13.3 396.9 %all-gather.21.cloned.1.call-start = ((), (), s32[]{:S(2)}) async-start(), calls=%async_computation.25 | async-start | bytes 1310720 | tf_op jit(solution)/shard_map/all_gather | solution.py:414
  20.9 163.7 %collective-permute-start.44 = (bf16[480,2048]{1,0:T(8,128)(2,1)}, bf16[480,2048]{1,0:T(8,128)(2,1)}, u32[]{:S(2)}, u32[]{:S(2)}) collective-permute-start(bf16[480,2048]{1,0:T(8,128)(2,1)} %constant_dynamic-update-slice_fusion.30), channel_id=1, source_target_pairs={{0,4},{4,0},{8,12},{12,8},{16,20},{20,16},{24,28},{28,24},{1,5},{5... | collective-permute-start | bytes 5898248 | tf_op jit(solution)/shard_map/ppermute | solution.py:322
  21.6 182.7 %collective-permute-start.45 = (bf16[480,2048]{1,0:T(8,128)(2,1)}, bf16[480,2048]{1,0:T(8,128)(2,1)}, u32[]{:S(2)}, u32[]{:S(2)}) collective-permute-start(bf16[480,2048]{1,0:T(8,128)(2,1)} %constant_dynamic-update-slice_fusion.30), channel_id=1, source_target_pairs={{0,8},{4,12},{8,0},{12,4},{16,24},{20,28},{24,16},{28,20},{1,9},{5... | collective-permute-start | bytes 5898248 | tf_op jit(solution)/shard_map/ppermute | solution.py:322
  22.8 74.1 %collective-permute-start.55 = (bf16[128,2048]{1,0:T(8,128)(2,1)S(1)}, bf16[128,2048]{1,0:T(8,128)(2,1)}, u32[]{:S(2)}, u32[]{:S(2)}) collective-permute-start(bf16[128,2048]{1,0:T(8,128)(2,1)S(1)} %copy-done.97), channel_id=1, source_target_pairs={{0,0},{1,5},{2,10},{3,15},{4,20},{5,17},{6,30},{7,27},{8,8},{9,13}... | collective-permute-start | bytes 1572872 | tf_op jit(solution)/shard_map/ppermute | solution.py:98
  31.8 426.7 %all-gather.13.cloned.1.call-start = ((), (), s32[]{:S(2)}) async-start(), calls=%async_computation.12 | async-start | bytes 2621440 | tf_op jit(solution)/shard_map/all_gather | solution.py:135
  129.0 82.5 %collective-permute-start.47 = (bf16[480,2048]{1,0:T(8,128)(2,1)}, bf16[480,2048]{1,0:T(8,128)(2,1)}, u32[]{:S(2)}, u32[]{:S(2)}) collective-permute-start(bf16[480,2048]{1,0:T(8,128)(2,1)} %constant_dynamic-update-slice_fusion.30), channel_id=1, source_target_pairs={{0,16},{4,20},{8,24},{12,28},{16,0},{20,4},{24,8},{28,12},{1,17},{... | collective-permute-start | bytes 5898248 | tf_op jit(solution)/shard_map/ppermute | solution.py:322
  144.5 350.8 %all-gather.11.cloned.1.call-start = ((), (), s32[]{:S(2)}) async-start(), calls=%async_computation.10 | async-start | bytes 2621440 | tf_op jit(solution)/shard_map/all_gather | solution.py:135
  289.1 128.3 %collective-permute-start.49 = (bf16[240,2048]{1,0:T(8,128)(2,1)}, bf16[240,2048]{1,0:T(8,128)(2,1)}, u32[]{:S(2)}, u32[]{:S(2)}) collective-permute-start(bf16[240,2048]{1,0:T(8,128)(2,1)} %slice.1389), channel_id=1, source_target_pairs={{0,16},{4,20},{8,24},{12,28},{16,0},{20,4},{24,8},{28,12},{1,17},{... | collective-permute-start | bytes 2949128 | tf_op jit(solution)/shard_map/ppermute | solution.py:322
  308.5 109.4 %collective-permute-start.50 = (bf16[240,2048]{1,0:T(8,128)(2,1)}, bf16[240,2048]{1,0:T(8,128)(2,1)}, u32[]{:S(2)}, u32[]{:S(2)}) collective-permute-start(bf16[240,2048]{1,0:T(8,128)(2,1)} %slice.1391), channel_id=1, source_target_pairs={{0,8},{4,12},{8,0},{12,4},{16,24},{20,28},{24,16},{28,20},{1,9},{5... | collective-permute-start | bytes 2949128 | tf_op jit(solution)/shard_map/ppermute | solution.py:322
  447.8 166.8 %reduce-scatter.13.cloned.1.call-start = ((), (), s32[]{:S(2)}) async-start(), calls=%async_computation.13 | async-start | bytes 2621440 | tf_op jit(solution)/shard_map/reduce_scatter | solution.py:139
  517.0 97.6 %reduce-scatter.11.cloned.1.call-start = ((), (), s32[]{:S(2)}) async-start(), calls=%async_computation.11 | async-start | bytes 2621440 | tf_op jit(solution)/shard_map/reduce_scatter | solution.py:139
  550.8 210.1 %reduce-scatter.21.cloned.1.call-start = ((), (), s32[]{:S(2)}) async-start(), calls=%async_computation.17 | async-start | bytes 1310720 | tf_op jit(solution)/shard_map/reduce_scatter | solution.py:420
  642.6 134.4 %collective-permute-start.131 = (bf16[480,2048]{1,0:T(8,128)(2,1)}, bf16[480,2048]{1,0:T(8,128)(2,1)}, u32[]{:S(2)}, u32[]{:S(2)}) collective-permute-start(bf16[480,2048]{1,0:T(8,128)(2,1)} %constant_dynamic-update-slice_fusion.258), channel_id=1, source_target_pairs={{0,0},{1,5},{2,10},{3,15},{4,20},{5,17},{6,30},{7,27},{8,8},{9,13}... | collective-permute-start | bytes 5898248 | tf_op jit(solution)/shard_map/ppermute | solution.py:98
  647.1 109.9 %collective-permute-start.54 = (bf16[128,2048]{1,0:T(8,128)(2,1)}, bf16[128,2048]{1,0:T(8,128)(2,1)}, u32[]{:S(2)}, u32[]{:S(2)}) collective-permute-start(bf16[128,2048]{1,0:T(8,128)(2,1)} %collective-permute-done.53), channel_id=1, source_target_pairs={{0,0},{5,1},{10,2},{15,3},{20,4},{17,5},{30,6},{27,7},{8,8},{13,9}... | collective-permute-start | bytes 1572872 | tf_op jit(solution)/shard_map/ppermute | solution.py:329
  659.4 103.2 %reduce-scatter.23.cloned.1.call-start = ((), (), s32[]{:S(2)}) async-start(), calls=%async_computation.18 | async-start | bytes 1310720 | tf_op jit(solution)/shard_map/reduce_scatter | solution.py:420
  689.2 78.8 %reduce-scatter.25.cloned.1.call-start = ((), (), s32[]{:S(2)}) async-start(), calls=%async_computation.19 | async-start | bytes 1310720 | tf_op jit(solution)/shard_map/reduce_scatter | solution.py:420
  711.8 90.9 %reduce-scatter.27.cloned.1.call-start = ((), (), s32[]{:S(2)}) async-start(), calls=%async_computation.20 | async-start | bytes 1310720 | tf_op jit(solution)/shard_map/reduce_scatter | solution.py:420
  757.0 197.2 %reduce-scatter.29.cloned.1.call-start = ((), (), s32[]{:S(2)}) async-start(), calls=%async_computation.21 | async-start | bytes 1310720 | tf_op jit(solution)/shard_map/reduce_scatter | solution.py:420
  777.0 112.1 %collective-permute-start.87 = (bf16[2,2,256,2048]{3,2,1,0:T(8,128)(2,1)}, bf16[2,2,256,2048]{3,2,1,0:T(8,128)(2,1)}, u32[]{:S(2)}, u32[]{:S(2)}) collective-permute-start(bf16[2,2,256,2048]{3,2,1,0:T(8,128)(2,1)} %fusion.12), channel_id=1, source_target_pairs={{0,4},{4,0},{8,12},{12,8},{16,20},{20,16},{24,28},{28,24},{1,5},{5... | collective-permute-start | bytes 12582920 | tf_op jit(solution)/shard_map/ppermute | solution.py:322
  791.7 164.1 %reduce-scatter.19.cloned.1.call-start = ((), (), s32[]{:S(2)}) async-start(), calls=%async_computation.16 | async-start | bytes 1310720 | tf_op jit(solution)/shard_map/reduce_scatter | solution.py:420
  818.6 87.5 %collective-permute-start.133 = (bf16[480,2048]{1,0:T(8,128)(2,1)}, bf16[480,2048]{1,0:T(8,128)(2,1)}, u32[]{:S(2)}, u32[]{:S(2)}) collective-permute-start(bf16[480,2048]{1,0:T(8,128)(2,1)} %bitcast.273), channel_id=1, source_target_pairs={{0,4},{4,0},{8,12},{12,8},{16,20},{20,16},{24,28},{28,24},{1,5},{5... | collective-permute-start | bytes 5898248 | tf_op jit(solution)/shard_map/ppermute | solution.py:322
  818.6 82.2 %collective-permute-start.134 = (bf16[480,2048]{1,0:T(8,128)(2,1)}, bf16[480,2048]{1,0:T(8,128)(2,1)}, u32[]{:S(2)}, u32[]{:S(2)}) collective-permute-start(bf16[480,2048]{1,0:T(8,128)(2,1)} %bitcast.273), channel_id=1, source_target_pairs={{0,8},{4,12},{8,0},{12,4},{16,24},{20,28},{24,16},{28,20},{1,9},{5... | collective-permute-start | bytes 5898248 | tf_op jit(solution)/shard_map/ppermute | solution.py:322
  857.2 98.6 %reduce-scatter.17.cloned.1.call-start = ((), (), s32[]{:S(2)}) async-start(), calls=%async_computation.15 | async-start | bytes 1310720 | tf_op jit(solution)/shard_map/reduce_scatter | solution.py:420
  873.1 82.7 %reduce-scatter.15.cloned.1.call-start = ((), (), s32[]{:S(2)}) async-start(), calls=%async_computation.14 | async-start | bytes 1310720 | tf_op jit(solution)/shard_map/reduce_scatter | solution.py:420
  957.9 132.4 %collective-permute-start.92 = (bf16[256,2048]{1,0:T(8,128)(2,1)S(1)}, bf16[256,2048]{1,0:T(8,128)(2,1)}, u32[]{:S(2)}, u32[]{:S(2)}) collective-permute-start(bf16[256,2048]{1,0:T(8,128)(2,1)S(1)} %pad_maximum_fusion.2), channel_id=1, source_target_pairs={{0,0},{4,5},{8,10},{12,15},{20,20},{16,17},{28,30},{24,27},{9,8},{... | collective-permute-start | bytes 3145736 | tf_op jit(solution)/shard_map/ppermute | solution.py:328
  981.4 95.2 %collective-permute-start.94 = (bf16[192,2048]{1,0:T(8,128)(2,1)}, bf16[192,2048]{1,0:T(8,128)(2,1)}, u32[]{:S(2)}, u32[]{:S(2)}) collective-permute-start(bf16[192,2048]{1,0:T(8,128)(2,1)} %pad_maximum_fusion.4), channel_id=1, source_target_pairs={{0,0},{1,5},{2,10},{3,15},{4,20},{5,17},{6,30},{7,27},{8,8},{9,13}... | collective-permute-start | bytes 2359304 | tf_op jit(solution)/shard_map/ppermute | solution.py:98
  986.4 169.0 %collective-permute-start.105 = (bf16[320,2048]{1,0:T(8,128)(2,1)}, bf16[320,2048]{1,0:T(8,128)(2,1)}, u32[]{:S(2)}, u32[]{:S(2)}) collective-permute-start(bf16[320,2048]{1,0:T(8,128)(2,1)} %constant_dynamic-update-slice_fusion.162), channel_id=1, source_target_pairs={{0,0},{1,5},{2,10},{3,15},{4,20},{5,17},{6,30},{7,27},{8,8},{9,13}... | collective-permute-start | bytes 3932168 | tf_op jit(solution)/shard_map/ppermute | solution.py:98
  1076.6 81.9 %collective-permute-start.95 = (bf16[192,2048]{1,0:T(8,128)(2,1)}, bf16[192,2048]{1,0:T(8,128)(2,1)S(1)}, u32[]{:S(2)}, u32[]{:S(2)}) collective-permute-start(bf16[192,2048]{1,0:T(8,128)(2,1)} %collective-permute-done.94), channel_id=1, source_target_pairs={{0,0},{5,4},{10,8},{15,12},{20,20},{17,16},{30,28},{27,24},{8,9},{... | collective-permute-start | bytes 2359304 | tf_op jit(solution)/shard_map/ppermute | solution.py:100
  1080.9 80.6 %collective-permute-start.86 = (bf16[128,2048]{1,0:T(8,128)(2,1)}, bf16[128,2048]{1,0:T(8,128)(2,1)}, u32[]{:S(2)}, u32[]{:S(2)}) collective-permute-start(bf16[128,2048]{1,0:T(8,128)(2,1)} %collective-permute-done.85), channel_id=1, source_target_pairs={{0,0},{5,1},{10,2},{15,3},{20,4},{17,5},{30,6},{27,7},{8,8},{13,9}... | collective-permute-start | bytes 1572872 | tf_op jit(solution)/shard_map/ppermute | solution.py:329
  (246 other events, 4958.7 us)
Sparse Core Ops, SparseCore 0:
  10.1 44.8 all-gather.16
  57.2 78.1 all-gather.14
  136.9 66.8 all-gather.18
  205.2 32.2 all-gather.20
  239.5 44.9 all-gather.12
  447.9 47.3 all-gather.10
  517.1 42.7 reduce-scatter.12
  562.3 42.8 reduce-scatter.10
  659.5 38.5 reduce-scatter.20
  700.3 27.6 reduce-scatter.22
  730.2 25.7 reduce-scatter.24
  758.8 43.9 reduce-scatter.26
  805.1 59.0 reduce-scatter.28
  866.3 25.7 reduce-scatter.18
  894.3 25.7 reduce-scatter.16
  922.9 25.7 reduce-scatter.14

commit v2 on v1

--- a/solution.py
+++ b/solution.py
@@ -1,6 +1,8 @@
 import jax
 import jax.numpy as jnp
 from jax import lax
+from jax.experimental import pallas as pl
+from jax.experimental.pallas import tpu as pltpu
 from jax.sharding import PartitionSpec as P
 
 HEAD_DIM = 128
@@ -99,6 +101,16 @@
     if second is not None:
         piece = lax.ppermute(piece, axes, second)
     return piece
+
+
+def plane_hop(piece):
+    first, _, _ = spread_tables(lax.axis_size("wide"), lax.axis_size("narrow"))
+    return lax.ppermute(piece, ("wide", "narrow"), first)
+
+
+def level_hop(piece):
+    _, second, _ = spread_tables(lax.axis_size("wide"), lax.axis_size("narrow"))
+    return lax.ppermute(piece, ("wide", "narrow"), second)
 
 
 def wide_gather(pieces):
@@ -329,42 +341,55 @@
     return lax.ppermute(piece, axes, [(b, a) for a, b in first])
 
 
-def plane_pieces(shard):
-    half = shard.shape[0] // 2
-    over_x = flip(shard, XDIM)
-    over_y = flip(shard, YDIM)
-    over_xy = (flip(over_x[:half], YDIM), flip(over_y[half:], XDIM))
-    own = [(shard[:half], shard[half:]), (over_x[:half], over_x[half:])]
-    own += [(over_y[:half], over_y[half:]), over_xy]
-    partner = [flip(shard, CORE), flip(over_x, CORE), flip(over_y, CORE)]
-    partner = [(part[:half], part[half:]) for part in partner]
-    partner.append((flip(over_xy[0], CORE), flip(over_xy[1], CORE)))
-    return [pair for both in zip(own, partner) for pair in both]
-
-
-def plane_gather(shard):
-    return jnp.concatenate([part for pair in plane_pieces(shard) for part in pair], axis=0)
+def after(value, *others):
+    return lax.optimization_barrier((value,) + others)[0]
 
 
 def low(value):
-    return value.astype(jnp.bfloat16)
+    return jax.tree.map(lambda part: part.astype(jnp.bfloat16), value)
 
 
 def plus(kept, moved):
     return kept.astype(jnp.float32) + moved.astype(jnp.float32)
 
 
-def plane_scatter(partial_rows):
-    rows = partial_rows.shape[0] // PLANE
+def side_pieces(shard):
+    return [shard, flip(shard, XDIM), flip(shard, YDIM)]
+
+
+def corner_pieces(sides):
+    half = sides[0].shape[-2] // 2
+    return sides + [flip(sides[1][..., :half, :], YDIM), flip(sides[2][..., half:, :], XDIM)]
+
+
+def chip_pieces(shard):
+    return corner_pieces(side_pieces(shard))
+
+
+def plane_gather(shard):
+    own = jnp.concatenate(chip_pieces(shard), axis=0)
+    return (own, flip(own, CORE))
+
+
+def plane_scatter(kept, sent):
+    return scatter_end(*scatter_start(kept, sent))
+
+
+def scatter_start(kept, sent):
+    chip = low(plus(kept, flip(low(sent), CORE)))
+    lead, rows, width = chip.shape[:-2], chip.shape[-2] // 4, chip.shape[-1]
     half = rows // 2
-    view = partial_rows.reshape(2, 2, 2, rows, -1)
-    chip = low(plus(view[:, :, 0], flip(low(view[:, :, 1]), CORE)))
-    part_a, part_b = chip[:, :, :half], chip[:, :, half:]
+    view = jnp.moveaxis(chip.reshape(lead + (2, 2, rows, width)), (-4, -3), (0, 1))
+    part_a, part_b = view[..., :half, :], view[..., half:, :]
     part_a = plus(part_a[:, 0], flip(part_a[:, 1], XDIM))
     part_b = plus(part_b[0], flip(part_b[1], YDIM))
+    return (part_a, part_b)
+
+
+def scatter_end(part_a, part_b):
     done_a = plus(part_a[0], flip(low(part_a[1]), YDIM))
     done_b = plus(part_b[0], flip(low(part_b[1]), XDIM))
-    return jnp.concatenate([done_a, done_b], axis=0)
+    return jnp.concatenate([done_a, done_b], axis=-2)
 
 
 def group_attend(queries, keys_all, values_all, allowed):
@@ -409,39 +434,153 @@
     return (grad_query, grad_keys, grad_values)
 
 
-def narrow_full(pieces):
-    rows, width = pieces[0].shape
-    full = lax.all_gather(jnp.concatenate(pieces, axis=0), "narrow", axis=0, tiled=False)
-    full = full.reshape(-1, len(pieces), rows, width)
-    return [full[:, kind].reshape(-1, width) for kind in range(len(pieces))]
+def narrow_full(stacked):
+    kinds, rows, width = stacked.shape
+    full = lax.all_gather(stacked.reshape(kinds * rows, width), "narrow", axis=0, tiled=False)
+    full = full.reshape(-1, kinds, rows, width)
+    return [full[:, kind].reshape(-1, width) for kind in range(kinds)]
 
 
 def narrow_total(term):
     return lax.psum_scatter(low(term), "narrow", scatter_dimension=0, tiled=True)
 
 
-def placed(shards, spot_zero):
-    rows = shards[0].shape[0]
-    moved = spread(jnp.concatenate(shards, axis=0))
-    kinds = len(shards)
-    stacked = plane_gather(
-        moved.reshape(kinds, 2, rows // 2, -1).swapaxes(0, 1).reshape(kinds * rows, -1)
-    )
-    width = stacked.shape[-1]
-    stacked = stacked.reshape(PLANE, 2, kinds, rows // 2, width)
-    order = [0] * PLANE
-    for e in range(PLANE):
-        ey, ex, ec = e >> 2, (e >> 1) & 1, e & 1
-        order[4 * ey + 2 * ex + (ec ^ ey)] = e
-    outs = []
-    for kind in range(kinds):
-        by_flip = jnp.stack([stacked[e, :, kind].reshape(rows, width) for e in order], axis=0)
-        blocks = [
-            lax.dynamic_index_in_dim(by_flip, spot_zero ^ j, 0, keepdims=False)
-            for j in range(PLANE)
-        ]
-        outs.append(jnp.concatenate(blocks, axis=0).astype(jnp.float32))
-    return outs
+PIECE_FLIPS = (0, 2, 5, 7, 1, 3, 4, 6)
+
+
+def place_body(spots, *refs, plan, source_count):
+    sources, outs = refs[:source_count], refs[source_count:]
+    step, part = pl.program_id(0), pl.program_id(1)
+
+    def write(source):
+        for out, kinds in zip(outs, plan):
+            if len(kinds) == 1:
+                out[...] = source[kinds[0]].astype(jnp.float32)
+            elif len(kinds) == 2:
+                for slot, kind in enumerate(kinds):
+                    out[:, slot, :] = source[kind].astype(jnp.float32)
+            else:
+                for slot, kind in enumerate(kinds):
+                    out[slot] = source[kind].astype(jnp.float32)
+
+    for number, source in enumerate(sources):
+        which, spot = number // 5, number % 5
+        if spot < 3:
+            hit = step == 4 * which + spot
+        else:
+            hit = (step == 4 * which + 3) & (part == spot - 3)
+
+        @pl.when(hit)
+        def _(source=source):
+            write(source)
+
+
+def core_pieces(chip):
+    return chip + [flip(piece, CORE) for piece in chip]
+
+
+def placed(sources, spot_zero, plan):
+    kinds, rows, width = sources[0].shape
+    half = rows // 2
+    spots = spot_zero ^ jnp.asarray(PIECE_FLIPS, jnp.int32)
+
+    def source_spec(number):
+        which, spot = number // 5, number % 5
+        if spot >= 3:
+            return pl.BlockSpec((kinds, half, width), lambda step, part, spots: (0, 0, 0))
+        mine = 4 * which + spot
+
+        def index(step, part, spots):
+            return (0, jnp.where(step == mine, part, jnp.where(step < mine, 0, 1)), 0)
+
+        return pl.BlockSpec((kinds, half, width), index)
+
+    out_specs, out_shapes = [], []
+    for group in plan:
+        count = len(group)
+        if count == 1:
+            block, shape = (half, width), (PLANE * rows, width)
+            index = lambda step, part, spots: (2 * spots[step] + part, 0)
+        elif count == 2:
+            block, shape = (half, 2, width), (PLANE * rows, 2, width)
+            index = lambda step, part, spots: (2 * spots[step] + part, 0, 0)
+        else:
+            block, shape = (count, half, width), (count, PLANE * rows, width)
+            index = lambda step, part, spots: (0, 2 * spots[step] + part, 0)
+        out_specs.append(pl.BlockSpec(block, index))
+        out_shapes.append(jax.ShapeDtypeStruct(shape, jnp.float32))
+    body = lambda *refs: place_body(*refs, plan=plan, source_count=len(sources))
+    return pl.pallas_call(
+        body,
+        grid_spec=pltpu.PrefetchScalarGridSpec(
+            num_scalar_prefetch=1,
+            grid=(PLANE, 2),
+            in_specs=[source_spec(number) for number in range(len(sources))],
+            out_specs=out_specs,
+        ),
+        out_shape=out_shapes,
+        compiler_params=pltpu.CompilerParams(
+            dimension_semantics=("arbitrary", "arbitrary"), vmem_limit_bytes=56 * 1024 * 1024
+        ),
+        name="place",
+    )(spots, *sources)
+
+
+def laid_body(spots, source, *outs, plan):
+    for out, kinds in zip(outs, plan):
+        if len(kinds) == 1:
+            out[...] = source[0, kinds[0]].astype(jnp.float32)
+        else:
+            for slot, kind in enumerate(kinds):
+                value = source[0, kind].astype(jnp.float32)
+                if len(kinds) == 2:
+                    out[:, slot, :] = value
+                else:
+                    out[slot] = value
+
+
+def laid(moved, plan):
+    kinds, rows, width = moved.shape
+    half = rows // 2
+    full = lax.all_gather(moved.reshape(kinds * rows, width), "wide", axis=0, tiled=False)
+    full = full.reshape(PLANE, kinds, rows, width)
+    _, _, spots = spread_tables(lax.axis_size("wide"), lax.axis_size("narrow"))
+    order = jnp.asarray(spots, jnp.int32)[lax.axis_index("narrow")]
+    out_specs, out_shapes = [], []
+    for group in plan:
+        count = len(group)
+        if count == 1:
+            block, shape = (half, width), (PLANE * rows, width)
+            index = lambda step, part, spots: (2 * step + part, 0)
+        elif count == 2:
+            block, shape = (half, 2, width), (PLANE * rows, 2, width)
+            index = lambda step, part, spots: (2 * step + part, 0, 0)
+        else:
+            block, shape = (count, half, width), (count, PLANE * rows, width)
+            index = lambda step, part, spots: (0, 2 * step + part, 0)
+        out_specs.append(pl.BlockSpec(block, index))
+        out_shapes.append(jax.ShapeDtypeStruct(shape, jnp.float32))
+    source_spec = pl.BlockSpec(
+        (1, kinds, half, width), lambda step, part, spots: (spots[step], 0, part, 0)
+    )
+    return pl.pallas_call(
+        lambda *refs: laid_body(*refs, plan=plan),
+        grid_spec=pltpu.PrefetchScalarGridSpec(
+            num_scalar_prefetch=1, grid=(PLANE, 2), in_specs=[source_spec], out_specs=out_specs
+        ),
+        out_shape=out_shapes,
+        compiler_params=pltpu.CompilerParams(
+            dimension_semantics=("arbitrary", "arbitrary"), vmem_limit_bytes=32 * 1024 * 1024
+        ),
+        name="laid",
+    )(order, full)
+
+
+def wide_full(stacked):
+    kinds, rows, width = stacked.shape
+    full = lax.all_gather(stacked.reshape(kinds * rows, width), "wide", axis=0, tiled=False)
+    full = full.reshape(-1, kinds, rows, width)
+    return [full[:, kind].reshape(-1, width) for kind in range(kinds)]
 
 
 def per_device(
@@ -463,31 +602,18 @@
     mem_rows = memory.shape[0]
     item_count = item_len.shape[1]
     gain = norm_gains.astype(jnp.float32)
-    x = spread(tokens).astype(jnp.float32)
+    tokens_here = spread(tokens)
+    ws_q, ws_k, ws_v = narrow_full(after(w_self_in.swapaxes(0, 1), tokens_here))
+    x = tokens_here.astype(jnp.float32)
     h1 = low(normed(x, gain[0]))
     rows_one = plane_gather(h1)
-    ws_q, ws_k, ws_v = narrow_full([w_self_in[:, 0], w_self_in[:, 1], w_self_in[:, 2]])
-    ws_out, wc_q = narrow_full([w_self_out, w_cross_q])
-    wc_k, wc_v = narrow_full([w_cross_kv[:, 0], w_cross_kv[:, 1]])
-    (wc_out,) = narrow_full([w_cross_out])
-    memory_all = plane_gather(spread(memory))
-    units = w_mlp_out.shape[0] // 2
-    mlp_shard = jnp.concatenate(
-        [
-            part[lo : lo + units]
-            for lo in (0, units)
-            for part in (w_mlp_in[:, 0], w_mlp_in[:, 1], w_mlp_out)
-        ],
-        axis=0,
-    )
-    mlp_pieces = plane_pieces(mlp_shard)
-    wm_gate, wm_up, wm_out = (
-        jnp.concatenate(
-            [part[kind * units : (kind + 1) * units] for pair in mlp_pieces for part in pair],
-            axis=0,
-        )
-        for kind in range(3)
-    )
+    ws_out, wc_q = narrow_full(after(jnp.stack([w_self_out, w_cross_q]), ws_q))
+    wc_k, wc_v = narrow_full(after(w_cross_kv.swapaxes(0, 1), ws_out))
+    (wc_out,) = narrow_full(after(w_cross_out[None], wc_k))
+    wm_gate, wm_up = wide_full(after(w_mlp_in.swapaxes(0, 1), wc_out))
+    memory_here = level_hop(after(plane_hop(memory), tokens_here))
+    memory_all = plane_gather(after(memory_here, rows_one[0]))
+    cotangent_here = level_hop(after(plane_hop(cotangent), memory_here))
 
     me, level = lax.axis_index("wide"), lax.axis_index("narrow")
     differ = (me >> 1) ^ level
@@ -496,7 +622,7 @@
     spot_zero = 4 * side + quarter
     info_own = spread(jnp.concatenate([item_len, item_kind], axis=1))
     info = jnp.stack([info_own[0], flip(info_own, YDIM)[0]], axis=0)
-    order = jnp.arange(PLANE // 2, dtype=jnp.int32)
+    order = jnp.asarray([0, 2, 1, 3], jnp.int32)
     quarters = jnp.stack([quarter ^ order, quarter ^ 1 ^ order], axis=0)
     positions = (
         quarters[:, :, None] * tok_rows + jnp.arange(tok_rows, dtype=jnp.int32)
@@ -518,30 +644,40 @@
     own_width = ws_out.shape[0]
     heads_here = own_width // HEAD_DIM
 
-    def split(mat):
-        return mat.reshape(2, -1, heads_here, HEAD_DIM)
+    def project(rows, mat):
+        parts = [low(matmul_nt(part, mat)).reshape(2, -1, heads_here, HEAD_DIM) for part in rows]
+        return jnp.concatenate(parts, axis=1)
 
     def merge(mat):
-        return low(mat.reshape(-1, own_width))
-
-    def project(rows, mat):
-        return low(matmul_nt(rows, mat))
-
-    sq, sk, sv = (split(project(rows_one, mat)) for mat in (ws_q, ws_k, ws_v))
+        count = mat.shape[1] // 2
+        return tuple(
+            low(part.reshape(-1, own_width)) for part in (mat[:, :count], mat[:, count:])
+        )
+
+    def spread_out(terms):
+        parts = [sum(matmul_nn(mat[part], weight) for mat, weight in terms) for part in (0, 1)]
+        return plane_scatter(*parts)
+
+    def weight_sum(mats, rows):
+        return narrow_total(matmul_tn(mats[0], rows[0]) + matmul_tn(mats[1], rows[1]))
+
+    sq, sk, sv = (project(rows_one, mat) for mat in (ws_q, ws_k, ws_v))
     self_result, self_lse = group_attend(sq, sk, sv, self_ok)
     self_heads = merge(self_result)
-    x1 = x + plane_scatter(matmul_nn(self_heads, ws_out))
+    self_heads, cotangent_here = lax.optimization_barrier((self_heads, cotangent_here))
+    x1 = x + spread_out([(self_heads, ws_out)])
     h2 = low(normed(x1, gain[1]))
     rows_two = plane_gather(h2)
-    ck, cv = (split(project(memory_all, mat)) for mat in (wc_k, wc_v))
-    cq = split(project(rows_two, wc_q))
+    ck, cv = (project(memory_all, mat) for mat in (wc_k, wc_v))
+    cq = project(rows_two, wc_q)
     cross_result, cross_lse = group_attend(cq, ck, cv, cross_ok)
     cross_heads = merge(cross_result * valid_float[:, :, None, None])
-    x2 = x1 + plane_scatter(matmul_nn(cross_heads, wc_out))
+    x2 = x1 + spread_out([(cross_heads, wc_out)])
     h3 = low(normed(x2, gain[2]))
-    grad_y = spread(cotangent).astype(jnp.float32) * local_weight[:, None]
-    grad_mlp = row_gather(low(grad_y))
-    rows_three = row_gather(h3)
+    grad_y = cotangent_here.astype(jnp.float32) * local_weight[:, None]
+    grad_mlp = row_gather(after(low(grad_y), wm_gate))
+    rows_three = row_gather(after(h3, grad_mlp))
+    (wm_out,) = wide_full(after(w_mlp_out[None], rows_three))
     gate = matmul_nt(rows_three, wm_gate)
     up = matmul_nt(rows_three, wm_up)
     hidden = low(jax.nn.gelu(gate, approximate=True) * up)
@@ -552,23 +688,22 @@
     grad_gate, grad_up = gelu_pull(grad_hidden)
     grad_gate, grad_up = low(grad_gate), low(grad_up)
     grad_h3 = branch_sum(matmul_nn(grad_gate, wm_gate) + matmul_nn(grad_up, wm_up))
-    output = unspread(low(x2 + branch_sum(matmul_nn(hidden, wm_out))))
+    mlp_terms = ((grad_gate, rows_three), (grad_up, rows_three), (hidden, grad_mlp))
+    mlp_packed = jnp.stack(
+        [
+            low(matmul_tn(mat, rows)).reshape(PLANE, -1, width)
+            for mat, rows in mlp_terms
+        ],
+        axis=1,
+    ).reshape(-1, width)
+    mlp_packed, grad_h3 = lax.optimization_barrier((mlp_packed, grad_h3))
+    mlp_sums = lax.psum_scatter(mlp_packed, "wide", scatter_dimension=0, tiled=True)
+    mlp_sums = mlp_sums.reshape(3, -1, width)
     _, norm_pull3 = jax.vjp(normed, x2, gain[2])
     part_x2, grad_gain3 = norm_pull3(grad_h3)
     grad_x2 = grad_y + part_x2
     grad_cross = plane_gather(low(grad_x2))
-    mlp_totals = placed(
-        [
-            low(plane_scatter(matmul_tn(term, rows)))
-            for term, rows in (
-                (grad_gate, rows_three),
-                (grad_up, rows_three),
-                (hidden, grad_mlp),
-            )
-        ],
-        spot_zero,
-    )
-    grad_cross_heads = split(project(grad_cross, wc_out))
+    grad_cross_heads = project(grad_cross, wc_out)
     grad_cross_heads = jnp.where(
         token_valid[:, :, None, None], grad_cross_heads, jnp.zeros_like(grad_cross_heads)
     )
@@ -576,49 +711,60 @@
         merge(mat)
         for mat in group_attend_back(cq, ck, cv, cross_ok, cross_lse, grad_cross_heads)
     )
-    grad_h2 = plane_scatter(matmul_nn(grad_cq, wc_q))
+    grad_h2 = spread_out([(grad_cq, wc_q)])
     _, norm_pull2 = jax.vjp(normed, x1, gain[1])
     part_x1, grad_gain2 = norm_pull2(grad_h2)
     grad_x1 = grad_x2 + part_x1
     grad_self = plane_gather(low(grad_x1))
-    mid_totals = placed(
-        [
-            narrow_total(matmul_tn(cross_heads, grad_cross)),
-            narrow_total(matmul_tn(grad_cv, memory_all)),
-            narrow_total(matmul_tn(grad_ck, memory_all)),
-            narrow_total(matmul_tn(grad_cq, rows_two)),
-            narrow_total(matmul_tn(self_heads, grad_self)),
-        ],
-        spot_zero,
-    )
-    grad_memory = unspread(
-        low(plane_scatter(matmul_nn(grad_ck, wc_k) + matmul_nn(grad_cv, wc_v)))
-    )
-    grad_self_heads = split(project(grad_self, ws_out))
+    mlp_here = spread(mlp_sums)
+    grad_self, mlp_here = lax.optimization_barrier((grad_self, mlp_here))
+    mlp_totals = laid(mlp_here, ((0, 1), (2,)))
+    memory_sums = low(
+        spread_out([(after(grad_ck, grad_self[0]), wc_k), (after(grad_cv, grad_self[0]), wc_v)])
+    )
+    mid_here = spread(
+        jnp.stack(
+            [
+                weight_sum(cross_heads, grad_cross),
+                weight_sum(grad_cv, memory_all),
+                weight_sum(grad_ck, memory_all),
+                weight_sum(grad_cq, rows_two),
+            ]
+        )
+    )
+    self_out_sum = weight_sum(self_heads, grad_self)
+    grad_self_heads = project(grad_self, ws_out)
     gsq, gsk, gsv = (
         merge(mat) for mat in group_attend_back(sq, sk, sv, self_ok, self_lse, grad_self_heads)
     )
-    in_totals = placed(
-        [narrow_total(matmul_tn(term, rows_one)) for term in (gsq, gsk, gsv)], spot_zero
-    )
-    grad_h1 = plane_scatter(matmul_nn(gsq, ws_q) + matmul_nn(gsk, ws_k) + matmul_nn(gsv, ws_v))
+    gsq, gsk, gsv, mid_here, memory_sums = lax.optimization_barrier(
+        (gsq, gsk, gsv, mid_here, memory_sums)
+    )
+    grad_memory = unspread(memory_sums)
+    in_sums = [weight_sum(term, rows_one) for term in (gsv, gsk, gsq)]
+    branch_three = branch_sum(after(matmul_nn(hidden, wm_out), gsq))
+    output = unspread(low(x2 + branch_three))
+    mid_totals = placed(core_pieces(chip_pieces(mid_here)), spot_zero, ((3,), (2, 1), (0,)))
+    last = jnp.stack([in_sums[2], in_sums[1], in_sums[0], self_out_sum])
+    in_totals, out_totals = laid(spread(last), ((0, 1, 2), (3,)))
+    grad_h1 = spread_out([(gsq, ws_q), (gsk, ws_k), (gsv, ws_v)])
     _, norm_pull1 = jax.vjp(normed, x, gain[0])
     part_x, grad_gain1 = norm_pull1(grad_h1)
     grad_tokens = unspread(low(grad_x1 + part_x))
-    gain_terms = lax.psum(jnp.stack([grad_gain1, grad_gain2, grad_gain3]), ("wide", "narrow"))
+    gain_terms = jnp.stack([grad_gain1, grad_gain2, grad_gain3])
+    levels = jnp.sum(lax.all_gather(gain_terms, "narrow", axis=0, tiled=False), axis=0)
     own_gains = width // lax.axis_size("narrow")
+    gain_own = lax.dynamic_slice_in_dim(levels, level * own_gains, own_gains, 1)
+    gain_total = jnp.sum(lax.all_gather(gain_own, "wide", axis=0, tiled=False), axis=0)
     return (
         output,
         grad_tokens,
         grad_memory,
-        lax.dynamic_slice_in_dim(gain_terms, level * own_gains, own_gains, 1),
-        jnp.stack(in_totals, axis=1),
-        mid_totals[4],
-        mid_totals[3],
-        jnp.stack([mid_totals[2], mid_totals[1]], axis=1),
-        mid_totals[0],
-        jnp.stack([mlp_totals[0], mlp_totals[1]], axis=1),
-        mlp_totals[2],
+        gain_total,
+        in_totals.swapaxes(0, 1),
+        out_totals,
+        *mid_totals,
+        *mlp_totals,
     )
 
 

time: 1300 us -> 1460 us (1.12)
  waiting for transfers between devices: 374 us -> 755 us
  local copies, waits for them, and re-layouts: 318 us -> 149 us
  other arithmetic: 105 us -> 52.2 us
  Pallas kernels: 0 us -> 39.1 us
  blocking collectives: 62.5 us -> 24.2 us
  matrix products: 179 us -> 201 us
  starting transfers between devices: 224 us -> 205 us
    all_gather x4 -> x8, waiting for transfers between devices: 0.03 us -> 172 us  [the longest x4 136 us: narrow_full(): lax.all_gather(stacked.reshape(kinds * rows, width), 'narrow', axis=0, ti...]
    unnamed x498 -> x264, local copies, waits for them, and re-layouts: 214 us -> 58.1 us
    reduce_scatter x8, waiting for transfers between devices: 10.6 us -> 106 us  [narrow_total(): lax.psum_scatter(low(term), 'narrow', scatter_dimension=0, tiled=True)]
    ppermute x122 -> x60, starting transfers between devices: 162 us -> 99.2 us  [flip(): return lax.ppermute(value, 'wide', [(i, i ^ bit) for i in range(PLANE)])]
    psum x1 -> x0, blocking collectives: 62.5 us -> none  [per_device(): lax.psum(jnp.stack([grad_gain1, grad_gain2, grad_gain3]), ('wide', 'narro...]
    all_gather x2, waiting for transfers between devices: 25.8 us -> 77.6 us  [row_gather(): return lax.all_gather(local_rows, 'narrow', axis=0, tiled=True)]
    pallas_call x0 -> x3, Pallas kernels: none -> 39.1 us  [the longest x2 23.1 us: laid(): pl.pallas_call(lambda *refs: laid_body(*refs, plan=plan), grid_spec=pltpu...]
    ppermute x3, waiting for transfers between devices: 0.01 us -> 38.7 us  [unspread(): return lax.ppermute(piece, axes, [(b, a) for a, b in first])]
  transfers between devices with their start and end apart: 158 -> 101, of which waited for: 52 -> 48; matrix products, arithmetic and copies ran while one was open for 40% -> 24% of each run, Pallas kernels for 0% -> 2%
where the time goes in v2:
time: 1460 us; the launch traced here: 1440 us
  waiting for transfers between devices  755 us (52%)
  starting transfers between devices  205 us (14%)
  matrix products  201 us (14%)
  local copies, waits for them, and re-layouts  149 us (10%)
  other arithmetic  52.2 us (4%)
  Pallas kernels  39.1 us (3%)
  blocking collectives  24.2 us (2%)
  between operations  16.9 us (1%)
    ppermute x60, waiting for transfers between devices, flip(): return lax.ppermute(value, 'wide', [(i, i ^ bit) for i in range(PLANE)])  239 us
    all_gather x4, waiting for transfers between devices, narrow_full(): lax.all_gather(stacked.reshape(kinds * rows, width), 'narrow', axis=0, ti...  136 us
    reduce_scatter x8, waiting for transfers between devices, narrow_total(): lax.psum_scatter(low(term), 'narrow', scatter_dimension=0, tiled=True)  106 us
    ppermute x60, starting transfers between devices, flip(): return lax.ppermute(value, 'wide', [(i, i ^ bit) for i in range(PLANE)])  99.2 us
    all_gather x2, waiting for transfers between devices, row_gather(): return lax.all_gather(local_rows, 'narrow', axis=0, tiled=True)  77.6 us
    dot_general x19, matrix products, matmul_nt(): lax.dot_general(a, b, (((1,), (1,)), ((), ())), preferred_element_type=jn...  68.2 us
    dot_general x19, matrix products, matmul_tn(): lax.dot_general(a, b, (((0,), (0,)), ((), ())), preferred_element_type=jn...  59.8 us
    unnamed x264, local copies, waits for them, and re-layouts  58.1 us
  transfers between devices with their start and end apart: 101, of which 48 were waited for; matrix products, arithmetic and copies ran while one was open for 24% of the time, Pallas kernels for 2%

profile of v2, /device:TPU:25, one launch (start us, length us, event | category | flops | bytes accessed | tf_op | source)
XLA Modules:
  0.0 1443.0 jit_solution(8860746804224598102)
XLA Ops:
  11.9 11.1 collective-permute-done
  53.2 48.7 %all-gather.15.cloned.1.call-done = bf16[4,192,2048]{2,1,0:T(8,128)(2,1)} async-done(((bf16[1,192,2048]{2,1,0:T(8,128)(2,1)}), bf16[4,192,2048]{2,1,0:T(8,128)(2,1)}) %all-gather.15.cloned.1.call-update) | async-done | bytes 3145744 | tf_op jit(solution)/shard_map/all_gather | solution.py:439
  134.7 30.1 %all-gather.17.cloned.1.call-done = bf16[4,128,2048]{2,1,0:T(8,128)(2,1)} async-done(((bf16[1,128,2048]{2,1,0:T(8,128)(2,1)}), bf16[4,128,2048]{2,1,0:T(8,128)(2,1)}) %all-gather.17.cloned.1.call-update) | async-done | bytes 2097168 | tf_op jit(solution)/shard_map/all_gather | solution.py:439
  189.2 31.7 %all-gather.19.cloned.1.call-done = bf16[4,128,2048]{2,1,0:T(8,128)(2,1)} async-done(((bf16[1,128,2048]{2,1,0:T(8,128)(2,1)}), bf16[4,128,2048]{2,1,0:T(8,128)(2,1)}) %all-gather.19.cloned.1.call-update) | async-done | bytes 2097168 | tf_op jit(solution)/shard_map/all_gather | solution.py:439
  230.0 25.3 %all-gather.21.cloned.1.call-done = bf16[4,64,2048]{2,1,0:T(8,128)(2,1)} async-done(((bf16[1,64,2048]{2,1,0:T(8,128)(2,1)}), bf16[4,64,2048]{2,1,0:T(8,128)(2,1)}) %all-gather.21.cloned.1.call-update) | async-done | bytes 1048592 | tf_op jit(solution)/shard_map/all_gather | solution.py:439
  263.7 30.5 %collective-permute-done.20 = bf16[256,2048]{1,0:T(8,128)(2,1)S(1)} collective-permute-done((bf16[256,2048]{1,0:T(8,128)(2,1)}, bf16[256,2048]{1,0:T(8,128)(2,1)S(1)}, u32[]{:S(2)}, u32[]{:S(2)}) %collective-permute-start.20) | collective-permute-done | bytes 1048608 | tf_op jit(solution)/shard_map/ppermute | solution.py:334
  312.3 11.3 collective-permute-start.23
  462.8 31.1 %all-gather.25.cloned.1.call-done = bf16[512,2048]{1,0:T(8,128)(2,1)} async-done(((bf16[128,2048]{1,0:T(8,128)(2,1)}), bf16[512,2048]{1,0:T(8,128)(2,1)}) %all-gather.25.cloned.1.call-update) | async-done | bytes 2097168 | tf_op jit(solution)/shard_map/all_gather | solution.py:147
  493.9 46.6 %all-gather.27.cloned.1.call-done = bf16[512,2048]{1,0:T(8,128)(2,1)} async-done(((bf16[128,2048]{1,0:T(8,128)(2,1)}), bf16[512,2048]{1,0:T(8,128)(2,1)}) %all-gather.27.cloned.1.call-update) | async-done | bytes 2097168 | tf_op jit(solution)/shard_map/all_gather | solution.py:147
  548.1 36.3 %all-gather.29.cloned.1.call-done = bf16[8,160,2048]{2,1,0:T(8,128)(2,1)} async-done(((bf16[1,160,2048]{2,1,0:T(8,128)(2,1)}), bf16[8,160,2048]{2,1,0:T(8,128)(2,1)}) %all-gather.29.cloned.1.call-update) | async-done | bytes 5242896 | tf_op jit(solution)/shard_map/all_gather | solution.py:581
  624.5 23.8 %reduce-scatter.12.cloned.1.call-done = bf16[128,2048]{1,0:T(8,128)(2,1)} async-done(((bf16[512,2048]{1,0:T(8,128)(2,1)}), bf16[128,2048]{1,0:T(8,128)(2,1)}) %reduce-scatter.12.cloned.1.call-update) | async-done | bytes 524304 | tf_op jit(solution)/shard_map/reduce_scatter | solution.py:151
  657.0 11.0 collective-permute-done.35
  761.6 10.9 collective-permute-done.40
  803.6 12.7 collective-permute-done.45
  818.1 25.8 %collective-permute-done.44 = bf16[128,2048]{1,0:T(8,128)(2,1)} collective-permute-done((bf16[128,2048]{1,0:T(8,128)(2,1)}, bf16[128,2048]{1,0:T(8,128)(2,1)}, u32[]{:S(2)}, u32[]{:S(2)}) %collective-permute-start.44) | collective-permute-done | bytes 524320 | tf_op jit(solution)/shard_map/ppermute | solution.py:334
  859.5 40.7 %reduce-scatter.20.cloned.1.call-done = bf16[64,2048]{1,0:T(8,128)(2,1)} async-done(((bf16[256,2048]{1,0:T(8,128)(2,1)}), bf16[64,2048]{1,0:T(8,128)(2,1)}) %reduce-scatter.20.cloned.1.call-update) | async-done | bytes 262160 | tf_op jit(solution)/shard_map/reduce_scatter | solution.py:445
  901.5 23.8 %collective-permute-start.51 = (bf16[4,64,2048]{2,1,0:T(8,128)(2,1)S(1)}, bf16[4,64,2048]{2,1,0:T(8,128)(2,1)}, u32[]{:S(2)}, u32[]{:S(2)}) collective-permute-start(bf16[4,64,2048]{2,1,0:T(8,128)(2,1)S(1)} %pad_maximum_fusion.3), channel_id=1, source_target_pairs={{0,0},{1,5},{2,10},{3,15},{4,20},{5,17},{6,30},{7,27},{8,8},{9,13}... | collective-permute-start | bytes 3145736 | tf_op jit(solution)/shard_map/ppermute | solution.py:100
  930.5 18.4 %collective-permute-done.51 = bf16[4,64,2048]{2,1,0:T(8,128)(2,1)} collective-permute-done((bf16[4,64,2048]{2,1,0:T(8,128)(2,1)S(1)}, bf16[4,64,2048]{2,1,0:T(8,128)(2,1)}, u32[]{:S(2)}, u32[]{:S(2)}) %collective-permute-start.51) | collective-permute-done | bytes 1048608 | tf_op jit(solution)/shard_map/ppermute | solution.py:100
  992.5 11.9 collective-permute-done.56
  1062.0 28.6 %reduce-scatter.26.cloned.1.call-done = bf16[64,2048]{1,0:T(8,128)(2,1)} async-done(((bf16[256,2048]{1,0:T(8,128)(2,1)}), bf16[64,2048]{1,0:T(8,128)(2,1)}) %reduce-scatter.26.cloned.1.call-update) | async-done | bytes 262160 | tf_op jit(solution)/shard_map/reduce_scatter | solution.py:445
  1090.6 28.6 %reduce-scatter.30.cloned.1.call-done = bf16[64,2048]{1,0:T(8,128)(2,1)} async-done(((bf16[256,2048]{1,0:T(8,128)(2,1)}), bf16[64,2048]{1,0:T(8,128)(2,1)}) %reduce-scatter.30.cloned.1.call-update) | async-done | bytes 262160 | tf_op jit(solution)/shard_map/reduce_scatter | solution.py:445
  1125.4 22.3 %collective-permute-done.69 = bf16[4,64,2048]{2,1,0:T(8,128)(2,1)S(1)} collective-permute-done((bf16[4,64,2048]{2,1,0:T(8,128)(2,1)S(1)}, bf16[4,64,2048]{2,1,0:T(8,128)(2,1)S(1)}, u32[]{:S(2)}, u32[]{:S(2)}) %collective-permute-start.69) | collective-permute-done | bytes 1048608 | tf_op jit(solution)/shard_map/ppermute | solution.py:100
  1149.7 25.6 %collective-permute-done.70 = bf16[4,64,2048]{2,1,0:T(8,128)(2,1)S(1)} collective-permute-done((bf16[4,64,2048]{2,1,0:T(8,128)(2,1)S(1)}, bf16[4,64,2048]{2,1,0:T(8,128)(2,1)S(1)}, u32[]{:S(2)}, u32[]{:S(2)}) %collective-permute-start.70) | collective-permute-done | bytes 1048608 | tf_op jit(solution)/shard_map/ppermute | solution.py:102
  1182.2 12.4 collective-permute-start.71
  1209.5 21.1 %collective-permute-start.67 = (bf16[256,2048]{1,0:T(8,128)(2,1)S(1)}, bf16[256,2048]{1,0:T(8,128)(2,1)}, u32[]{:S(2)}, u32[]{:S(2)}) collective-permute-start(bf16[256,2048]{1,0:T(8,128)(2,1)S(1)} %copy-done.78), channel_id=1, source_target_pairs={{0,0},{4,5},{8,10},{12,15},{20,20},{16,17},{28,30},{24,27},{9,8},{... | collective-permute-start | bytes 3145736 | tf_op jit(solution)/shard_map/ppermute | solution.py:340
  1236.4 12.2 collective-permute-done.61
  1251.2 28.6 %collective-permute-done.64 = bf16[64,2048]{1,0:T(8,128)(2,1)S(1)} collective-permute-done((bf16[64,2048]{1,0:T(8,128)(2,1)S(1)}, bf16[64,2048]{1,0:T(8,128)(2,1)S(1)}, u32[]{:S(2)}, u32[]{:S(2)}) %collective-permute-start.64) | collective-permute-done | bytes 262176 | tf_op jit(solution)/shard_map/ppermute | solution.py:334
  1297.8 38.7 %collective-permute-done.68 = bf16[256,2048]{1,0:T(8,128)(2,1)} collective-permute-done((bf16[256,2048]{1,0:T(8,128)(2,1)}, bf16[256,2048]{1,0:T(8,128)(2,1)}, u32[]{:S(2)}, u32[]{:S(2)}) %collective-permute-start.68) | collective-permute-done | bytes 1048608 | tf_op jit(solution)/shard_map/ppermute | solution.py:341
  1356.9 16.1 %place.1 = (f32[512,2048]{1,0:T(8,128)}, f32[512,2,2048]{2,1,0:T(2,128)}, f32[512,2048]{1,0:T(8,128)}) custom-call(s32[8]{0:T(128)} %broadcast_xor_fusion.refs_0_, bf16[4,64,2048]{2,1,0:T(8,128)(2,1)} %collective-permute-done.52.refs_1_, bf16[4,64,2048]{2,1,0:T(8,128)(2,1)} %collective-permute-done.71.refs_2_, bf16[4,64,2048]{2,1,0:T(8,128)(2,1)} %copy-done.45, ...), custom_call_target="tpu_custom_call" | custom-call | tf_op jit(solution)/shard_map/place/pallas_call | solution.py:513
  1373.0 10.6 all-gather.2
  1383.7 13.6 all-gather.3
  1416.1 13.7 laid.3
  (691 shorter events, 672.4 us)
Async XLA Ops:
  7.2 94.7 %all-gather.15.cloned.1.call-start = ((), (), s32[]{:S(2)}) async-start(), calls=%async_computation.11 | async-start | bytes 3932160 | tf_op jit(solution)/shard_map/all_gather | solution.py:439
  32.9 131.9 %all-gather.17.cloned.1.call-start = ((), (), s32[]{:S(2)}) async-start(), calls=%async_computation.12 | async-start | bytes 2621440 | tf_op jit(solution)/shard_map/all_gather | solution.py:439
  33.8 78.2 %collective-permute-start.7 = (s32[1,8]{1,0:T(1,128)S(1)}, s32[1,8]{1,0:T(1,128)S(1)}, u32[]{:S(2)}, u32[]{:S(2)}) collective-permute-start(s32[1,8]{1,0:T(1,128)S(1)} %pad_add_fusion.2), channel_id=1, source_target_pairs={{0,0},{1,5},{2,10},{3,15},{4,20},{5,17},{6,30},{7,27},{8,8},{9,13}... | collective-permute-start | bytes 104 | tf_op jit(solution)/shard_map/ppermute | solution.py:100
  42.7 126.9 %collective-permute-start.10 = (bf16[128,2048]{1,0:T(8,128)(2,1)}, bf16[128,2048]{1,0:T(8,128)(2,1)}, u32[]{:S(2)}, u32[]{:S(2)}) collective-permute-start(bf16[128,2048]{1,0:T(8,128)(2,1)} %param.29), channel_id=1, source_target_pairs={{0,0},{1,5},{2,10},{3,15},{4,20},{5,17},{6,30},{7,27},{8,8},{9,13}... | collective-permute-start | bytes 1572872 | tf_op jit(solution)/shard_map/ppermute | solution.py:108
  44.7 88.1 %collective-permute-start.11 = (bf16[256,2048]{1,0:T(8,128)(2,1)}, bf16[256,2048]{1,0:T(8,128)(2,1)}, u32[]{:S(2)}, u32[]{:S(2)}) collective-permute-start(bf16[256,2048]{1,0:T(8,128)(2,1)} %param.18), channel_id=1, source_target_pairs={{0,0},{1,5},{2,10},{3,15},{4,20},{5,17},{6,30},{7,27},{8,8},{9,13}... | collective-permute-start | bytes 3145736 | tf_op jit(solution)/shard_map/ppermute | solution.py:108
  105.6 115.3 %all-gather.19.cloned.1.call-start = ((), (), s32[]{:S(2)}) async-start(), calls=%async_computation.13 | async-start | bytes 2621440 | tf_op jit(solution)/shard_map/all_gather | solution.py:439
  168.0 87.3 %all-gather.21.cloned.1.call-start = ((), (), s32[]{:S(2)}) async-start(), calls=%async_computation.14 | async-start | bytes 1310720 | tf_op jit(solution)/shard_map/all_gather | solution.py:439
  223.7 215.7 %all-gather.23.cloned.1.call-start = ((), (), s32[]{:S(2)}) async-start(), calls=%async_computation.15 | async-start | bytes 11796480 | tf_op jit(solution)/shard_map/all_gather | solution.py:581
  255.3 238.5 %all-gather.25.cloned.1.call-start = ((), (), s32[]{:S(2)}) async-start(), calls=%async_computation.16 | async-start | bytes 2621440 | tf_op jit(solution)/shard_map/all_gather | solution.py:147
  312.3 78.8 %collective-permute-start.23 = (bf16[1024,2048]{1,0:T(8,128)(2,1)}, bf16[1024,2048]{1,0:T(8,128)(2,1)}, u32[]{:S(2)}, u32[]{:S(2)}) collective-permute-start(bf16[1024,2048]{1,0:T(8,128)(2,1)} %constant_dynamic-update-slice_fusion.5), channel_id=1, source_target_pairs={{0,4},{4,0},{8,12},{12,8},{16,20},{20,16},{24,28},{28,24},{1,5},{5... | collective-permute-start | bytes 12582920 | tf_op jit(solution)/shard_map/ppermute | solution.py:334
  449.8 90.6 %all-gather.27.cloned.1.call-start = ((), (), s32[]{:S(2)}) async-start(), calls=%async_computation.17 | async-start | bytes 2621440 | tf_op jit(solution)/shard_map/all_gather | solution.py:147
  493.8 90.5 %all-gather.29.cloned.1.call-start = ((), (), s32[]{:S(2)}) async-start(), calls=%async_computation.18 | async-start | bytes 5898240 | tf_op jit(solution)/shard_map/all_gather | solution.py:581
  540.5 107.8 %reduce-scatter.12.cloned.1.call-start = ((), (), s32[]{:S(2)}) async-start(), calls=%async_computation.19 | async-start | bytes 2621440 | tf_op jit(solution)/shard_map/reduce_scatter | solution.py:151
  606.4 177.2 %reduce-scatter.14.cloned.1.call-start = ((), (), s32[]{:S(2)}) async-start(), calls=%async_computation.20 | async-start | bytes 17694720 | tf_op jit(solution)/shard_map/reduce_scatter | solution.py:700
  650.5 209.0 %reduce-scatter.16.cloned.1.call-start = ((), (), s32[]{:S(2)}) async-start(), calls=%async_computation.21 | async-start | bytes 1310720 | tf_op jit(solution)/shard_map/reduce_scatter | solution.py:445
  712.0 147.5 %reduce-scatter.18.cloned.1.call-start = ((), (), s32[]{:S(2)}) async-start(), calls=%async_computation.22 | async-start | bytes 1310720 | tf_op jit(solution)/shard_map/reduce_scatter | solution.py:445
  738.3 121.2 %reduce-scatter.22.cloned.1.call-start = ((), (), s32[]{:S(2)}) async-start(), calls=%async_computation.24 | async-start | bytes 1310720 | tf_op jit(solution)/shard_map/reduce_scatter | solution.py:445
  761.5 138.6 %reduce-scatter.20.cloned.1.call-start = ((), (), s32[]{:S(2)}) async-start(), calls=%async_computation.23 | async-start | bytes 1310720 | tf_op jit(solution)/shard_map/reduce_scatter | solution.py:445
  783.6 70.0 %collective-permute-start.49 = (bf16[3,160,2048]{2,1,0:T(8,128)(2,1)}, bf16[3,160,2048]{2,1,0:T(8,128)(2,1)}, u32[]{:S(2)}, u32[]{:S(2)}) collective-permute-start(bf16[3,160,2048]{2,1,0:T(8,128)(2,1)} %bitcast.604), channel_id=1, source_target_pairs={{0,0},{1,5},{2,10},{3,15},{4,20},{5,17},{6,30},{7,27},{8,8},{9,13}... | collective-permute-start | bytes 5898248 | tf_op jit(solution)/shard_map/ppermute | solution.py:100
  803.6 250.1 %reduce-scatter.32.cloned.1.call-start = ((), (), s32[]{:S(2)}) async-start(), calls=%async_computation.29 | async-start | bytes 1310720 | tf_op jit(solution)/shard_map/reduce_scatter | solution.py:445
  853.6 71.7 %collective-permute-start.48 = (bf16[512,2048]{1,0:T(8,128)(2,1)}, bf16[512,2048]{1,0:T(8,128)(2,1)}, u32[]{:S(2)}, u32[]{:S(2)}) collective-permute-start(bf16[512,2048]{1,0:T(8,128)(2,1)} %constant_dynamic-update-slice_fusion.20), channel_id=1, source_target_pairs={{0,4},{4,0},{8,12},{12,8},{16,20},{20,16},{24,28},{28,24},{1,5},{5... | collective-permute-start | bytes 6291464 | tf_op jit(solution)/shard_map/ppermute | solution.py:334
  853.6 71.7 %collective-permute-start.50 = (bf16[3,160,2048]{2,1,0:T(8,128)(2,1)}, bf16[3,160,2048]{2,1,0:T(8,128)(2,1)}, u32[]{:S(2)}, u32[]{:S(2)}) collective-permute-start(bf16[3,160,2048]{2,1,0:T(8,128)(2,1)} %collective-permute-done.49), channel_id=1, source_target_pairs={{0,0},{5,4},{10,8},{15,12},{20,20},{17,16},{30,28},{27,24},{8,9},{... | collective-permute-start | bytes 5898248 | tf_op jit(solution)/shard_map/ppermute | solution.py:102
  948.9 84.6 %collective-permute-start.52 = (bf16[4,64,2048]{2,1,0:T(8,128)(2,1)}, bf16[4,64,2048]{2,1,0:T(8,128)(2,1)}, u32[]{:S(2)}, u32[]{:S(2)}) collective-permute-start(bf16[4,64,2048]{2,1,0:T(8,128)(2,1)} %collective-permute-done.51), channel_id=1, source_target_pairs={{0,0},{5,4},{10,8},{15,12},{20,20},{17,16},{30,28},{27,24},{8,9},{... | collective-permute-start | bytes 3145736 | tf_op jit(solution)/shard_map/ppermute | solution.py:102
  961.7 100.4 %reduce-scatter.28.cloned.1.call-start = ((), (), s32[]{:S(2)}) async-start(), calls=%async_computation.27 | async-start | bytes 1310720 | tf_op jit(solution)/shard_map/reduce_scatter | solution.py:445
  1041.9 77.2 %reduce-scatter.30.cloned.1.call-start = ((), (), s32[]{:S(2)}) async-start(), calls=%async_computation.28 | async-start | bytes 1310720 | tf_op jit(solution)/shard_map/reduce_scatter | solution.py:445
  1046.4 247.2 %reduce-scatter.24.cloned.1.call-start = ((), (), s32[]{:S(2)}) async-start(), calls=%async_computation.25 | async-start | bytes 2621440 | tf_op jit(solution)/shard_map/reduce_scatter | solution.py:151
  1053.6 344.3 %all-gather.31.cloned.1.call-start = ((), (), s32[]{:S(2)}) async-start(), calls=%async_computation.30 | async-start | bytes 9437184 | tf_op jit(solution)/shard_map/all_gather | solution.py:545
  1176.2 234.4 %all-gather.33.cloned.1.call-start = ((), (), s32[]{:S(2)}) async-start(), calls=%async_computation.31 | async-start | bytes 17694720 | tf_op jit(solution)/shard_map/all_gather | solution.py:545
  1199.5 93.6 %collective-permute-start.75 = (bf16[4,64,2048]{2,1,0:T(8,128)(2,1)}, bf16[4,64,2048]{2,1,0:T(8,128)(2,1)S(1)}, u32[]{:S(2)}, u32[]{:S(2)}) collective-permute-start(bf16[4,64,2048]{2,1,0:T(8,128)(2,1)} %collective-permute-done.52.refs_1_), channel_id=1, source_target_pairs={{0,4},{4,0},{8,12},{12,8},{16,20},{20,16},{24,28},{28,24},{1,5},{5... | collective-permute-start | bytes 3145736 | tf_op jit(solution)/shard_map/ppermute | solution.py:334
  1209.5 70.6 %collective-permute-start.67 = (bf16[256,2048]{1,0:T(8,128)(2,1)S(1)}, bf16[256,2048]{1,0:T(8,128)(2,1)}, u32[]{:S(2)}, u32[]{:S(2)}) collective-permute-start(bf16[256,2048]{1,0:T(8,128)(2,1)S(1)} %copy-done.78), channel_id=1, source_target_pairs={{0,0},{4,5},{8,10},{12,15},{20,20},{16,17},{28,30},{24,27},{9,8},{... | collective-permute-start | bytes 3145736 | tf_op jit(solution)/shard_map/ppermute | solution.py:340
  1280.1 76.0 %collective-permute-start.77 = (bf16[4,64,2048]{2,1,0:T(8,128)(2,1)S(1)}, bf16[4,64,2048]{2,1,0:T(8,128)(2,1)}, u32[]{:S(2)}, u32[]{:S(2)}) collective-permute-start(bf16[4,64,2048]{2,1,0:T(8,128)(2,1)S(1)} %collective-permute-done.72.refs_3_), channel_id=1, source_target_pairs={{0,4},{4,0},{8,12},{12,8},{16,20},{20,16},{24,28},{28,24},{1,5},{5... | collective-permute-start | bytes 3145736 | tf_op jit(solution)/shard_map/ppermute | solution.py:334
  1293.1 63.0 %collective-permute-start.76 = (bf16[4,64,2048]{2,1,0:T(8,128)(2,1)}, bf16[4,64,2048]{2,1,0:T(8,128)(2,1)}, u32[]{:S(2)}, u32[]{:S(2)}) collective-permute-start(bf16[4,64,2048]{2,1,0:T(8,128)(2,1)} %collective-permute-done.71.refs_2_), channel_id=1, source_target_pairs={{0,4},{4,0},{8,12},{12,8},{16,20},{20,16},{24,28},{28,24},{1,5},{5... | collective-permute-start | bytes 3145736 | tf_op jit(solution)/shard_map/ppermute | solution.py:334
  (179 other events, 3397.3 us)
Sparse Core Ops, SparseCore 0:
  33.0 68.7 all-gather.14
  105.7 59.0 all-gather.16
  168.1 52.7 all-gather.18
  223.8 31.4 all-gather.20
  257.6 99.8 all-gather.22
  449.9 43.8 all-gather.24
  496.0 44.4 all-gather.26
  542.3 41.9 all-gather.28
  606.5 41.7 reduce-scatter.11
  652.2 116.7 reduce-scatter.13
  771.3 25.3 reduce-scatter.15
  798.8 25.7 reduce-scatter.17
  826.9 25.7 reduce-scatter.21
  855.5 44.5 reduce-scatter.19
  961.8 30.6 reduce-scatter.31
  1037.9 24.0 reduce-scatter.27
  1064.7 25.7 reduce-scatter.25
  1093.3 25.7 reduce-scatter.29
  1122.0 48.5 reduce-scatter.23
  1176.3 102.7 all-gather.30
  1281.0 128.0 all-gather.32

commit v3 on v2

--- a/solution.py
+++ b/solution.py
@@ -95,22 +95,31 @@
 
 
 def spread(piece):
-    axes = ("wide", "narrow")
     first, second, _ = spread_tables(lax.axis_size("wide"), lax.axis_size("narrow"))
-    piece = lax.ppermute(piece, axes, first)
+    piece = hop(piece, first)
     if second is not None:
-        piece = lax.ppermute(piece, axes, second)
+        piece = hop(piece, second)
     return piece
 
 
+def hop(piece, pairs):
+    narrow = lax.axis_size("narrow")
+    stay = [0] * (lax.axis_size("wide") * narrow)
+    for source, target in pairs:
+        stay[source] = int(source == target)
+    here = lax.axis_index("wide") * narrow + lax.axis_index("narrow")
+    moved = lax.ppermute(
+        piece, ("wide", "narrow"), [pair for pair in pairs if pair[0] != pair[1]]
+    )
+    return jnp.where(jnp.asarray(stay, jnp.int32)[here] == 1, piece, moved)
+
+
 def plane_hop(piece):
-    first, _, _ = spread_tables(lax.axis_size("wide"), lax.axis_size("narrow"))
-    return lax.ppermute(piece, ("wide", "narrow"), first)
+    return hop(piece, spread_tables(lax.axis_size("wide"), lax.axis_size("narrow"))[0])
 
 
 def level_hop(piece):
-    _, second, _ = spread_tables(lax.axis_size("wide"), lax.axis_size("narrow"))
-    return lax.ppermute(piece, ("wide", "narrow"), second)
+    return hop(piece, spread_tables(lax.axis_size("wide"), lax.axis_size("narrow"))[1])
 
 
 def wide_gather(pieces):
@@ -335,10 +344,9 @@
 
 
 def unspread(piece):
-    axes = ("wide", "narrow")
     first, second, _ = spread_tables(lax.axis_size("wide"), lax.axis_size("narrow"))
-    piece = lax.ppermute(piece, axes, [(b, a) for a, b in second])
-    return lax.ppermute(piece, axes, [(b, a) for a, b in first])
+    piece = hop(piece, [(b, a) for a, b in second])
+    return hop(piece, [(b, a) for a, b in first])
 
 
 def after(value, *others):
@@ -446,6 +454,7 @@
 
 
 PIECE_FLIPS = (0, 2, 5, 7, 1, 3, 4, 6)
+WIDE_FLIPS = (0, 2, 4, 6, 1, 3, 5, 7)
 
 
 def place_body(spots, *refs, plan, source_count):
@@ -455,13 +464,13 @@
     def write(source):
         for out, kinds in zip(outs, plan):
             if len(kinds) == 1:
-                out[...] = source[kinds[0]].astype(jnp.float32)
+                out[...] = source[kinds[0]].astype(out.dtype)
             elif len(kinds) == 2:
                 for slot, kind in enumerate(kinds):
-                    out[:, slot, :] = source[kind].astype(jnp.float32)
+                    out[:, slot, :] = source[kind].astype(out.dtype)
             else:
                 for slot, kind in enumerate(kinds):
-                    out[slot] = source[kind].astype(jnp.float32)
+                    out[slot] = source[kind].astype(out.dtype)
 
     for number, source in enumerate(sources):
         which, spot = number // 5, number % 5
@@ -479,10 +488,10 @@
     return chip + [flip(piece, CORE) for piece in chip]
 
 
-def placed(sources, spot_zero, plan):
+def placed(sources, spot_zero, plan, flips=PIECE_FLIPS, kind=jnp.float32):
     kinds, rows, width = sources[0].shape
     half = rows // 2
-    spots = spot_zero ^ jnp.asarray(PIECE_FLIPS, jnp.int32)
+    spots = spot_zero ^ jnp.asarray(flips, jnp.int32)
 
     def source_spec(number):
         which, spot = number // 5, number % 5
@@ -508,7 +517,7 @@
             block, shape = (count, half, width), (count, PLANE * rows, width)
             index = lambda step, part, spots: (0, 2 * spots[step] + part, 0)
         out_specs.append(pl.BlockSpec(block, index))
-        out_shapes.append(jax.ShapeDtypeStruct(shape, jnp.float32))
+        out_shapes.append(jax.ShapeDtypeStruct(shape, kind))
     body = lambda *refs: place_body(*refs, plan=plan, source_count=len(sources))
     return pl.pallas_call(
         body,
@@ -524,63 +533,6 @@
         ),
         name="place",
     )(spots, *sources)
-
-
-def laid_body(spots, source, *outs, plan):
-    for out, kinds in zip(outs, plan):
-        if len(kinds) == 1:
-            out[...] = source[0, kinds[0]].astype(jnp.float32)
-        else:
-            for slot, kind in enumerate(kinds):
-                value = source[0, kind].astype(jnp.float32)
-                if len(kinds) == 2:
-                    out[:, slot, :] = value
-                else:
-                    out[slot] = value
-
-
-def laid(moved, plan):
-    kinds, rows, width = moved.shape
-    half = rows // 2
-    full = lax.all_gather(moved.reshape(kinds * rows, width), "wide", axis=0, tiled=False)
-    full = full.reshape(PLANE, kinds, rows, width)
-    _, _, spots = spread_tables(lax.axis_size("wide"), lax.axis_size("narrow"))
-    order = jnp.asarray(spots, jnp.int32)[lax.axis_index("narrow")]
-    out_specs, out_shapes = [], []
-    for group in plan:
-        count = len(group)
-        if count == 1:
-            block, shape = (half, width), (PLANE * rows, width)
-            index = lambda step, part, spots: (2 * step + part, 0)
-        elif count == 2:
-            block, shape = (half, 2, width), (PLANE * rows, 2, width)
-            index = lambda step, part, spots: (2 * step + part, 0, 0)
-        else:
-            block, shape = (count, half, width), (count, PLANE * rows, width)
-            index = lambda step, part, spots: (0, 2 * step + part, 0)
-        out_specs.append(pl.BlockSpec(block, index))
-        out_shapes.append(jax.ShapeDtypeStruct(shape, jnp.float32))
-    source_spec = pl.BlockSpec(
-        (1, kinds, half, width), lambda step, part, spots: (spots[step], 0, part, 0)
-    )
-    return pl.pallas_call(
-        lambda *refs: laid_body(*refs, plan=plan),
-        grid_spec=pltpu.PrefetchScalarGridSpec(
-            num_scalar_prefetch=1, grid=(PLANE, 2), in_specs=[source_spec], out_specs=out_specs
-        ),
-        out_shape=out_shapes,
-        compiler_params=pltpu.CompilerParams(
-            dimension_semantics=("arbitrary", "arbitrary"), vmem_limit_bytes=32 * 1024 * 1024
-        ),
-        name="laid",
-    )(order, full)
-
-
-def wide_full(stacked):
-    kinds, rows, width = stacked.shape
-    full = lax.all_gather(stacked.reshape(kinds * rows, width), "wide", axis=0, tiled=False)
-    full = full.reshape(-1, kinds, rows, width)
-    return [full[:, kind].reshape(-1, width) for kind in range(kinds)]
 
 
 def per_device(
@@ -602,7 +554,10 @@
     mem_rows = memory.shape[0]
     item_count = item_len.shape[1]
     gain = norm_gains.astype(jnp.float32)
-    tokens_here = spread(tokens)
+    tokens_hop = plane_hop(tokens)
+    mlp_shard = jnp.concatenate([w_mlp_in.swapaxes(0, 1), w_mlp_out[None]], axis=0)
+    mlp_sides = side_pieces(after(mlp_shard, tokens_hop))
+    tokens_here = level_hop(tokens_hop)
     ws_q, ws_k, ws_v = narrow_full(after(w_self_in.swapaxes(0, 1), tokens_here))
     x = tokens_here.astype(jnp.float32)
     h1 = low(normed(x, gain[0]))
@@ -610,9 +565,10 @@
     ws_out, wc_q = narrow_full(after(jnp.stack([w_self_out, w_cross_q]), ws_q))
     wc_k, wc_v = narrow_full(after(w_cross_kv.swapaxes(0, 1), ws_out))
     (wc_out,) = narrow_full(after(w_cross_out[None], wc_k))
-    wm_gate, wm_up = wide_full(after(w_mlp_in.swapaxes(0, 1), wc_out))
+    mlp_chip = corner_pieces(
+        [mlp_sides[0], *lax.optimization_barrier((*mlp_sides[1:], rows_one[1]))[:2]]
+    )
     memory_here = level_hop(after(plane_hop(memory), tokens_here))
-    memory_all = plane_gather(after(memory_here, rows_one[0]))
     cotangent_here = level_hop(after(plane_hop(cotangent), memory_here))
 
     me, level = lax.axis_index("wide"), lax.axis_index("narrow")
@@ -664,20 +620,25 @@
     sq, sk, sv = (project(rows_one, mat) for mat in (ws_q, ws_k, ws_v))
     self_result, self_lse = group_attend(sq, sk, sv, self_ok)
     self_heads = merge(self_result)
-    self_heads, cotangent_here = lax.optimization_barrier((self_heads, cotangent_here))
+    self_heads, mlp_chip = lax.optimization_barrier((self_heads, mlp_chip))
     x1 = x + spread_out([(self_heads, ws_out)])
     h2 = low(normed(x1, gain[1]))
+    h2, cotangent_here, memory_here = lax.optimization_barrier((h2, cotangent_here, memory_here))
+    memory_all = plane_gather(memory_here)
     rows_two = plane_gather(h2)
     ck, cv = (project(memory_all, mat) for mat in (wc_k, wc_v))
     cq = project(rows_two, wc_q)
     cross_result, cross_lse = group_attend(cq, ck, cv, cross_ok)
     cross_heads = merge(cross_result * valid_float[:, :, None, None])
+    grad_y = cotangent_here.astype(jnp.float32) * local_weight[:, None]
+    grad_mlp = row_gather(after(low(grad_y), wc_out))
+    cross_heads, grad_mlp = lax.optimization_barrier((cross_heads, grad_mlp))
     x2 = x1 + spread_out([(cross_heads, wc_out)])
     h3 = low(normed(x2, gain[2]))
-    grad_y = cotangent_here.astype(jnp.float32) * local_weight[:, None]
-    grad_mlp = row_gather(after(low(grad_y), wm_gate))
-    rows_three = row_gather(after(h3, grad_mlp))
-    (wm_out,) = wide_full(after(w_mlp_out[None], rows_three))
+    rows_three = row_gather(h3)
+    wm_gate, wm_up, wm_out = placed(
+        core_pieces(mlp_chip), me, ((0,), (1,), (2,)), WIDE_FLIPS, jnp.bfloat16
+    )
     gate = matmul_nt(rows_three, wm_gate)
     up = matmul_nt(rows_three, wm_up)
     hidden = low(jax.nn.gelu(gate, approximate=True) * up)
@@ -715,47 +676,68 @@
     _, norm_pull2 = jax.vjp(normed, x1, gain[1])
     part_x1, grad_gain2 = norm_pull2(grad_h2)
     grad_x1 = grad_x2 + part_x1
+    grad_x1, mlp_sums = lax.optimization_barrier((grad_x1, mlp_sums))
     grad_self = plane_gather(low(grad_x1))
+    memory_sides = scatter_start(
+        *(
+            matmul_nn(grad_ck[part], wc_k) + matmul_nn(grad_cv[part], wc_v)
+            for part in (0, 1)
+        )
+    )
     mlp_here = spread(mlp_sums)
-    grad_self, mlp_here = lax.optimization_barrier((grad_self, mlp_here))
-    mlp_totals = laid(mlp_here, ((0, 1), (2,)))
-    memory_sums = low(
-        spread_out([(after(grad_ck, grad_self[0]), wc_k), (after(grad_cv, grad_self[0]), wc_v)])
-    )
-    mid_here = spread(
-        jnp.stack(
-            [
-                weight_sum(cross_heads, grad_cross),
-                weight_sum(grad_cv, memory_all),
-                weight_sum(grad_ck, memory_all),
-                weight_sum(grad_cq, rows_two),
-            ]
-        )
+    mid_sums = jnp.stack(
+        [
+            weight_sum(cross_heads, grad_cross),
+            weight_sum(grad_cv, memory_all),
+            weight_sum(grad_ck, memory_all),
+            weight_sum(grad_cq, rows_two),
+        ]
     )
     self_out_sum = weight_sum(self_heads, grad_self)
     grad_self_heads = project(grad_self, ws_out)
+    grad_self_heads, memory_sides = lax.optimization_barrier((grad_self_heads, memory_sides))
+    memory_sums = low(scatter_end(*memory_sides))
     gsq, gsk, gsv = (
         merge(mat) for mat in group_attend_back(sq, sk, sv, self_ok, self_lse, grad_self_heads)
     )
-    gsq, gsk, gsv, mid_here, memory_sums = lax.optimization_barrier(
-        (gsq, gsk, gsv, mid_here, memory_sums)
+    gsq, gsk, gsv, mlp_here, memory_sums = lax.optimization_barrier(
+        (gsq, gsk, gsv, mlp_here, memory_sums)
     )
     grad_memory = unspread(memory_sums)
-    in_sums = [weight_sum(term, rows_one) for term in (gsv, gsk, gsq)]
-    branch_three = branch_sum(after(matmul_nn(hidden, wm_out), gsq))
-    output = unspread(low(x2 + branch_three))
-    mid_totals = placed(core_pieces(chip_pieces(mid_here)), spot_zero, ((3,), (2, 1), (0,)))
-    last = jnp.stack([in_sums[2], in_sums[1], in_sums[0], self_out_sum])
-    in_totals, out_totals = laid(spread(last), ((0, 1, 2), (3,)))
+
+    def weight_part(mats, rows):
+        return low(matmul_tn(mats[0], rows[0]) + matmul_tn(mats[1], rows[1]))
+
+    in_parts = [weight_part(term, rows_one) for term in (gsv, gsk, gsq)]
+    in_parts, mlp_here = lax.optimization_barrier((in_parts, mlp_here))
+    in_sums = [narrow_total(part) for part in in_parts]
+    mlp_pieces = core_pieces(chip_pieces(mlp_here))
     grad_h1 = spread_out([(gsq, ws_q), (gsk, ws_k), (gsv, ws_v)])
     _, norm_pull1 = jax.vjp(normed, x, gain[0])
     part_x, grad_gain1 = norm_pull1(grad_h1)
-    grad_tokens = unspread(low(grad_x1 + part_x))
+    grad_x = low(grad_x1 + part_x)
     gain_terms = jnp.stack([grad_gain1, grad_gain2, grad_gain3])
     levels = jnp.sum(lax.all_gather(gain_terms, "narrow", axis=0, tiled=False), axis=0)
     own_gains = width // lax.axis_size("narrow")
     gain_own = lax.dynamic_slice_in_dim(levels, level * own_gains, own_gains, 1)
     gain_total = jnp.sum(lax.all_gather(gain_own, "wide", axis=0, tiled=False), axis=0)
+    mid_sides = side_pieces(spread(after(mid_sums, grad_x, *mlp_pieces[1:3])))
+    last = jnp.stack([in_sums[2], in_sums[1], in_sums[0], self_out_sum])
+    last, mlp_pieces, mid_sides, grad_x, gain_total = lax.optimization_barrier(
+        (last, mlp_pieces, mid_sides, grad_x, gain_total)
+    )
+    grad_tokens = unspread(grad_x)
+    mid_pieces = core_pieces(corner_pieces(mid_sides))
+    mlp_totals = placed(mlp_pieces, spot_zero, ((0, 1), (2,)))
+    last_hop, mlp_totals = lax.optimization_barrier((plane_hop(last), mlp_totals))
+    last_sides = side_pieces(level_hop(last_hop))
+    last_sides, mid_pieces = lax.optimization_barrier((last_sides, mid_pieces))
+    mid_totals = placed(mid_pieces, spot_zero, ((3,), (2, 1), (0,)))
+    last_chip = corner_pieces(last_sides)
+    last_chip, mid_totals = lax.optimization_barrier((last_chip, mid_totals))
+    in_totals, out_totals = placed(core_pieces(last_chip), spot_zero, ((0, 1, 2), (3,)))
+    branch_three = branch_sum(after(matmul_nn(hidden, wm_out), in_parts[2]))
+    output = unspread(low(x2 + branch_three))
     return (
         output,
         grad_tokens,

time: 1460 us -> 1260 us (0.86)
  waiting for transfers between devices: 755 us -> 506 us
  Pallas kernels: 39.1 us -> 72 us
    ppermute x60 -> x87, waiting for transfers between devices: 239 us -> 350 us  [flip(): return lax.ppermute(value, 'wide', [(i, i ^ bit) for i in range(PLANE)])]
    all_gather x4, waiting for transfers between devices: 136 us -> 27 us  [narrow_full(): lax.all_gather(stacked.reshape(kinds * rows, width), 'narrow', axis=0, ti...]
    reduce_scatter x8, waiting for transfers between devices: 106 us -> 0.04 us  [narrow_total(): lax.psum_scatter(low(term), 'narrow', scatter_dimension=0, tiled=True)]
    all_gather x2, waiting for transfers between devices: 77.6 us -> 12.9 us  [row_gather(): return lax.all_gather(local_rows, 'narrow', axis=0, tiled=True)]
    pallas_call x1 -> x4, Pallas kernels: 16.1 us -> 72 us  [placed(): pl.pallas_call(body, grid_spec=pltpu.PrefetchScalarGridSpec(num_scalar_pr...]
    ppermute x60 -> x87, starting transfers between devices: 99.2 us -> 150 us  [flip(): return lax.ppermute(value, 'wide', [(i, i ^ bit) for i in range(PLANE)])]
    ppermute x20, starting transfers between devices: 103 us -> 57 us  [hop(): lax.ppermute(piece, ('wide', 'narrow'), [pair for pair in pairs if pair[0...]
    ppermute x20, waiting for transfers between devices: 136 us -> 93 us  [hop(): lax.ppermute(piece, ('wide', 'narrow'), [pair for pair in pairs if pair[0...]
  transfers between devices with their start and end apart: 101 -> 124, of which waited for: 48 -> 47; matrix products, arithmetic and copies ran while one was open for 24% -> 30% of each run, Pallas kernels for 2% -> 5%
where the time goes in v3:
time: 1260 us; the launch traced here: 1250 us
  waiting for transfers between devices  506 us (40%)
  starting transfers between devices  209 us (17%)
  matrix products  205 us (16%)
  local copies, waits for them, and re-layouts  148 us (12%)
  Pallas kernels  72 us (6%)
  other arithmetic  64.7 us (5%)
  blocking collectives  24.3 us (2%)
  between operations  18.2 us (1%)
    ppermute x87, waiting for transfers between devices, flip(): return lax.ppermute(value, 'wide', [(i, i ^ bit) for i in range(PLANE)])  350 us
    ppermute x87, starting transfers between devices, flip(): return lax.ppermute(value, 'wide', [(i, i ^ bit) for i in range(PLANE)])  150 us
    ppermute x20, waiting for transfers between devices, hop(): lax.ppermute(piece, ('wide', 'narrow'), [pair for pair in pairs if pair[0...  93 us
    pallas_call x4, Pallas kernels, placed(): pl.pallas_call(body, grid_spec=pltpu.PrefetchScalarGridSpec(num_scalar_pr...  72 us
    dot_general x19, matrix products, matmul_nt(): lax.dot_general(a, b, (((1,), (1,)), ((), ())), preferred_element_type=jn...  65.7 us
    dot_general x19, matrix products, matmul_tn(): lax.dot_general(a, b, (((0,), (0,)), ((), ())), preferred_element_type=jn...  61.3 us
    ppermute x20, starting transfers between devices, hop(): lax.ppermute(piece, ('wide', 'narrow'), [pair for pair in pairs if pair[0...  57 us
    unnamed x293, local copies, waits for them, and re-layouts  47 us
  transfers between devices with their start and end apart: 124, of which 47 were waited for; matrix products, arithmetic and copies ran while one was open for 30% of the time, Pallas kernels for 5%

profile of v3, /device:TPU:25, one launch (start us, length us, event | category | flops | bytes accessed | tf_op | source)
XLA Modules:
  0.0 1247.7 jit_solution(11910106318976564219)
XLA Ops:
  34.4 9.8 collective-permute-start.2
  60.4 10.1 collective-permute-done.4
  70.6 14.2 %collective-permute-done.5 = bf16[64,2048]{1,0:T(8,128)(2,1)S(1)} collective-permute-done((bf16[64,2048]{1,0:T(8,128)(2,1)S(1)}, bf16[64,2048]{1,0:T(8,128)(2,1)S(1)}, u32[]{:S(2)}, u32[]{:S(2)}) %collective-permute-start.5) | collective-permute-done | bytes 262176 | tf_op jit(solution)/shard_map/ppermute | solution.py:343
  93.9 35.4 %collective-permute-done.9 = s32[1,8]{1,0:T(1,128)S(1)} collective-permute-done((s32[1,8]{1,0:T(1,128)S(1)}, s32[1,8]{1,0:T(1,128)S(1)}, u32[]{:S(2)}, u32[]{:S(2)}) %collective-permute-start.9) | collective-permute-done | bytes 64 | tf_op jit(solution)/shard_map/ppermute | solution.py:343
  166.4 21.7 %all-gather.13.cloned.1.call-done = bf16[4,128,2048]{2,1,0:T(8,128)(2,1)} async-done(((bf16[1,128,2048]{2,1,0:T(8,128)(2,1)}), bf16[4,128,2048]{2,1,0:T(8,128)(2,1)}) %all-gather.13.cloned.1.call-update) | async-done | bytes 2097168 | tf_op jit(solution)/shard_map/all_gather | solution.py:447
  201.5 11.6 collective-permute-done.19
  216.1 12.2 collective-permute-start.15
  229.5 10.8 collective-permute-done.15
  256.1 18.1 %collective-permute-done.23 = bf16[256,2048]{1,0:T(8,128)(2,1)} collective-permute-done((bf16[256,2048]{1,0:T(8,128)(2,1)S(1)}, bf16[256,2048]{1,0:T(8,128)(2,1)}, u32[]{:S(2)}, u32[]{:S(2)}) %collective-permute-start.23) | collective-permute-done | bytes 1048608 | tf_op jit(solution)/shard_map/ppermute | solution.py:343
  282.9 14.2 %collective-permute-done.25 = bf16[128,2048]{1,0:T(8,128)(2,1)S(1)} collective-permute-done((bf16[128,2048]{1,0:T(8,128)(2,1)S(1)}, bf16[128,2048]{1,0:T(8,128)(2,1)S(1)}, u32[]{:S(2)}, u32[]{:S(2)}) %collective-permute-start.25) | collective-permute-done | bytes 524320 | tf_op jit(solution)/shard_map/ppermute | solution.py:343
  381.7 9.7 all-gather.19.cloned.1.call-done
  399.6 11.0 collective-permute-done.34
  437.1 18.6 %place.4 = (bf16[1280,2048]{1,0:T(8,128)(2,1)}, bf16[1280,2048]{1,0:T(8,128)(2,1)}, bf16[1280,2048]{1,0:T(8,128)(2,1)}) custom-call(s32[8]{0:T(128)} %broadcast_xor_fusion.1.refs_0_, bf16[3,160,2048]{2,1,0:T(8,128)(2,1)} %pad_maximum_fusion.1.refs_1_, bf16[3,160,2048]{2,1,0:T(8,128)(2,1)} %collective-permute-done.10.refs_2_, ...), custom_call_target="tpu_custom_call" | custom-call | tf_op jit(solution)/shard_map/place/pallas_call | solution.py:522
  505.4 23.2 %reduce-scatter.12.cloned.1.call-done = bf16[128,2048]{1,0:T(8,128)(2,1)} async-done(((bf16[512,2048]{1,0:T(8,128)(2,1)}), bf16[128,2048]{1,0:T(8,128)(2,1)}) %reduce-scatter.12.cloned.1.call-update) | async-done | bytes 524304 | tf_op jit(solution)/shard_map/reduce_scatter | solution.py:160
  535.9 11.0 collective-permute-done.44
  642.8 9.8 collective-permute-done.49
  686.7 29.0 %collective-permute-done.55 = bf16[64,2048]{1,0:T(8,128)(2,1)S(1)} collective-permute-done((bf16[64,2048]{1,0:T(8,128)(2,1)S(1)}, bf16[64,2048]{1,0:T(8,128)(2,1)S(1)}, u32[]{:S(2)}, u32[]{:S(2)}) %collective-permute-start.55) | collective-permute-done | bytes 262176 | tf_op jit(solution)/shard_map/ppermute | solution.py:343
  716.4 36.7 %collective-permute-done.56 = bf16[64,2048]{1,0:T(8,128)(2,1)S(1)} collective-permute-done((bf16[64,2048]{1,0:T(8,128)(2,1)S(1)}, bf16[64,2048]{1,0:T(8,128)(2,1)S(1)}, u32[]{:S(2)}, u32[]{:S(2)}) %collective-permute-start.56) | collective-permute-done | bytes 262176 | tf_op jit(solution)/shard_map/ppermute | solution.py:343
  850.0 34.0 %collective-permute-start.77 = (bf16[2,64,2048]{2,1,0:T(8,128)(2,1)}, bf16[2,64,2048]{2,1,0:T(8,128)(2,1)}, u32[]{:S(2)}, u32[]{:S(2)}) collective-permute-start(bf16[2,64,2048]{2,1,0:T(8,128)(2,1)} %slice_bitcast_fusion.8), channel_id=1, source_target_pairs={{0,8},{4,12},{8,0},{12,4},{16,24},{20,28},{24,16},{28,20},{1,9},{5... | collective-permute-start | bytes 1572872 | tf_op jit(solution)/shard_map/ppermute | solution.py:343
  899.6 44.6 %collective-permute-done.80 = bf16[64,2048]{1,0:T(8,128)(2,1)S(1)} collective-permute-done((bf16[64,2048]{1,0:T(8,128)(2,1)S(1)}, bf16[64,2048]{1,0:T(8,128)(2,1)S(1)}, u32[]{:S(2)}, u32[]{:S(2)}) %collective-permute-start.80) | collective-permute-done | bytes 262176 | tf_op jit(solution)/shard_map/ppermute | solution.py:343
  950.0 24.0 %collective-permute-done.81 = bf16[4,64,2048]{2,1,0:T(8,128)(2,1)S(1)} collective-permute-done((bf16[4,64,2048]{2,1,0:T(8,128)(2,1)S(1)}, bf16[4,64,2048]{2,1,0:T(8,128)(2,1)S(1)}, u32[]{:S(2)}, u32[]{:S(2)}) %collective-permute-start.81) | collective-permute-done | bytes 1048608 | tf_op jit(solution)/shard_map/ppermute | solution.py:111
  982.4 20.0 %collective-permute-done.70.refs_5_ = bf16[3,80,2048]{2,1,0:T(8,128)(2,1)} collective-permute-done((bf16[3,80,2048]{2,1,0:T(8,128)(2,1)}, bf16[3,80,2048]{2,1,0:T(8,128)(2,1)}, u32[]{:S(2)}, u32[]{:S(2)}) %collective-permute-start.70) | collective-permute-done | bytes 983072 | tf_op jit(solution)/shard_map/ppermute | solution.py:343
  1008.2 15.3 %collective-permute-start.83 = (bf16[4,64,2048]{2,1,0:T(8,128)(2,1)S(1)}, bf16[4,64,2048]{2,1,0:T(8,128)(2,1)}, u32[]{:S(2)}, u32[]{:S(2)}) collective-permute-start(bf16[4,64,2048]{2,1,0:T(8,128)(2,1)S(1)} %broadcast_select_fusion.5.refs_1_), channel_id=1, source_target_pairs={{0,8},{4,12},{8,0},{12,4},{16,24},{20,28},{24,16},{28,20},{1,9},{5... | collective-permute-start | bytes 3145736 | tf_op jit(solution)/shard_map/ppermute | solution.py:343
  1031.8 12.1 all-gather.2
  1044.0 12.1 all-gather.3
  1060.5 22.1 %place.5 = (f32[1280,2,2048]{2,1,0:T(2,128)}, f32[1280,2048]{1,0:T(8,128)}) custom-call(s32[8]{0:T(128)} %broadcast_xor_fusion.refs_0_, bf16[3,160,2048]{2,1,0:T(8,128)(2,1)} %broadcast_select_fusion.1.refs_1_, bf16[3,160,2048]{2,1,0:T(8,128)(2,1)} %collective-permute-done.67.refs_2_, bf16[3,160,2048]{2,1,0:T(8,128)(2,1)} %collective-permute-done.68.refs_3_, ...), custom_call_target="tpu_custom_call" | custom-call | tf_op jit(solution)/shard_map/place/pallas_call | solution.py:522
  1103.7 18.1 %collective-permute-done.87 = bf16[256,2048]{1,0:T(8,128)(2,1)S(1)} collective-permute-done((bf16[256,2048]{1,0:T(8,128)(2,1)S(1)}, bf16[256,2048]{1,0:T(8,128)(2,1)S(1)}, u32[]{:S(2)}, u32[]{:S(2)}) %collective-permute-start.87) | collective-permute-done | bytes 1048608 | tf_op jit(solution)/shard_map/ppermute | solution.py:111
  1124.1 15.0 %collective-permute-start.91 = (bf16[4,64,2048]{2,1,0:T(8,128)(2,1)S(1)}, bf16[4,64,2048]{2,1,0:T(8,128)(2,1)}, u32[]{:S(2)}, u32[]{:S(2)}) collective-permute-start(bf16[4,64,2048]{2,1,0:T(8,128)(2,1)S(1)} %broadcast_select_fusion.4.refs_1_), channel_id=1, source_target_pairs={{0,8},{4,12},{8,0},{12,4},{16,24},{20,28},{24,16},{28,20},{1,9},{5... | collective-permute-start | bytes 3145736 | tf_op jit(solution)/shard_map/ppermute | solution.py:343
  1148.0 14.4 %collective-permute-done.91.refs_2_ = bf16[4,64,2048]{2,1,0:T(8,128)(2,1)} collective-permute-done((bf16[4,64,2048]{2,1,0:T(8,128)(2,1)S(1)}, bf16[4,64,2048]{2,1,0:T(8,128)(2,1)}, u32[]{:S(2)}, u32[]{:S(2)}) %collective-permute-start.91) | collective-permute-done | bytes 1048608 | tf_op jit(solution)/shard_map/ppermute | solution.py:343
  1173.0 15.9 %place.6 = (f32[512,2048]{1,0:T(8,128)}, f32[512,2,2048]{2,1,0:T(2,128)}, f32[512,2048]{1,0:T(8,128)}) custom-call(s32[8]{0:T(128)} %broadcast_xor_fusion.refs_0_, bf16[4,64,2048]{2,1,0:T(8,128)(2,1)} %copy-done.30, bf16[4,64,2048]{2,1,0:T(8,128)(2,1)} %collective-permute-done.83.refs_2_, bf16[4,64,2048]{2,1,0:T(8,128)(2,1)} %collective-permute-done.84.refs_3_, ...), custom_call_target="tpu_custom_call" | custom-call | tf_op jit(solution)/shard_map/place/pallas_call | solution.py:522
  1208.5 10.4 collective-permute-done.86
  1225.5 15.4 %place.7 = (f32[3,512,2048]{2,1,0:T(8,128)}, f32[512,2048]{1,0:T(8,128)}) custom-call(s32[8]{0:T(128)} %broadcast_xor_fusion.refs_0_, bf16[4,64,2048]{2,1,0:T(8,128)(2,1)} %copy-done.31, bf16[4,64,2048]{2,1,0:T(8,128)(2,1)} %collective-permute-done.91.refs_2_, bf16[4,64,2048]{2,1,0:T(8,128)(2,1)} %collective-permute-done.92.refs_3_, ...), custom_call_target="tpu_custom_call" | custom-call | tf_op jit(solution)/shard_map/place/pallas_call | solution.py:522
  (794 shorter events, 649.0 us)
Async XLA Ops:
  7.2 130.5 %all-gather.11.cloned.1.call-start = ((), (), s32[]{:S(2)}) async-start(), calls=%async_computation.11 | async-start | bytes 3932160 | tf_op jit(solution)/shard_map/all_gather | solution.py:447
  33.3 154.8 %all-gather.13.cloned.1.call-start = ((), (), s32[]{:S(2)}) async-start(), calls=%async_computation.12 | async-start | bytes 2621440 | tf_op jit(solution)/shard_map/all_gather | solution.py:447
  47.0 145.1 %collective-permute-start.20 = (bf16[256,2048]{1,0:T(8,128)(2,1)}, bf16[256,2048]{1,0:T(8,128)(2,1)}, u32[]{:S(2)}, u32[]{:S(2)}) collective-permute-start(bf16[256,2048]{1,0:T(8,128)(2,1)} %param.39), channel_id=1, source_target_pairs={{1,5},{2,10},{3,15},{4,20},{5,17},{6,30},{7,27},{9,13},{10,2},{11,... | collective-permute-start | bytes 3145736 | tf_op jit(solution)/shard_map/ppermute | solution.py:111
  143.1 173.1 %all-gather.15.cloned.1.call-start = ((), (), s32[]{:S(2)}) async-start(), calls=%async_computation.13 | async-start | bytes 2621440 | tf_op jit(solution)/shard_map/all_gather | solution.py:447
  252.1 93.0 %all-gather.17.cloned.1.call-start = ((), (), s32[]{:S(2)}) async-start(), calls=%async_computation.14 | async-start | bytes 1310720 | tf_op jit(solution)/shard_map/all_gather | solution.py:447
  254.2 49.3 %collective-permute-start.29 = (bf16[128,2048]{1,0:T(8,128)(2,1)S(1)}, bf16[128,2048]{1,0:T(8,128)(2,1)}, u32[]{:S(2)}, u32[]{:S(2)}) collective-permute-start(bf16[128,2048]{1,0:T(8,128)(2,1)S(1)} %multiply_convert_fusion.5), channel_id=1, source_target_pairs={{0,16},{4,20},{8,24},{12,28},{16,0},{20,4},{24,8},{28,12},{1,17},{... | collective-permute-start | bytes 1572872 | tf_op jit(solution)/shard_map/ppermute | solution.py:343
  255.7 49.3 %collective-permute-start.28 = (bf16[128,2048]{1,0:T(8,128)(2,1)S(1)}, bf16[128,2048]{1,0:T(8,128)(2,1)}, u32[]{:S(2)}, u32[]{:S(2)}) collective-permute-start(bf16[128,2048]{1,0:T(8,128)(2,1)S(1)} %multiply_convert_fusion.5), channel_id=1, source_target_pairs={{0,8},{4,12},{8,0},{12,4},{16,24},{20,28},{24,16},{28,20},{1,9},{5... | collective-permute-start | bytes 1572872 | tf_op jit(solution)/shard_map/ppermute | solution.py:343
  298.8 51.4 %collective-permute-start.27 = (bf16[1024,2048]{1,0:T(8,128)(2,1)}, bf16[1024,2048]{1,0:T(8,128)(2,1)}, u32[]{:S(2)}, u32[]{:S(2)}) collective-permute-start(bf16[1024,2048]{1,0:T(8,128)(2,1)} %constant_dynamic-update-slice_fusion.5), channel_id=1, source_target_pairs={{0,4},{4,0},{8,12},{12,8},{16,20},{20,16},{24,28},{28,24},{1,5},{5... | collective-permute-start | bytes 12582920 | tf_op jit(solution)/shard_map/ppermute | solution.py:343
  318.0 73.5 %all-gather.19.cloned.1.call-start = ((), (), s32[]{:S(2)}) async-start(), calls=%async_computation.15 | async-start | bytes 2621440 | tf_op jit(solution)/shard_map/all_gather | solution.py:156
  345.1 121.3 %all-gather.21.cloned.1.call-start = ((), (), s32[]{:S(2)}) async-start(), calls=%async_computation.16 | async-start | bytes 2621440 | tf_op jit(solution)/shard_map/all_gather | solution.py:156
  419.7 108.9 %reduce-scatter.12.cloned.1.call-start = ((), (), s32[]{:S(2)}) async-start(), calls=%async_computation.17 | async-start | bytes 2621440 | tf_op jit(solution)/shard_map/reduce_scatter | solution.py:160
  485.6 184.4 %reduce-scatter.14.cloned.1.call-start = ((), (), s32[]{:S(2)}) async-start(), calls=%async_computation.18 | async-start | bytes 17694720 | tf_op jit(solution)/shard_map/reduce_scatter | solution.py:661
  530.7 353.3 %reduce-scatter.26.cloned.1.call-start = ((), (), s32[]{:S(2)}) async-start(), calls=%async_computation.24 | async-start | bytes 1310720 | tf_op jit(solution)/shard_map/reduce_scatter | solution.py:453
  591.1 293.0 %reduce-scatter.28.cloned.1.call-start = ((), (), s32[]{:S(2)}) async-start(), calls=%async_computation.25 | async-start | bytes 1310720 | tf_op jit(solution)/shard_map/reduce_scatter | solution.py:453
  619.4 264.7 %reduce-scatter.32.cloned.1.call-start = ((), (), s32[]{:S(2)}) async-start(), calls=%async_computation.27 | async-start | bytes 1310720 | tf_op jit(solution)/shard_map/reduce_scatter | solution.py:453
  639.7 244.4 %reduce-scatter.30.cloned.1.call-start = ((), (), s32[]{:S(2)}) async-start(), calls=%async_computation.26 | async-start | bytes 1310720 | tf_op jit(solution)/shard_map/reduce_scatter | solution.py:453
  673.8 90.8 %collective-permute-start.60 = (bf16[2,128,2048]{2,1,0:T(8,128)(2,1)S(1)}, bf16[2,128,2048]{2,1,0:T(8,128)(2,1)}, u32[]{:S(2)}, u32[]{:S(2)}) collective-permute-start(bf16[2,128,2048]{2,1,0:T(8,128)(2,1)S(1)} %slice_bitcast_fusion), channel_id=1, source_target_pairs={{0,16},{4,20},{8,24},{12,28},{16,0},{20,4},{24,8},{28,12},{1,17},{... | collective-permute-start | bytes 3145736 | tf_op jit(solution)/shard_map/ppermute | solution.py:343
  676.5 88.2 %collective-permute-start.59 = (bf16[2,128,2048]{2,1,0:T(8,128)(2,1)}, bf16[2,128,2048]{2,1,0:T(8,128)(2,1)}, u32[]{:S(2)}, u32[]{:S(2)}) collective-permute-start(bf16[2,128,2048]{2,1,0:T(8,128)(2,1)} %slice_bitcast_fusion.2), channel_id=1, source_target_pairs={{0,8},{4,12},{8,0},{12,4},{16,24},{20,28},{24,16},{28,20},{1,9},{5... | collective-permute-start | bytes 3145736 | tf_op jit(solution)/shard_map/ppermute | solution.py:343
  677.6 94.9 %collective-permute-start.61 = (bf16[3,160,2048]{2,1,0:T(8,128)(2,1)}, bf16[3,160,2048]{2,1,0:T(8,128)(2,1)}, u32[]{:S(2)}, u32[]{:S(2)}) collective-permute-start(bf16[3,160,2048]{2,1,0:T(8,128)(2,1)} %bitcast.64), channel_id=1, source_target_pairs={{1,5},{2,10},{3,15},{4,20},{5,17},{6,30},{7,27},{9,13},{10,2},{11,... | collective-permute-start | bytes 5898248 | tf_op jit(solution)/shard_map/ppermute | solution.py:111
  683.5 69.6 %collective-permute-start.56 = (bf16[64,2048]{1,0:T(8,128)(2,1)S(1)}, bf16[64,2048]{1,0:T(8,128)(2,1)S(1)}, u32[]{:S(2)}, u32[]{:S(2)}) collective-permute-start(bf16[64,2048]{1,0:T(8,128)(2,1)S(1)} %slice.452), channel_id=1, source_target_pairs={{0,8},{4,12},{8,0},{12,4},{16,24},{20,28},{24,16},{28,20},{1,9},{5... | collective-permute-start | bytes 786440 | tf_op jit(solution)/shard_map/ppermute | solution.py:343
  764.6 265.8 %reduce-scatter.24.cloned.1.call-start = ((), (), s32[]{:S(2)}) async-start(), calls=%async_computation.23 | async-start | bytes 1310720 | tf_op jit(solution)/shard_map/reduce_scatter | solution.py:453
  811.6 218.8 %reduce-scatter.20.cloned.1.call-start = ((), (), s32[]{:S(2)}) async-start(), calls=%async_computation.21 | async-start | bytes 1310720 | tf_op jit(solution)/shard_map/reduce_scatter | solution.py:453
  842.4 188.0 %reduce-scatter.22.cloned.1.call-start = ((), (), s32[]{:S(2)}) async-start(), calls=%async_computation.22 | async-start | bytes 1310720 | tf_op jit(solution)/shard_map/reduce_scatter | solution.py:453
  886.4 60.5 %collective-permute-start.68 = (bf16[3,160,2048]{2,1,0:T(8,128)(2,1)}, bf16[3,160,2048]{2,1,0:T(8,128)(2,1)}, u32[]{:S(2)}, u32[]{:S(2)}) collective-permute-start(bf16[3,160,2048]{2,1,0:T(8,128)(2,1)} %broadcast_select_fusion.1.refs_1_), channel_id=1, source_target_pairs={{0,16},{4,20},{8,24},{12,28},{16,0},{20,4},{24,8},{28,12},{1,17},{... | collective-permute-start | bytes 5898248 | tf_op jit(solution)/shard_map/ppermute | solution.py:343
  887.8 59.1 %collective-permute-start.67 = (bf16[3,160,2048]{2,1,0:T(8,128)(2,1)}, bf16[3,160,2048]{2,1,0:T(8,128)(2,1)}, u32[]{:S(2)}, u32[]{:S(2)}) collective-permute-start(bf16[3,160,2048]{2,1,0:T(8,128)(2,1)} %broadcast_select_fusion.1.refs_1_), channel_id=1, source_target_pairs={{0,8},{4,12},{8,0},{12,4},{16,24},{20,28},{24,16},{28,20},{1,9},{5... | collective-permute-start | bytes 5898248 | tf_op jit(solution)/shard_map/ppermute | solution.py:343
  887.8 142.6 %reduce-scatter.18.cloned.1.call-start = ((), (), s32[]{:S(2)}) async-start(), calls=%async_computation.20 | async-start | bytes 1310720 | tf_op jit(solution)/shard_map/reduce_scatter | solution.py:453
  949.6 55.6 %collective-permute-start.71 = (bf16[3,160,2048]{2,1,0:T(8,128)(2,1)}, bf16[3,160,2048]{2,1,0:T(8,128)(2,1)}, u32[]{:S(2)}, u32[]{:S(2)}) collective-permute-start(bf16[3,160,2048]{2,1,0:T(8,128)(2,1)} %broadcast_select_fusion.1.refs_1_), channel_id=1, source_target_pairs={{0,4},{4,0},{8,12},{12,8},{16,20},{20,16},{24,28},{28,24},{1,5},{5... | collective-permute-start | bytes 5898248 | tf_op jit(solution)/shard_map/ppermute | solution.py:343
  979.0 160.1 %reduce-scatter.16.cloned.1.call-start = ((), (), s32[]{:S(2)}) async-start(), calls=%async_computation.19 | async-start | bytes 2621440 | tf_op jit(solution)/shard_map/reduce_scatter | solution.py:160
  980.7 76.0 %collective-permute-start.73 = (bf16[3,160,2048]{2,1,0:T(8,128)(2,1)}, bf16[3,160,2048]{2,1,0:T(8,128)(2,1)}, u32[]{:S(2)}, u32[]{:S(2)}) collective-permute-start(bf16[3,160,2048]{2,1,0:T(8,128)(2,1)} %collective-permute-done.68.refs_3_), channel_id=1, source_target_pairs={{0,4},{4,0},{8,12},{12,8},{16,20},{20,16},{24,28},{28,24},{1,5},{5... | collective-permute-start | bytes 5898248 | tf_op jit(solution)/shard_map/ppermute | solution.py:343
  1002.4 54.4 %collective-permute-start.72 = (bf16[3,160,2048]{2,1,0:T(8,128)(2,1)}, bf16[3,160,2048]{2,1,0:T(8,128)(2,1)}, u32[]{:S(2)}, u32[]{:S(2)}) collective-permute-start(bf16[3,160,2048]{2,1,0:T(8,128)(2,1)} %collective-permute-done.67.refs_2_), channel_id=1, source_target_pairs={{0,4},{4,0},{8,12},{12,8},{16,20},{20,16},{24,28},{28,24},{1,5},{5... | collective-permute-start | bytes 5898248 | tf_op jit(solution)/shard_map/ppermute | solution.py:343
  1005.2 51.5 %collective-permute-start.84 = (bf16[4,64,2048]{2,1,0:T(8,128)(2,1)S(1)}, bf16[4,64,2048]{2,1,0:T(8,128)(2,1)}, u32[]{:S(2)}, u32[]{:S(2)}) collective-permute-start(bf16[4,64,2048]{2,1,0:T(8,128)(2,1)S(1)} %broadcast_select_fusion.5.refs_1_), channel_id=1, source_target_pairs={{0,16},{4,20},{8,24},{12,28},{16,0},{20,4},{24,8},{28,12},{1,17},{... | collective-permute-start | bytes 3145736 | tf_op jit(solution)/shard_map/ppermute | solution.py:343
  1142.7 55.7 %collective-permute-start.88 = (bf16[256,2048]{1,0:T(8,128)(2,1)S(1)}, bf16[256,2048]{1,0:T(8,128)(2,1)S(1)}, u32[]{:S(2)}, u32[]{:S(2)}) collective-permute-start(bf16[256,2048]{1,0:T(8,128)(2,1)S(1)} %broadcast_select_fusion.8), channel_id=1, source_target_pairs={{5,1},{10,2},{15,3},{20,4},{17,5},{30,6},{27,7},{13,9},{2,10},{7,1... | collective-permute-start | bytes 3145736 | tf_op jit(solution)/shard_map/ppermute | solution.py:111
  (219 other events, 4065.6 us)
Sparse Core Ops, SparseCore 0:
  33.5 68.7 all-gather.10
  143.2 44.8 all-gather.12
  252.2 47.4 all-gather.14
  318.1 26.9 all-gather.16
  346.5 44.9 all-gather.18
  419.8 46.5 all-gather.20
  485.8 42.7 reduce-scatter.11
  532.7 114.8 reduce-scatter.13
  649.9 25.3 reduce-scatter.25
  677.4 25.7 reduce-scatter.27
  705.6 25.7 reduce-scatter.31
  764.7 27.7 reduce-scatter.29
  811.8 29.4 reduce-scatter.23
  843.4 55.9 reduce-scatter.19
  902.1 25.7 reduce-scatter.21
  979.2 28.9 reduce-scatter.17
  1030.2 43.9 reduce-scatter.15

commit v4 on v3

--- a/solution.py
+++ b/solution.py
@@ -531,6 +531,11 @@
         compiler_params=pltpu.CompilerParams(
             dimension_semantics=("arbitrary", "arbitrary"), vmem_limit_bytes=56 * 1024 * 1024
         ),
+        cost_estimate=pl.CostEstimate(
+            flops=0,
+            transcendentals=0,
+            bytes_accessed=PLANE * kinds * rows * width * (2 + jnp.dtype(kind).itemsize),
+        ),
         name="place",
     )(spots, *sources)
 
@@ -556,28 +561,28 @@
     gain = norm_gains.astype(jnp.float32)
     tokens_hop = plane_hop(tokens)
     mlp_shard = jnp.concatenate([w_mlp_in.swapaxes(0, 1), w_mlp_out[None]], axis=0)
-    mlp_sides = side_pieces(after(mlp_shard, tokens_hop))
+    info_own = spread(jnp.concatenate([item_len, item_kind], axis=1))
+    info = jnp.stack([info_own[0], flip(info_own, YDIM)[0]], axis=0)
+    mlp_sides = side_pieces(after(mlp_shard, tokens_hop, info))
     tokens_here = level_hop(tokens_hop)
     ws_q, ws_k, ws_v = narrow_full(after(w_self_in.swapaxes(0, 1), tokens_here))
     x = tokens_here.astype(jnp.float32)
-    h1 = low(normed(x, gain[0]))
+    h1 = after(low(normed(x, gain[0])), info)
     rows_one = plane_gather(h1)
     ws_out, wc_q = narrow_full(after(jnp.stack([w_self_out, w_cross_q]), ws_q))
     wc_k, wc_v = narrow_full(after(w_cross_kv.swapaxes(0, 1), ws_out))
     (wc_out,) = narrow_full(after(w_cross_out[None], wc_k))
-    mlp_chip = corner_pieces(
-        [mlp_sides[0], *lax.optimization_barrier((*mlp_sides[1:], rows_one[1]))[:2]]
-    )
-    memory_here = level_hop(after(plane_hop(memory), tokens_here))
-    cotangent_here = level_hop(after(plane_hop(cotangent), memory_here))
+    rows_one, memory_hop, cotangent_hop = lax.optimization_barrier(
+        (rows_one, plane_hop(memory), plane_hop(cotangent))
+    )
+    memory_here = level_hop(memory_hop)
+    cotangent_here = level_hop(after(cotangent_hop, memory_here))
 
     me, level = lax.axis_index("wide"), lax.axis_index("narrow")
     differ = (me >> 1) ^ level
     side, upper = differ >> 1, differ & 1
     quarter = 2 * upper + ((me & 1) ^ side)
     spot_zero = 4 * side + quarter
-    info_own = spread(jnp.concatenate([item_len, item_kind], axis=1))
-    info = jnp.stack([info_own[0], flip(info_own, YDIM)[0]], axis=0)
     order = jnp.asarray([0, 2, 1, 3], jnp.int32)
     quarters = jnp.stack([quarter ^ order, quarter ^ 1 ^ order], axis=0)
     positions = (
@@ -614,25 +619,35 @@
         parts = [sum(matmul_nn(mat[part], weight) for mat, weight in terms) for part in (0, 1)]
         return plane_scatter(*parts)
 
-    def weight_sum(mats, rows):
-        return narrow_total(matmul_tn(mats[0], rows[0]) + matmul_tn(mats[1], rows[1]))
+    def weight_part(mats, rows):
+        return low(matmul_tn(mats[0], rows[0]) + matmul_tn(mats[1], rows[1]))
+
+    def packed_total(parts):
+        levels = lax.axis_size("narrow")
+        packed = jnp.stack([part.reshape(levels, -1, width) for part in parts], axis=1)
+        total = lax.psum_scatter(
+            packed.reshape(-1, width), "narrow", scatter_dimension=0, tiled=True
+        )
+        return total.reshape(len(parts), -1, width)
 
     sq, sk, sv = (project(rows_one, mat) for mat in (ws_q, ws_k, ws_v))
     self_result, self_lse = group_attend(sq, sk, sv, self_ok)
     self_heads = merge(self_result)
-    self_heads, mlp_chip = lax.optimization_barrier((self_heads, mlp_chip))
+    self_heads, mlp_sides, memory_here = lax.optimization_barrier(
+        (self_heads, mlp_sides, memory_here)
+    )
     x1 = x + spread_out([(self_heads, ws_out)])
     h2 = low(normed(x1, gain[1]))
-    h2, cotangent_here, memory_here = lax.optimization_barrier((h2, cotangent_here, memory_here))
-    memory_all = plane_gather(memory_here)
-    rows_two = plane_gather(h2)
+    memory_all = plane_gather(after(memory_here, h2))
+    rows_two, cotangent_here = lax.optimization_barrier((plane_gather(h2), cotangent_here))
     ck, cv = (project(memory_all, mat) for mat in (wc_k, wc_v))
     cq = project(rows_two, wc_q)
     cross_result, cross_lse = group_attend(cq, ck, cv, cross_ok)
     cross_heads = merge(cross_result * valid_float[:, :, None, None])
     grad_y = cotangent_here.astype(jnp.float32) * local_weight[:, None]
     grad_mlp = row_gather(after(low(grad_y), wc_out))
-    cross_heads, grad_mlp = lax.optimization_barrier((cross_heads, grad_mlp))
+    mlp_chip = corner_pieces(lax.optimization_barrier((mlp_sides, memory_all[0]))[0])
+    cross_heads, grad_mlp, mlp_chip = lax.optimization_barrier((cross_heads, grad_mlp, mlp_chip))
     x2 = x1 + spread_out([(cross_heads, wc_out)])
     h3 = low(normed(x2, gain[2]))
     rows_three = row_gather(h3)
@@ -678,65 +693,62 @@
     grad_x1 = grad_x2 + part_x1
     grad_x1, mlp_sums = lax.optimization_barrier((grad_x1, mlp_sums))
     grad_self = plane_gather(low(grad_x1))
-    memory_sides = scatter_start(
-        *(
-            matmul_nn(grad_ck[part], wc_k) + matmul_nn(grad_cv[part], wc_v)
-            for part in (0, 1)
-        )
-    )
+    memory_parts = [
+        low(matmul_nn(grad_ck[part], wc_k) + matmul_nn(grad_cv[part], wc_v)) for part in (0, 1)
+    ]
     mlp_here = spread(mlp_sums)
-    mid_sums = jnp.stack(
-        [
-            weight_sum(cross_heads, grad_cross),
-            weight_sum(grad_cv, memory_all),
-            weight_sum(grad_ck, memory_all),
-            weight_sum(grad_cq, rows_two),
-        ]
-    )
-    self_out_sum = weight_sum(self_heads, grad_self)
+    mid_parts = [
+        weight_part(cross_heads, grad_cross),
+        weight_part(grad_cv, memory_all),
+        weight_part(grad_ck, memory_all),
+        weight_part(grad_cq, rows_two),
+    ]
+    mid_sums = packed_total(mid_parts)
+    self_out_part = weight_part(self_heads, grad_self)
     grad_self_heads = project(grad_self, ws_out)
-    grad_self_heads, memory_sides = lax.optimization_barrier((grad_self_heads, memory_sides))
-    memory_sums = low(scatter_end(*memory_sides))
     gsq, gsk, gsv = (
         merge(mat) for mat in group_attend_back(sq, sk, sv, self_ok, self_lse, grad_self_heads)
     )
-    gsq, gsk, gsv, mlp_here, memory_sums = lax.optimization_barrier(
-        (gsq, gsk, gsv, mlp_here, memory_sums)
-    )
-    grad_memory = unspread(memory_sums)
-
-    def weight_part(mats, rows):
-        return low(matmul_tn(mats[0], rows[0]) + matmul_tn(mats[1], rows[1]))
-
-    in_parts = [weight_part(term, rows_one) for term in (gsv, gsk, gsq)]
-    in_parts, mlp_here = lax.optimization_barrier((in_parts, mlp_here))
-    in_sums = [narrow_total(part) for part in in_parts]
-    mlp_pieces = core_pieces(chip_pieces(mlp_here))
+    gsq, gsk, gsv, mlp_here, memory_parts = lax.optimization_barrier(
+        (gsq, gsk, gsv, mlp_here, memory_parts)
+    )
+
+    last_parts = [weight_part(term, rows_one) for term in (gsq, gsk, gsv)] + [self_out_part]
+    last_parts, mlp_here = lax.optimization_barrier((last_parts, mlp_here))
+    last = packed_total(last_parts)
+    mlp_sides = side_pieces(mlp_here)
     grad_h1 = spread_out([(gsq, ws_q), (gsk, ws_k), (gsv, ws_v)])
     _, norm_pull1 = jax.vjp(normed, x, gain[0])
     part_x, grad_gain1 = norm_pull1(grad_h1)
     grad_x = low(grad_x1 + part_x)
     gain_terms = jnp.stack([grad_gain1, grad_gain2, grad_gain3])
-    levels = jnp.sum(lax.all_gather(gain_terms, "narrow", axis=0, tiled=False), axis=0)
+    for bit in (1, 2):
+        pairs = [(i, i ^ bit) for i in range(lax.axis_size("narrow"))]
+        gain_terms = gain_terms + lax.ppermute(gain_terms, "narrow", pairs)
+    for bit in (CORE, XDIM, YDIM):
+        gain_terms = gain_terms + flip(gain_terms, bit)
     own_gains = width // lax.axis_size("narrow")
-    gain_own = lax.dynamic_slice_in_dim(levels, level * own_gains, own_gains, 1)
-    gain_total = jnp.sum(lax.all_gather(gain_own, "wide", axis=0, tiled=False), axis=0)
-    mid_sides = side_pieces(spread(after(mid_sums, grad_x, *mlp_pieces[1:3])))
-    last = jnp.stack([in_sums[2], in_sums[1], in_sums[0], self_out_sum])
-    last, mlp_pieces, mid_sides, grad_x, gain_total = lax.optimization_barrier(
-        (last, mlp_pieces, mid_sides, grad_x, gain_total)
+    gain_total = lax.dynamic_slice_in_dim(gain_terms, level * own_gains, own_gains, 1)
+    group_hop = plane_hop(jnp.concatenate([last, mid_sums], axis=0))
+    memory_sums = low(plane_scatter(memory_parts[0], after(memory_parts[1], mlp_sides[1])))
+    mlp_sides, group_hop, grad_x, memory_sums = lax.optimization_barrier(
+        (mlp_sides, group_hop, grad_x, memory_sums)
+    )
+    mlp_chip = corner_pieces(mlp_sides)
+    group_here = level_hop(group_hop)
+    mlp_chip, group_here = lax.optimization_barrier((mlp_chip, group_here))
+    grad_memory = unspread(memory_sums)
+    mlp_pieces = core_pieces(mlp_chip)
+    group_sides = side_pieces(group_here)
+    group_sides, mlp_pieces = lax.optimization_barrier((group_sides, mlp_pieces))
+    mlp_totals = placed(mlp_pieces, spot_zero, ((0, 1), (2,)))
+    group_chip = corner_pieces(group_sides)
+    group_chip, mlp_totals = lax.optimization_barrier((group_chip, mlp_totals))
+    in_totals, *other_totals = placed(
+        core_pieces(group_chip), spot_zero, ((0, 1, 2), (3,), (7,), (6, 5), (4,))
     )
     grad_tokens = unspread(grad_x)
-    mid_pieces = core_pieces(corner_pieces(mid_sides))
-    mlp_totals = placed(mlp_pieces, spot_zero, ((0, 1), (2,)))
-    last_hop, mlp_totals = lax.optimization_barrier((plane_hop(last), mlp_totals))
-    last_sides = side_pieces(level_hop(last_hop))
-    last_sides, mid_pieces = lax.optimization_barrier((last_sides, mid_pieces))
-    mid_totals = placed(mid_pieces, spot_zero, ((3,), (2, 1), (0,)))
-    last_chip = corner_pieces(last_sides)
-    last_chip, mid_totals = lax.optimization_barrier((last_chip, mid_totals))
-    in_totals, out_totals = placed(core_pieces(last_chip), spot_zero, ((0, 1, 2), (3,)))
-    branch_three = branch_sum(after(matmul_nn(hidden, wm_out), in_parts[2]))
+    branch_three = branch_sum(after(matmul_nn(hidden, wm_out), group_here))
     output = unspread(low(x2 + branch_three))
     return (
         output,
@@ -744,8 +756,7 @@
         grad_memory,
         gain_total,
         in_totals.swapaxes(0, 1),
-        out_totals,
-        *mid_totals,
+        *other_totals,
         *mlp_totals,
     )
 

time: 1260 us -> 1190 us (0.944)
  blocking collectives: 24.3 us -> 0 us
  local copies, waits for them, and re-layouts: 148 us -> 131 us
    all_gather x2 -> x0, blocking collectives: 24.3 us -> none  [the longest x1 12.1 us: per_device(): lax.all_gather(gain_own, 'wide', axis=0, tiled=False)]
    ppermute x87 -> x81, waiting for transfers between devices: 350 us -> 333 us  [flip(): return lax.ppermute(value, 'wide', [(i, i ^ bit) for i in range(PLANE)])]
    unnamed x293 -> x273, local copies, waits for them, and re-layouts: 47 us -> 34.1 us
    select_n x19 -> x17, other arithmetic: 15.9 us -> 25.5 us  [hop(): return jnp.where(jnp.asarray(stay, jnp.int32)[here] == 1, piece, moved)]
    pallas_call x4 -> x3, Pallas kernels: 72 us -> 63.2 us  [placed(): pl.pallas_call(body, grid_spec=pltpu.PrefetchScalarGridSpec(num_scalar_pr...]
    ppermute x20 -> x18, waiting for transfers between devices: 93 us -> 101 us  [hop(): lax.ppermute(piece, ('wide', 'narrow'), [pair for pair in pairs if pair[0...]
    ppermute x87 -> x81, starting transfers between devices: 150 us -> 143 us  [flip(): return lax.ppermute(value, 'wide', [(i, i ^ bit) for i in range(PLANE)])]
    reshape x24 -> x22, local copies, waits for them, and re-layouts: 22.6 us -> 26.6 us  [project(): low(matmul_nt(part, mat)).reshape(2, -1, heads_here, HEAD_DIM)]
  transfers between devices with their start and end apart: 124 -> 112, of which waited for: 47 -> 55; matrix products, arithmetic and copies ran while one was open for 30% -> 30% of each run, Pallas kernels for 5% -> 3%
where the time goes in v4:
time: 1190 us
  waiting for transfers between devices  500 us (42%)
  starting transfers between devices  203 us (17%)
  matrix products  197 us (17%)
  local copies, waits for them, and re-layouts  131 us (11%)
  other arithmetic  72.8 us (6%)
  Pallas kernels  63.2 us (5%)
  between operations  18.1 us (2%)
    ppermute x81, waiting for transfers between devices, flip(): return lax.ppermute(value, 'wide', [(i, i ^ bit) for i in range(PLANE)])  333 us
    ppermute x81, starting transfers between devices, flip(): return lax.ppermute(value, 'wide', [(i, i ^ bit) for i in range(PLANE)])  143 us
    ppermute x18, waiting for transfers between devices, hop(): lax.ppermute(piece, ('wide', 'narrow'), [pair for pair in pairs if pair[0...  101 us
    dot_general x19, matrix products, matmul_nt(): lax.dot_general(a, b, (((1,), (1,)), ((), ())), preferred_element_type=jn...  68.7 us
    pallas_call x3, Pallas kernels, placed(): pl.pallas_call(body, grid_spec=pltpu.PrefetchScalarGridSpec(num_scalar_pr...  63.2 us
    ppermute x18, starting transfers between devices, hop(): lax.ppermute(piece, ('wide', 'narrow'), [pair for pair in pairs if pair[0...  57.8 us
    dot_general x19, matrix products, matmul_tn(): lax.dot_general(a, b, (((0,), (0,)), ((), ())), preferred_element_type=jn...  49.5 us
    dot_general x19, matrix products, matmul_nn(): lax.dot_general(a, b, (((1,), (0,)), ((), ())), preferred_element_type=jn...  45.2 us
  transfers between devices with their start and end apart: 112, of which 55 were waited for; matrix products, arithmetic and copies ran while one was open for 30% of the time, Pallas kernels for 3%

profile of v4, /device:TPU:25, one launch (start us, length us, event | category | flops | bytes accessed | tf_op | source)
XLA Modules:
  0.0 1185.3 jit_solution(8410365495379420139)
XLA Ops:
  36.4 9.5 collective-permute-start.5
  47.6 10.2 collective-permute-start.8
  85.7 21.6 %collective-permute-done.10 = bf16[256,2048]{1,0:T(8,128)(2,1)} collective-permute-done((bf16[256,2048]{1,0:T(8,128)(2,1)}, bf16[256,2048]{1,0:T(8,128)(2,1)}, u32[]{:S(2)}, u32[]{:S(2)}) %collective-permute-start.10) | collective-permute-done | bytes 1048608 | tf_op jit(solution)/shard_map/ppermute | solution.py:111
  115.4 10.3 collective-permute-done.14
  158.3 29.3 %all-gather.9.cloned.1.call-done = bf16[4,128,2048]{2,1,0:T(8,128)(2,1)} async-done(((bf16[1,128,2048]{2,1,0:T(8,128)(2,1)}), bf16[4,128,2048]{2,1,0:T(8,128)(2,1)}) %all-gather.9.cloned.1.call-update) | async-done | bytes 2097168 | tf_op jit(solution)/shard_map/all_gather | solution.py:447
  199.5 9.9 collective-permute-done.16
  227.9 25.0 %collective-permute-done.26 = bf16[128,2048]{1,0:T(8,128)(2,1)S(1)} collective-permute-done((bf16[128,2048]{1,0:T(8,128)(2,1)}, bf16[128,2048]{1,0:T(8,128)(2,1)S(1)}, u32[]{:S(2)}, u32[]{:S(2)}) %collective-permute-start.26) | collective-permute-done | bytes 524320 | tf_op jit(solution)/shard_map/ppermute | solution.py:343
  347.9 9.7 all-gather.15.cloned.1.call-done
  365.8 11.0 collective-permute-done.34
  390.3 9.3 collective-permute-done.41.refs_9_
  403.3 18.5 %place.3 = (bf16[1280,2048]{1,0:T(8,128)(2,1)}, bf16[1280,2048]{1,0:T(8,128)(2,1)}, bf16[1280,2048]{1,0:T(8,128)(2,1)}) custom-call(s32[8]{0:T(128)} %broadcast_xor_fusion.1.refs_0_, bf16[3,160,2048]{2,1,0:T(8,128)(2,1)} %pad_maximum_fusion.4.refs_1_, bf16[3,160,2048]{2,1,0:T(8,128)(2,1)} %collective-permute-done.12.refs_2_, ...), custom_call_target="tpu_custom_call" | custom-call | bytes 31457280 | tf_op jit(solution)/shard_map/place/pallas_call | solution.py:522
  421.8 7.5 fusion.146
  471.6 23.2 %reduce-scatter.6.cloned.1.call-done = bf16[128,2048]{1,0:T(8,128)(2,1)} async-done(((bf16[512,2048]{1,0:T(8,128)(2,1)}), bf16[128,2048]{1,0:T(8,128)(2,1)}) %reduce-scatter.6.cloned.1.call-update) | async-done | bytes 524304 | tf_op jit(solution)/shard_map/reduce_scatter | solution.py:160
  502.1 11.1 collective-permute-done.44
  610.9 8.0 collective-permute-done.49
  649.7 9.7 collective-permute-done.55
  660.1 34.7 %collective-permute-done.56 = bf16[64,2048]{1,0:T(8,128)(2,1)S(1)} collective-permute-done((bf16[64,2048]{1,0:T(8,128)(2,1)S(1)}, bf16[64,2048]{1,0:T(8,128)(2,1)S(1)}, u32[]{:S(2)}, u32[]{:S(2)}) %collective-permute-start.56) | collective-permute-done | bytes 262176 | tf_op jit(solution)/shard_map/ppermute | solution.py:343
  745.3 17.3 %collective-permute-start.60 = (bf16[3,160,2048]{2,1,0:T(8,128)(2,1)}, bf16[3,160,2048]{2,1,0:T(8,128)(2,1)}, u32[]{:S(2)}, u32[]{:S(2)}) collective-permute-start(bf16[3,160,2048]{2,1,0:T(8,128)(2,1)} %broadcast_select_fusion.3.refs_1_), channel_id=1, source_target_pairs={{0,8},{4,12},{8,0},{12,4},{16,24},{20,28},{24,16},{28,20},{1,9},{5... | collective-permute-start | bytes 5898248 | tf_op jit(solution)/shard_map/ppermute | solution.py:343
  776.0 23.8 %collective-permute-done.60.refs_2_ = bf16[3,160,2048]{2,1,0:T(8,128)(2,1)} collective-permute-done((bf16[3,160,2048]{2,1,0:T(8,128)(2,1)}, bf16[3,160,2048]{2,1,0:T(8,128)(2,1)}, u32[]{:S(2)}, u32[]{:S(2)}) %collective-permute-start.60) | collective-permute-done | bytes 1966112 | tf_op jit(solution)/shard_map/ppermute | solution.py:343
  817.0 8.9 collective-permute-done.64
  834.9 41.3 %collective-permute-done.65 = bf16[64,2048]{1,0:T(8,128)(2,1)S(1)} collective-permute-done((bf16[64,2048]{1,0:T(8,128)(2,1)S(1)}, bf16[64,2048]{1,0:T(8,128)(2,1)S(1)}, u32[]{:S(2)}, u32[]{:S(2)}) %collective-permute-start.65) | collective-permute-done | bytes 262176 | tf_op jit(solution)/shard_map/ppermute | solution.py:343
  876.7 22.0 %collective-permute-done.71 = bf16[2,128,2048]{2,1,0:T(8,128)(2,1)S(1)} collective-permute-done((bf16[2,128,2048]{2,1,0:T(8,128)(2,1)S(1)}, bf16[2,128,2048]{2,1,0:T(8,128)(2,1)S(1)}, u32[]{:S(2)}, u32[]{:S(2)}) %collective-permute-start.71) | collective-permute-done | bytes 1048608 | tf_op jit(solution)/shard_map/ppermute | solution.py:343
  915.6 14.2 %collective-permute-done.70 = bf16[128,2048]{1,0:T(8,128)(2,1)S(1)} collective-permute-done((bf16[128,2048]{1,0:T(8,128)(2,1)S(1)}, bf16[128,2048]{1,0:T(8,128)(2,1)S(1)}, u32[]{:S(2)}, u32[]{:S(2)}) %collective-permute-start.70) | collective-permute-done | bytes 524320 | tf_op jit(solution)/shard_map/ppermute | solution.py:343
  931.1 29.7 %collective-permute-done.62 = bf16[8,64,2048]{2,1,0:T(8,128)(2,1)S(1)} collective-permute-done((bf16[8,64,2048]{2,1,0:T(8,128)(2,1)S(1)}, bf16[8,64,2048]{2,1,0:T(8,128)(2,1)S(1)}, u32[]{:S(2)}, u32[]{:S(2)}) %collective-permute-start.62) | collective-permute-done | bytes 2097184 | tf_op jit(solution)/shard_map/ppermute | solution.py:111
  976.1 12.5 %collective-permute-done.75 = bf16[8,64,2048]{2,1,0:T(8,128)(2,1)} collective-permute-done((bf16[8,64,2048]{2,1,0:T(8,128)(2,1)S(1)}, bf16[8,64,2048]{2,1,0:T(8,128)(2,1)}, u32[]{:S(2)}, u32[]{:S(2)}) %collective-permute-start.75) | collective-permute-done | bytes 2097184 | tf_op jit(solution)/shard_map/ppermute | solution.py:111
  1006.4 20.5 %collective-permute-start.85 = (f32[3,2048]{1,0:T(4,128)S(1)}, f32[3,2048]{1,0:T(4,128)S(1)}, u32[]{:S(2)}, u32[]{:S(2)}) collective-permute-start(f32[3,2048]{1,0:T(4,128)S(1)} %add.395), channel_id=1, source_target_pairs={{0,8},{4,12},{8,0},{12,4},{16,24},{20,28},{24,16},{28,20},{1,9},{5... | collective-permute-start | bytes 73736 | tf_op jit(solution)/shard_map/ppermute | solution.py:343
  1038.2 35.4 %collective-permute-done.88.refs_3_ = bf16[8,64,2048]{2,1,0:T(8,128)(2,1)} collective-permute-done((bf16[8,64,2048]{2,1,0:T(8,128)(2,1)S(1)}, bf16[8,64,2048]{2,1,0:T(8,128)(2,1)}, u32[]{:S(2)}, u32[]{:S(2)}) %collective-permute-start.88) | collective-permute-done | bytes 2097184 | tf_op jit(solution)/shard_map/ppermute | solution.py:343
  1091.4 9.4 collective-permute-done.95.refs_5_
  1100.8 7.9 collective-permute-start.81
  1109.3 22.1 %place.4 = (f32[1280,2,2048]{2,1,0:T(2,128)}, f32[1280,2048]{1,0:T(8,128)}) custom-call(s32[8]{0:T(128)} %broadcast_xor_fusion.refs_0_, bf16[3,160,2048]{2,1,0:T(8,128)(2,1)} %broadcast_select_fusion.3.refs_1_, bf16[3,160,2048]{2,1,0:T(8,128)(2,1)} %collective-permute-done.60.refs_2_, bf16[3,160,2048]{2,1,0:T(8,128)(2,1)} %collective-permute-done.61.refs_3_, ...), custom_call_target="tpu_custom_call" | custom-call | bytes 47185920 | tf_op jit(solution)/shard_map/place/pallas_call | solution.py:522
  1135.9 11.2 collective-permute-done.77
  1156.0 22.7 %place.5 = (f32[3,512,2048]{2,1,0:T(8,128)}, f32[512,2048]{1,0:T(8,128)}, f32[512,2048]{1,0:T(8,128)}, f32[512,2,2048]{2,1,0:T(2,128)}, f32[512,2048]{1,0:T(8,128)}) custom-call(s32[8]{0:T(128)} %broadcast_xor_fusion.refs_0_, bf16[8,64,2048]{2,1,0:T(8,128)(2,1)} %copy-done.23, bf16[8,64,2048]{2,1,0:T(8,128)(2,1)} %collective-permute-done.87.refs_2_, ...), custom_call_target="tpu_custom_call" | custom-call | bytes 50331648 | tf_op jit(solution)/shard_map/place/pallas_call | solution.py:522
  (741 shorter events, 610.1 us)
Async XLA Ops:
  7.2 120.9 %all-gather.7.cloned.1.call-start = ((), (), s32[]{:S(2)}) async-start(), calls=%async_computation.5 | async-start | bytes 3932160 | tf_op jit(solution)/shard_map/all_gather | solution.py:447
  45.9 141.7 %all-gather.9.cloned.1.call-start = ((), (), s32[]{:S(2)}) async-start(), calls=%async_computation.6 | async-start | bytes 2621440 | tf_op jit(solution)/shard_map/all_gather | solution.py:447
  113.9 44.4 %collective-permute-start.13 = (bf16[3,160,2048]{2,1,0:T(8,128)(2,1)}, bf16[3,160,2048]{2,1,0:T(8,128)(2,1)}, u32[]{:S(2)}, u32[]{:S(2)}) collective-permute-start(bf16[3,160,2048]{2,1,0:T(8,128)(2,1)} %pad_maximum_fusion.4.refs_1_), channel_id=1, source_target_pairs={{0,16},{4,20},{8,24},{12,28},{16,0},{20,4},{24,8},{28,12},{1,17},{... | collective-permute-start | bytes 5898248 | tf_op jit(solution)/shard_map/ppermute | solution.py:343
  114.7 43.6 %collective-permute-start.12 = (bf16[3,160,2048]{2,1,0:T(8,128)(2,1)}, bf16[3,160,2048]{2,1,0:T(8,128)(2,1)}, u32[]{:S(2)}, u32[]{:S(2)}) collective-permute-start(bf16[3,160,2048]{2,1,0:T(8,128)(2,1)} %pad_maximum_fusion.4.refs_1_), channel_id=1, source_target_pairs={{0,8},{4,12},{8,0},{12,4},{16,24},{20,28},{24,16},{28,20},{1,9},{5... | collective-permute-start | bytes 5898248 | tf_op jit(solution)/shard_map/ppermute | solution.py:343
  131.7 146.7 %all-gather.11.cloned.1.call-start = ((), (), s32[]{:S(2)}) async-start(), calls=%async_computation.7 | async-start | bytes 2621440 | tf_op jit(solution)/shard_map/all_gather | solution.py:447
  221.1 92.8 %all-gather.13.cloned.1.call-start = ((), (), s32[]{:S(2)}) async-start(), calls=%async_computation.8 | async-start | bytes 1310720 | tf_op jit(solution)/shard_map/all_gather | solution.py:447
  223.6 53.9 %collective-permute-start.30 = (bf16[128,2048]{1,0:T(8,128)(2,1)}, bf16[128,2048]{1,0:T(8,128)(2,1)S(1)}, u32[]{:S(2)}, u32[]{:S(2)}) collective-permute-start(bf16[128,2048]{1,0:T(8,128)(2,1)} %broadcast_select_fusion.13), channel_id=1, source_target_pairs={{5,4},{10,8},{15,12},{17,16},{30,28},{27,24},{8,9},{2,1},{7,5},{28... | collective-permute-start | bytes 1572872 | tf_op jit(solution)/shard_map/ppermute | solution.py:111
  272.1 44.3 %collective-permute-start.24 = (bf16[1024,2048]{1,0:T(8,128)(2,1)}, bf16[1024,2048]{1,0:T(8,128)(2,1)}, u32[]{:S(2)}, u32[]{:S(2)}) collective-permute-start(bf16[1024,2048]{1,0:T(8,128)(2,1)} %constant_dynamic-update-slice_fusion.5), channel_id=1, source_target_pairs={{0,4},{4,0},{8,12},{12,8},{16,20},{20,16},{24,28},{28,24},{1,5},{5... | collective-permute-start | bytes 12582920 | tf_op jit(solution)/shard_map/ppermute | solution.py:343
  280.1 77.5 %all-gather.15.cloned.1.call-start = ((), (), s32[]{:S(2)}) async-start(), calls=%async_computation.9 | async-start | bytes 2621440 | tf_op jit(solution)/shard_map/all_gather | solution.py:156
  299.7 48.2 %collective-permute-start.32 = (bf16[3,80,2048]{2,1,0:T(8,128)(2,1)}, bf16[3,80,2048]{2,1,0:T(8,128)(2,1)}, u32[]{:S(2)}, u32[]{:S(2)}) collective-permute-start(bf16[3,80,2048]{2,1,0:T(8,128)(2,1)} %slice.339), channel_id=1, source_target_pairs={{0,8},{4,12},{8,0},{12,4},{16,24},{20,28},{24,16},{28,20},{1,9},{5... | collective-permute-start | bytes 2949128 | tf_op jit(solution)/shard_map/ppermute | solution.py:343
  300.6 47.3 %collective-permute-start.31 = (bf16[3,80,2048]{2,1,0:T(8,128)(2,1)}, bf16[3,80,2048]{2,1,0:T(8,128)(2,1)}, u32[]{:S(2)}, u32[]{:S(2)}) collective-permute-start(bf16[3,80,2048]{2,1,0:T(8,128)(2,1)} %slice.338), channel_id=1, source_target_pairs={{0,16},{4,20},{8,24},{12,28},{16,0},{20,4},{24,8},{28,12},{1,17},{... | collective-permute-start | bytes 2949128 | tf_op jit(solution)/shard_map/ppermute | solution.py:343
  313.9 118.7 %all-gather.17.cloned.1.call-start = ((), (), s32[]{:S(2)}) async-start(), calls=%async_computation.10 | async-start | bytes 2621440 | tf_op jit(solution)/shard_map/all_gather | solution.py:156
  385.9 108.9 %reduce-scatter.6.cloned.1.call-start = ((), (), s32[]{:S(2)}) async-start(), calls=%async_computation.11 | async-start | bytes 2621440 | tf_op jit(solution)/shard_map/reduce_scatter | solution.py:160
  451.8 178.5 %reduce-scatter.8.cloned.1.call-start = ((), (), s32[]{:S(2)}) async-start(), calls=%async_computation.12 | async-start | bytes 17694720 | tf_op jit(solution)/shard_map/reduce_scatter | solution.py:676
  496.9 405.7 %reduce-scatter.12.cloned.1.call-start = ((), (), s32[]{:S(2)}) async-start(), calls=%async_computation.14 | async-start | bytes 5242880 | tf_op jit(solution)/shard_map/reduce_scatter | solution.py:628
  604.8 297.8 %reduce-scatter.10.cloned.1.call-start = ((), (), s32[]{:S(2)}) async-start(), calls=%async_computation.13 | async-start | bytes 5242880 | tf_op jit(solution)/shard_map/reduce_scatter | solution.py:628
  640.9 61.8 %collective-permute-start.58 = (bf16[3,160,2048]{2,1,0:T(8,128)(2,1)}, bf16[3,160,2048]{2,1,0:T(8,128)(2,1)}, u32[]{:S(2)}, u32[]{:S(2)}) collective-permute-start(bf16[3,160,2048]{2,1,0:T(8,128)(2,1)} %bitcast.64), channel_id=1, source_target_pairs={{1,5},{2,10},{3,15},{4,20},{5,17},{6,30},{7,27},{9,13},{10,2},{11,... | collective-permute-start | bytes 5898248 | tf_op jit(solution)/shard_map/ppermute | solution.py:111
  646.3 48.5 %collective-permute-start.56 = (bf16[64,2048]{1,0:T(8,128)(2,1)S(1)}, bf16[64,2048]{1,0:T(8,128)(2,1)S(1)}, u32[]{:S(2)}, u32[]{:S(2)}) collective-permute-start(bf16[64,2048]{1,0:T(8,128)(2,1)S(1)} %slice.444), channel_id=1, source_target_pairs={{0,8},{4,12},{8,0},{12,4},{16,24},{20,28},{24,16},{28,20},{1,9},{5... | collective-permute-start | bytes 786440 | tf_op jit(solution)/shard_map/ppermute | solution.py:343
  745.3 54.5 %collective-permute-start.60 = (bf16[3,160,2048]{2,1,0:T(8,128)(2,1)}, bf16[3,160,2048]{2,1,0:T(8,128)(2,1)}, u32[]{:S(2)}, u32[]{:S(2)}) collective-permute-start(bf16[3,160,2048]{2,1,0:T(8,128)(2,1)} %broadcast_select_fusion.3.refs_1_), channel_id=1, source_target_pairs={{0,8},{4,12},{8,0},{12,4},{16,24},{20,28},{24,16},{28,20},{1,9},{5... | collective-permute-start | bytes 5898248 | tf_op jit(solution)/shard_map/ppermute | solution.py:343
  776.0 310.9 %reduce-scatter.14.cloned.1.call-start = ((), (), s32[]{:S(2)}) async-start(), calls=%async_computation.15 | async-start | bytes 2621440 | tf_op jit(solution)/shard_map/reduce_scatter | solution.py:160
  816.9 144.1 %collective-permute-start.61 = (bf16[3,160,2048]{2,1,0:T(8,128)(2,1)}, bf16[3,160,2048]{2,1,0:T(8,128)(2,1)}, u32[]{:S(2)}, u32[]{:S(2)}) collective-permute-start(bf16[3,160,2048]{2,1,0:T(8,128)(2,1)} %broadcast_select_fusion.3.refs_1_), channel_id=1, source_target_pairs={{0,16},{4,20},{8,24},{12,28},{16,0},{20,4},{24,8},{28,12},{1,17},{... | collective-permute-start | bytes 5898248 | tf_op jit(solution)/shard_map/ppermute | solution.py:343
  829.4 46.8 %collective-permute-start.65 = (bf16[64,2048]{1,0:T(8,128)(2,1)S(1)}, bf16[64,2048]{1,0:T(8,128)(2,1)S(1)}, u32[]{:S(2)}, u32[]{:S(2)}) collective-permute-start(bf16[64,2048]{1,0:T(8,128)(2,1)S(1)} %fusion.99), channel_id=1, source_target_pairs={{0,16},{4,20},{8,24},{12,28},{16,0},{20,4},{24,8},{28,12},{1,17},{... | collective-permute-start | bytes 786440 | tf_op jit(solution)/shard_map/ppermute | solution.py:343
  834.4 64.3 %collective-permute-start.71 = (bf16[2,128,2048]{2,1,0:T(8,128)(2,1)S(1)}, bf16[2,128,2048]{2,1,0:T(8,128)(2,1)S(1)}, u32[]{:S(2)}, u32[]{:S(2)}) collective-permute-start(bf16[2,128,2048]{2,1,0:T(8,128)(2,1)S(1)} %slice_bitcast_fusion.1), channel_id=1, source_target_pairs={{0,16},{4,20},{8,24},{12,28},{16,0},{20,4},{24,8},{28,12},{1,17},{... | collective-permute-start | bytes 3145736 | tf_op jit(solution)/shard_map/ppermute | solution.py:343
  904.4 56.3 %collective-permute-start.62 = (bf16[8,64,2048]{2,1,0:T(8,128)(2,1)S(1)}, bf16[8,64,2048]{2,1,0:T(8,128)(2,1)S(1)}, u32[]{:S(2)}, u32[]{:S(2)}) collective-permute-start(bf16[8,64,2048]{2,1,0:T(8,128)(2,1)S(1)} %pad_maximum_fusion.3), channel_id=1, source_target_pairs={{1,5},{2,10},{3,15},{4,20},{5,17},{6,30},{7,27},{9,13},{10,2},{11,... | collective-permute-start | bytes 6291464 | tf_op jit(solution)/shard_map/ppermute | solution.py:111
  1026.9 46.7 %collective-permute-start.88 = (bf16[8,64,2048]{2,1,0:T(8,128)(2,1)S(1)}, bf16[8,64,2048]{2,1,0:T(8,128)(2,1)}, u32[]{:S(2)}, u32[]{:S(2)}) collective-permute-start(bf16[8,64,2048]{2,1,0:T(8,128)(2,1)S(1)} %broadcast_select_fusion.refs_1_), channel_id=1, source_target_pairs={{0,16},{4,20},{8,24},{12,28},{16,0},{20,4},{24,8},{28,12},{1,17},{... | collective-permute-start | bytes 6291464 | tf_op jit(solution)/shard_map/ppermute | solution.py:343
  1028.6 46.5 %collective-permute-start.87 = (bf16[8,64,2048]{2,1,0:T(8,128)(2,1)S(1)}, bf16[8,64,2048]{2,1,0:T(8,128)(2,1)}, u32[]{:S(2)}, u32[]{:S(2)}) collective-permute-start(bf16[8,64,2048]{2,1,0:T(8,128)(2,1)S(1)} %broadcast_select_fusion.refs_1_), channel_id=1, source_target_pairs={{0,8},{4,12},{8,0},{12,4},{16,24},{20,28},{24,16},{28,20},{1,9},{5... | collective-permute-start | bytes 6291464 | tf_op jit(solution)/shard_map/ppermute | solution.py:343
  1031.5 47.0 %collective-permute-start.78 = (bf16[128,2048]{1,0:T(8,128)(2,1)}, bf16[128,2048]{1,0:T(8,128)(2,1)}, u32[]{:S(2)}, u32[]{:S(2)}) collective-permute-start(bf16[128,2048]{1,0:T(8,128)(2,1)} %fusion.53), channel_id=1, source_target_pairs={{4,5},{8,10},{12,15},{16,17},{28,30},{24,27},{9,8},{1,2},{5,7},{29... | collective-permute-start | bytes 1572872 | tf_op jit(solution)/shard_map/ppermute | solution.py:111
  1035.4 52.7 %collective-permute-start.80 = (bf16[256,2048]{1,0:T(8,128)(2,1)}, bf16[256,2048]{1,0:T(8,128)(2,1)}, u32[]{:S(2)}, u32[]{:S(2)}) collective-permute-start(bf16[256,2048]{1,0:T(8,128)(2,1)} %pad_maximum_fusion.8), channel_id=1, source_target_pairs={{4,5},{8,10},{12,15},{16,17},{28,30},{24,27},{9,8},{1,2},{5,7},{29... | collective-permute-start | bytes 3145736 | tf_op jit(solution)/shard_map/ppermute | solution.py:111
  1038.2 93.2 %collective-permute-start.86 = (f32[3,2048]{1,0:T(4,128)S(1)}, f32[3,2048]{1,0:T(4,128)S(1)}, u32[]{:S(2)}, u32[]{:S(2)}) collective-permute-start(f32[3,2048]{1,0:T(4,128)S(1)} %add.396), channel_id=1, source_target_pairs={{0,16},{4,20},{8,24},{12,28},{16,0},{20,4},{24,8},{28,12},{1,17},{... | collective-permute-start | bytes 73736 | tf_op jit(solution)/shard_map/ppermute | solution.py:343
  1080.5 52.4 %collective-permute-start.79 = (bf16[128,2048]{1,0:T(8,128)(2,1)}, bf16[128,2048]{1,0:T(8,128)(2,1)}, u32[]{:S(2)}, u32[]{:S(2)}) collective-permute-start(bf16[128,2048]{1,0:T(8,128)(2,1)} %broadcast_select_fusion.8), channel_id=1, source_target_pairs={{5,1},{10,2},{15,3},{20,4},{17,5},{30,6},{27,7},{13,9},{2,10},{7,1... | collective-permute-start | bytes 1572872 | tf_op jit(solution)/shard_map/ppermute | solution.py:111
  1086.8 44.5 %collective-permute-start.94 = (bf16[8,32,2048]{2,1,0:T(8,128)(2,1)}, bf16[8,32,2048]{2,1,0:T(8,128)(2,1)}, u32[]{:S(2)}, u32[]{:S(2)}) collective-permute-start(bf16[8,32,2048]{2,1,0:T(8,128)(2,1)} %slice.391), channel_id=1, source_target_pairs={{0,16},{4,20},{8,24},{12,28},{16,0},{20,4},{24,8},{28,12},{1,17},{... | collective-permute-start | bytes 3145736 | tf_op jit(solution)/shard_map/ppermute | solution.py:343
  1088.1 43.8 %collective-permute-start.76 = (bf16[128,2048]{1,0:T(8,128)(2,1)S(1)}, bf16[128,2048]{1,0:T(8,128)(2,1)S(1)}, u32[]{:S(2)}, u32[]{:S(2)}) collective-permute-start(bf16[128,2048]{1,0:T(8,128)(2,1)S(1)} %add_convert_fusion.9), channel_id=1, source_target_pairs={{4,5},{8,10},{12,15},{16,17},{28,30},{24,27},{9,8},{1,2},{5,7},{29... | collective-permute-start | bytes 1572872 | tf_op jit(solution)/shard_map/ppermute | solution.py:111
  (197 other events, 3192.1 us)
Sparse Core Ops, SparseCore 0:
  46.0 61.7 all-gather.6
  131.8 55.7 all-gather.8
  221.2 53.9 all-gather.10
  280.2 26.9 all-gather.12
  314.0 43.6 all-gather.14
  386.0 46.5 all-gather.16
  451.9 42.7 reduce-scatter.5
  498.8 115.3 reduce-scatter.7
  617.1 77.1 reduce-scatter.11
  776.1 74.7 reduce-scatter.9
  992.1 72.5 reduce-scatter.13

commit v5 on v4

--- a/solution.py
+++ b/solution.py
@@ -563,12 +563,12 @@
     mlp_shard = jnp.concatenate([w_mlp_in.swapaxes(0, 1), w_mlp_out[None]], axis=0)
     info_own = spread(jnp.concatenate([item_len, item_kind], axis=1))
     info = jnp.stack([info_own[0], flip(info_own, YDIM)[0]], axis=0)
-    mlp_sides = side_pieces(after(mlp_shard, tokens_hop, info))
     tokens_here = level_hop(tokens_hop)
     ws_q, ws_k, ws_v = narrow_full(after(w_self_in.swapaxes(0, 1), tokens_here))
     x = tokens_here.astype(jnp.float32)
     h1 = after(low(normed(x, gain[0])), info)
     rows_one = plane_gather(h1)
+    mlp_sides = side_pieces(after(mlp_shard, ws_q))
     ws_out, wc_q = narrow_full(after(jnp.stack([w_self_out, w_cross_q]), ws_q))
     wc_k, wc_v = narrow_full(after(w_cross_kv.swapaxes(0, 1), ws_out))
     (wc_out,) = narrow_full(after(w_cross_out[None], wc_k))
@@ -709,9 +709,7 @@
     gsq, gsk, gsv = (
         merge(mat) for mat in group_attend_back(sq, sk, sv, self_ok, self_lse, grad_self_heads)
     )
-    gsq, gsk, gsv, mlp_here, memory_parts = lax.optimization_barrier(
-        (gsq, gsk, gsv, mlp_here, memory_parts)
-    )
+    gsq, gsk, gsv, memory_parts = lax.optimization_barrier((gsq, gsk, gsv, memory_parts))
 
     last_parts = [weight_part(term, rows_one) for term in (gsq, gsk, gsv)] + [self_out_part]
     last_parts, mlp_here = lax.optimization_barrier((last_parts, mlp_here))
@@ -730,7 +728,7 @@
     own_gains = width // lax.axis_size("narrow")
     gain_total = lax.dynamic_slice_in_dim(gain_terms, level * own_gains, own_gains, 1)
     group_hop = plane_hop(jnp.concatenate([last, mid_sums], axis=0))
-    memory_sums = low(plane_scatter(memory_parts[0], after(memory_parts[1], mlp_sides[1])))
+    memory_sums = low(plane_scatter(memory_parts[0], memory_parts[1]))
     mlp_sides, group_hop, grad_x, memory_sums = lax.optimization_barrier(
         (mlp_sides, group_hop, grad_x, memory_sums)
     )

time: 1190 us -> 1150 us (0.966)
  waiting for transfers between devices: 500 us -> 454 us
    all_gather x4, waiting for transfers between devices: 29.3 us -> 1.61 us  [narrow_full(): lax.all_gather(stacked.reshape(kinds * rows, width), 'narrow', axis=0, ti...]
    ppermute x81, waiting for transfers between devices: 333 us -> 312 us  [flip(): return lax.ppermute(value, 'wide', [(i, i ^ bit) for i in range(PLANE)])]
    unnamed x273 -> x275, local copies, waits for them, and re-layouts: 34.1 us -> 35.4 us
  transfers between devices with their start and end apart: 112 -> 112, of which waited for: 55 -> 57; matrix products, arithmetic and copies ran while one was open for 30% -> 31% of each run, Pallas kernels for 3% -> 4%
where the time goes in v5:
time: 1150 us; the launch traced here: 1140 us
  waiting for transfers between devices  454 us (39%)
  starting transfers between devices  199 us (17%)
  matrix products  197 us (17%)
  local copies, waits for them, and re-layouts  130 us (11%)
  other arithmetic  74.6 us (6%)
  Pallas kernels  63.2 us (5%)
  between operations  18.1 us (2%)
    ppermute x81, waiting for transfers between devices, flip(): return lax.ppermute(value, 'wide', [(i, i ^ bit) for i in range(PLANE)])  312 us
    ppermute x81, starting transfers between devices, flip(): return lax.ppermute(value, 'wide', [(i, i ^ bit) for i in range(PLANE)])  138 us
    ppermute x18, waiting for transfers between devices, hop(): lax.ppermute(piece, ('wide', 'narrow'), [pair for pair in pairs if pair[0...  103 us
    dot_general x19, matrix products, matmul_nt(): lax.dot_general(a, b, (((1,), (1,)), ((), ())), preferred_element_type=jn...  68.9 us
    pallas_call x3, Pallas kernels, placed(): pl.pallas_call(body, grid_spec=pltpu.PrefetchScalarGridSpec(num_scalar_pr...  63.2 us
    ppermute x18, starting transfers between devices, hop(): lax.ppermute(piece, ('wide', 'narrow'), [pair for pair in pairs if pair[0...  59.7 us
    dot_general x19, matrix products, matmul_tn(): lax.dot_general(a, b, (((0,), (0,)), ((), ())), preferred_element_type=jn...  49.9 us
    dot_general x19, matrix products, matmul_nn(): lax.dot_general(a, b, (((1,), (0,)), ((), ())), preferred_element_type=jn...  43.4 us
  transfers between devices with their start and end apart: 112, of which 57 were waited for; matrix products, arithmetic and copies ran while one was open for 31% of the time, Pallas kernels for 4%

profile of v5, /device:TPU:25, one launch (start us, length us, event | category | flops | bytes accessed | tf_op | source)
XLA Modules:
  0.0 1136.2 jit_solution(12026767174075809470)
XLA Ops:
  36.4 9.5 collective-permute-start.5
  47.6 10.2 collective-permute-start.8
  85.7 21.6 %collective-permute-done.10 = bf16[256,2048]{1,0:T(8,128)(2,1)} collective-permute-done((bf16[256,2048]{1,0:T(8,128)(2,1)}, bf16[256,2048]{1,0:T(8,128)(2,1)}, u32[]{:S(2)}, u32[]{:S(2)}) %collective-permute-start.10) | collective-permute-done | bytes 1048608 | tf_op jit(solution)/shard_map/ppermute | solution.py:111
  113.9 11.5 %collective-permute-done.14 = bf16[256,2048]{1,0:T(8,128)(2,1)} collective-permute-done((bf16[256,2048]{1,0:T(8,128)(2,1)}, bf16[256,2048]{1,0:T(8,128)(2,1)}, u32[]{:S(2)}, u32[]{:S(2)}) %collective-permute-start.14) | collective-permute-done | bytes 1048608 | tf_op jit(solution)/shard_map/ppermute | solution.py:111
  131.4 13.5 %collective-permute-start.12 = (bf16[3,160,2048]{2,1,0:T(8,128)(2,1)}, bf16[3,160,2048]{2,1,0:T(8,128)(2,1)}, u32[]{:S(2)}, u32[]{:S(2)}) collective-permute-start(bf16[3,160,2048]{2,1,0:T(8,128)(2,1)} %pad_maximum_fusion.4.refs_1_), channel_id=1, source_target_pairs={{0,8},{4,12},{8,0},{12,4},{16,24},{20,28},{24,16},{28,20},{1,9},{5... | collective-permute-start | bytes 5898248 | tf_op jit(solution)/shard_map/ppermute | solution.py:343
  174.6 13.4 %collective-permute-done.12.refs_2_ = bf16[3,160,2048]{2,1,0:T(8,128)(2,1)} collective-permute-done((bf16[3,160,2048]{2,1,0:T(8,128)(2,1)}, bf16[3,160,2048]{2,1,0:T(8,128)(2,1)}, u32[]{:S(2)}, u32[]{:S(2)}) %collective-permute-start.12) | collective-permute-done | bytes 1966112 | tf_op jit(solution)/shard_map/ppermute | solution.py:343
  201.6 9.9 collective-permute-done.16
  229.9 25.0 %collective-permute-done.26 = bf16[128,2048]{1,0:T(8,128)(2,1)S(1)} collective-permute-done((bf16[128,2048]{1,0:T(8,128)(2,1)}, bf16[128,2048]{1,0:T(8,128)(2,1)S(1)}, u32[]{:S(2)}, u32[]{:S(2)}) %collective-permute-start.26) | collective-permute-done | bytes 524320 | tf_op jit(solution)/shard_map/ppermute | solution.py:343
  349.9 9.8 all-gather.15.cloned.1.call-done
  367.8 11.0 collective-permute-done.34
  392.4 9.2 collective-permute-done.41.refs_9_
  405.3 18.5 %place.3 = (bf16[1280,2048]{1,0:T(8,128)(2,1)}, bf16[1280,2048]{1,0:T(8,128)(2,1)}, bf16[1280,2048]{1,0:T(8,128)(2,1)}) custom-call(s32[8]{0:T(128)} %broadcast_xor_fusion.1.refs_0_, bf16[3,160,2048]{2,1,0:T(8,128)(2,1)} %pad_maximum_fusion.4.refs_1_, bf16[3,160,2048]{2,1,0:T(8,128)(2,1)} %collective-permute-done.12.refs_2_, ...), custom_call_target="tpu_custom_call" | custom-call | bytes 31457280 | tf_op jit(solution)/shard_map/place/pallas_call | solution.py:522
  423.9 7.5 fusion.146
  473.7 23.1 %reduce-scatter.6.cloned.1.call-done = bf16[128,2048]{1,0:T(8,128)(2,1)} async-done(((bf16[512,2048]{1,0:T(8,128)(2,1)}), bf16[128,2048]{1,0:T(8,128)(2,1)}) %reduce-scatter.6.cloned.1.call-update) | async-done | bytes 524304 | tf_op jit(solution)/shard_map/reduce_scatter | solution.py:160
  504.1 11.0 collective-permute-done.44
  613.0 8.0 collective-permute-done.49
  651.8 9.7 collective-permute-done.55
  662.2 34.7 %collective-permute-done.56 = bf16[64,2048]{1,0:T(8,128)(2,1)S(1)} collective-permute-done((bf16[64,2048]{1,0:T(8,128)(2,1)S(1)}, bf16[64,2048]{1,0:T(8,128)(2,1)S(1)}, u32[]{:S(2)}, u32[]{:S(2)}) %collective-permute-start.56) | collective-permute-done | bytes 262176 | tf_op jit(solution)/shard_map/ppermute | solution.py:343
  770.4 8.5 collective-permute-done.66
  787.7 31.8 %collective-permute-done.67 = bf16[64,2048]{1,0:T(8,128)(2,1)S(1)} collective-permute-done((bf16[64,2048]{1,0:T(8,128)(2,1)S(1)}, bf16[64,2048]{1,0:T(8,128)(2,1)S(1)}, u32[]{:S(2)}, u32[]{:S(2)}) %collective-permute-start.67) | collective-permute-done | bytes 262176 | tf_op jit(solution)/shard_map/ppermute | solution.py:343
  819.5 9.5 collective-permute-start.71
  829.6 12.3 %collective-permute-done.69 = bf16[2,128,2048]{2,1,0:T(8,128)(2,1)S(1)} collective-permute-done((bf16[2,128,2048]{2,1,0:T(8,128)(2,1)S(1)}, bf16[2,128,2048]{2,1,0:T(8,128)(2,1)S(1)}, u32[]{:S(2)}, u32[]{:S(2)}) %collective-permute-start.69) | collective-permute-done | bytes 1048608 | tf_op jit(solution)/shard_map/ppermute | solution.py:343
  841.8 8.9 collective-permute-done.71
  866.7 18.7 %collective-permute-done.70 = bf16[128,2048]{1,0:T(8,128)(2,1)S(1)} collective-permute-done((bf16[128,2048]{1,0:T(8,128)(2,1)S(1)}, bf16[128,2048]{1,0:T(8,128)(2,1)S(1)}, u32[]{:S(2)}, u32[]{:S(2)}) %collective-permute-start.70) | collective-permute-done | bytes 524320 | tf_op jit(solution)/shard_map/ppermute | solution.py:343
  886.6 26.3 %collective-permute-done.62 = bf16[8,64,2048]{2,1,0:T(8,128)(2,1)S(1)} collective-permute-done((bf16[8,64,2048]{2,1,0:T(8,128)(2,1)S(1)}, bf16[8,64,2048]{2,1,0:T(8,128)(2,1)S(1)}, u32[]{:S(2)}, u32[]{:S(2)}) %collective-permute-start.62) | collective-permute-done | bytes 2097184 | tf_op jit(solution)/shard_map/ppermute | solution.py:111
  927.0 13.7 %collective-permute-done.75 = bf16[8,64,2048]{2,1,0:T(8,128)(2,1)} collective-permute-done((bf16[8,64,2048]{2,1,0:T(8,128)(2,1)S(1)}, bf16[8,64,2048]{2,1,0:T(8,128)(2,1)}, u32[]{:S(2)}, u32[]{:S(2)}) %collective-permute-start.75) | collective-permute-done | bytes 2097184 | tf_op jit(solution)/shard_map/ppermute | solution.py:111
  945.0 22.8 %collective-permute-start.92 = (bf16[3,80,2048]{2,1,0:T(8,128)(2,1)}, bf16[3,80,2048]{2,1,0:T(8,128)(2,1)}, u32[]{:S(2)}, u32[]{:S(2)}) collective-permute-start(bf16[3,80,2048]{2,1,0:T(8,128)(2,1)} %collective-permute-done.73.refs_4_), channel_id=1, source_target_pairs={{0,4},{4,0},{8,12},{12,8},{16,20},{20,16},{24,28},{28,24},{1,5},{5... | collective-permute-start | bytes 2949128 | tf_op jit(solution)/shard_map/ppermute | solution.py:343
  989.1 35.4 %collective-permute-done.88.refs_3_ = bf16[8,64,2048]{2,1,0:T(8,128)(2,1)} collective-permute-done((bf16[8,64,2048]{2,1,0:T(8,128)(2,1)S(1)}, bf16[8,64,2048]{2,1,0:T(8,128)(2,1)}, u32[]{:S(2)}, u32[]{:S(2)}) %collective-permute-start.88) | collective-permute-done | bytes 2097184 | tf_op jit(solution)/shard_map/ppermute | solution.py:343
  1051.3 8.3 collective-permute-start.81
  1060.1 22.1 %place.4 = (f32[1280,2,2048]{2,1,0:T(2,128)}, f32[1280,2048]{1,0:T(8,128)}) custom-call(s32[8]{0:T(128)} %broadcast_xor_fusion.refs_0_, bf16[3,160,2048]{2,1,0:T(8,128)(2,1)} %broadcast_select_fusion.3.refs_1_, bf16[3,160,2048]{2,1,0:T(8,128)(2,1)} %collective-permute-done.60.refs_2_, bf16[3,160,2048]{2,1,0:T(8,128)(2,1)} %collective-permute-done.61.refs_3_, ...), custom_call_target="tpu_custom_call" | custom-call | bytes 47185920 | tf_op jit(solution)/shard_map/place/pallas_call | solution.py:522
  1086.7 11.7 %collective-permute-done.77 = bf16[128,2048]{1,0:T(8,128)(2,1)} collective-permute-done((bf16[128,2048]{1,0:T(8,128)(2,1)}, bf16[128,2048]{1,0:T(8,128)(2,1)}, u32[]{:S(2)}, u32[]{:S(2)}) %collective-permute-start.77) | collective-permute-done | bytes 524320 | tf_op jit(solution)/shard_map/ppermute | solution.py:111
  1106.9 22.7 %place.5 = (f32[3,512,2048]{2,1,0:T(8,128)}, f32[512,2048]{1,0:T(8,128)}, f32[512,2048]{1,0:T(8,128)}, f32[512,2,2048]{2,1,0:T(2,128)}, f32[512,2048]{1,0:T(8,128)}) custom-call(s32[8]{0:T(128)} %broadcast_xor_fusion.refs_0_, bf16[8,64,2048]{2,1,0:T(8,128)(2,1)} %copy-done.23, bf16[8,64,2048]{2,1,0:T(8,128)(2,1)} %collective-permute-done.87.refs_2_, ...), custom_call_target="tpu_custom_call" | custom-call | bytes 50331648 | tf_op jit(solution)/shard_map/place/pallas_call | solution.py:522
  (744 shorter events, 608.4 us)
Async XLA Ops:
  7.2 120.6 %all-gather.7.cloned.1.call-start = ((), (), s32[]{:S(2)}) async-start(), calls=%async_computation.5 | async-start | bytes 3932160 | tf_op jit(solution)/shard_map/all_gather | solution.py:447
  45.9 143.7 %all-gather.9.cloned.1.call-start = ((), (), s32[]{:S(2)}) async-start(), calls=%async_computation.6 | async-start | bytes 2621440 | tf_op jit(solution)/shard_map/all_gather | solution.py:447
  66.3 43.3 %collective-permute-start.9 = (bf16[512,2048]{1,0:T(8,128)(2,1)S(1)}, bf16[512,2048]{1,0:T(8,128)(2,1)}, u32[]{:S(2)}, u32[]{:S(2)}) collective-permute-start(bf16[512,2048]{1,0:T(8,128)(2,1)S(1)} %constant_dynamic-update-slice_fusion), channel_id=1, source_target_pairs={{0,4},{4,0},{8,12},{12,8},{16,20},{20,16},{24,28},{28,24},{1,5},{5... | collective-permute-start | bytes 6291464 | tf_op jit(solution)/shard_map/ppermute | solution.py:343
  131.4 56.6 %collective-permute-start.12 = (bf16[3,160,2048]{2,1,0:T(8,128)(2,1)}, bf16[3,160,2048]{2,1,0:T(8,128)(2,1)}, u32[]{:S(2)}, u32[]{:S(2)}) collective-permute-start(bf16[3,160,2048]{2,1,0:T(8,128)(2,1)} %pad_maximum_fusion.4.refs_1_), channel_id=1, source_target_pairs={{0,8},{4,12},{8,0},{12,4},{16,24},{20,28},{24,16},{28,20},{1,9},{5... | collective-permute-start | bytes 5898248 | tf_op jit(solution)/shard_map/ppermute | solution.py:343
  145.0 135.5 %all-gather.11.cloned.1.call-start = ((), (), s32[]{:S(2)}) async-start(), calls=%async_computation.7 | async-start | bytes 2621440 | tf_op jit(solution)/shard_map/all_gather | solution.py:447
  223.1 92.8 %all-gather.13.cloned.1.call-start = ((), (), s32[]{:S(2)}) async-start(), calls=%async_computation.8 | async-start | bytes 1310720 | tf_op jit(solution)/shard_map/all_gather | solution.py:447
  225.6 54.0 %collective-permute-start.30 = (bf16[128,2048]{1,0:T(8,128)(2,1)}, bf16[128,2048]{1,0:T(8,128)(2,1)S(1)}, u32[]{:S(2)}, u32[]{:S(2)}) collective-permute-start(bf16[128,2048]{1,0:T(8,128)(2,1)} %broadcast_select_fusion.13), channel_id=1, source_target_pairs={{5,4},{10,8},{15,12},{17,16},{30,28},{27,24},{8,9},{2,1},{7,5},{28... | collective-permute-start | bytes 1572872 | tf_op jit(solution)/shard_map/ppermute | solution.py:111
  274.1 44.3 %collective-permute-start.24 = (bf16[1024,2048]{1,0:T(8,128)(2,1)}, bf16[1024,2048]{1,0:T(8,128)(2,1)}, u32[]{:S(2)}, u32[]{:S(2)}) collective-permute-start(bf16[1024,2048]{1,0:T(8,128)(2,1)} %constant_dynamic-update-slice_fusion.5), channel_id=1, source_target_pairs={{0,4},{4,0},{8,12},{12,8},{16,20},{20,16},{24,28},{28,24},{1,5},{5... | collective-permute-start | bytes 12582920 | tf_op jit(solution)/shard_map/ppermute | solution.py:343
  282.2 77.5 %all-gather.15.cloned.1.call-start = ((), (), s32[]{:S(2)}) async-start(), calls=%async_computation.9 | async-start | bytes 2621440 | tf_op jit(solution)/shard_map/all_gather | solution.py:156
  301.7 48.2 %collective-permute-start.32 = (bf16[3,80,2048]{2,1,0:T(8,128)(2,1)}, bf16[3,80,2048]{2,1,0:T(8,128)(2,1)}, u32[]{:S(2)}, u32[]{:S(2)}) collective-permute-start(bf16[3,80,2048]{2,1,0:T(8,128)(2,1)} %slice.339), channel_id=1, source_target_pairs={{0,8},{4,12},{8,0},{12,4},{16,24},{20,28},{24,16},{28,20},{1,9},{5... | collective-permute-start | bytes 2949128 | tf_op jit(solution)/shard_map/ppermute | solution.py:343
  302.7 47.3 %collective-permute-start.31 = (bf16[3,80,2048]{2,1,0:T(8,128)(2,1)}, bf16[3,80,2048]{2,1,0:T(8,128)(2,1)}, u32[]{:S(2)}, u32[]{:S(2)}) collective-permute-start(bf16[3,80,2048]{2,1,0:T(8,128)(2,1)} %slice.338), channel_id=1, source_target_pairs={{0,16},{4,20},{8,24},{12,28},{16,0},{20,4},{24,8},{28,12},{1,17},{... | collective-permute-start | bytes 2949128 | tf_op jit(solution)/shard_map/ppermute | solution.py:343
  315.9 118.8 %all-gather.17.cloned.1.call-start = ((), (), s32[]{:S(2)}) async-start(), calls=%async_computation.10 | async-start | bytes 2621440 | tf_op jit(solution)/shard_map/all_gather | solution.py:156
  387.9 108.9 %reduce-scatter.6.cloned.1.call-start = ((), (), s32[]{:S(2)}) async-start(), calls=%async_computation.11 | async-start | bytes 2621440 | tf_op jit(solution)/shard_map/reduce_scatter | solution.py:160
  453.9 178.5 %reduce-scatter.8.cloned.1.call-start = ((), (), s32[]{:S(2)}) async-start(), calls=%async_computation.12 | async-start | bytes 17694720 | tf_op jit(solution)/shard_map/reduce_scatter | solution.py:676
  498.9 356.0 %reduce-scatter.12.cloned.1.call-start = ((), (), s32[]{:S(2)}) async-start(), calls=%async_computation.14 | async-start | bytes 5242880 | tf_op jit(solution)/shard_map/reduce_scatter | solution.py:628
  606.9 248.1 %reduce-scatter.10.cloned.1.call-start = ((), (), s32[]{:S(2)}) async-start(), calls=%async_computation.13 | async-start | bytes 5242880 | tf_op jit(solution)/shard_map/reduce_scatter | solution.py:628
  643.0 61.7 %collective-permute-start.58 = (bf16[3,160,2048]{2,1,0:T(8,128)(2,1)}, bf16[3,160,2048]{2,1,0:T(8,128)(2,1)}, u32[]{:S(2)}, u32[]{:S(2)}) collective-permute-start(bf16[3,160,2048]{2,1,0:T(8,128)(2,1)} %bitcast.64), channel_id=1, source_target_pairs={{1,5},{2,10},{3,15},{4,20},{5,17},{6,30},{7,27},{9,13},{10,2},{11,... | collective-permute-start | bytes 5898248 | tf_op jit(solution)/shard_map/ppermute | solution.py:111
  648.4 48.5 %collective-permute-start.56 = (bf16[64,2048]{1,0:T(8,128)(2,1)S(1)}, bf16[64,2048]{1,0:T(8,128)(2,1)S(1)}, u32[]{:S(2)}, u32[]{:S(2)}) collective-permute-start(bf16[64,2048]{1,0:T(8,128)(2,1)S(1)} %slice.444), channel_id=1, source_target_pairs={{0,8},{4,12},{8,0},{12,4},{16,24},{20,28},{24,16},{28,20},{1,9},{5... | collective-permute-start | bytes 786440 | tf_op jit(solution)/shard_map/ppermute | solution.py:343
  734.7 48.5 %collective-permute-start.68 = (bf16[1024,2048]{1,0:T(8,128)(2,1)}, bf16[1024,2048]{1,0:T(8,128)(2,1)}, u32[]{:S(2)}, u32[]{:S(2)}) collective-permute-start(bf16[1024,2048]{1,0:T(8,128)(2,1)} %add_convert_fusion.1), channel_id=1, source_target_pairs={{0,4},{4,0},{8,12},{12,8},{16,20},{20,16},{24,28},{28,24},{1,5},{5... | collective-permute-start | bytes 12582920 | tf_op jit(solution)/shard_map/ppermute | solution.py:343
  755.5 282.2 %reduce-scatter.14.cloned.1.call-start = ((), (), s32[]{:S(2)}) async-start(), calls=%async_computation.15 | async-start | bytes 2621440 | tf_op jit(solution)/shard_map/reduce_scatter | solution.py:160
  768.7 144.6 %collective-permute-start.61 = (bf16[3,160,2048]{2,1,0:T(8,128)(2,1)}, bf16[3,160,2048]{2,1,0:T(8,128)(2,1)}, u32[]{:S(2)}, u32[]{:S(2)}) collective-permute-start(bf16[3,160,2048]{2,1,0:T(8,128)(2,1)} %broadcast_select_fusion.3.refs_1_), channel_id=1, source_target_pairs={{0,16},{4,20},{8,24},{12,28},{16,0},{20,4},{24,8},{28,12},{1,17},{... | collective-permute-start | bytes 5898248 | tf_op jit(solution)/shard_map/ppermute | solution.py:343
  768.7 144.6 %collective-permute-start.60 = (bf16[3,160,2048]{2,1,0:T(8,128)(2,1)}, bf16[3,160,2048]{2,1,0:T(8,128)(2,1)}, u32[]{:S(2)}, u32[]{:S(2)}) collective-permute-start(bf16[3,160,2048]{2,1,0:T(8,128)(2,1)} %broadcast_select_fusion.3.refs_1_), channel_id=1, source_target_pairs={{0,8},{4,12},{8,0},{12,4},{16,24},{20,28},{24,16},{28,20},{1,9},{5... | collective-permute-start | bytes 5898248 | tf_op jit(solution)/shard_map/ppermute | solution.py:343
  779.8 49.3 %collective-permute-start.65 = (bf16[64,2048]{1,0:T(8,128)(2,1)S(1)}, bf16[64,2048]{1,0:T(8,128)(2,1)S(1)}, u32[]{:S(2)}, u32[]{:S(2)}) collective-permute-start(bf16[64,2048]{1,0:T(8,128)(2,1)S(1)} %fusion.99), channel_id=1, source_target_pairs={{0,16},{4,20},{8,24},{12,28},{16,0},{20,4},{24,8},{28,12},{1,17},{... | collective-permute-start | bytes 786440 | tf_op jit(solution)/shard_map/ppermute | solution.py:343
  787.5 54.3 %collective-permute-start.69 = (bf16[2,128,2048]{2,1,0:T(8,128)(2,1)S(1)}, bf16[2,128,2048]{2,1,0:T(8,128)(2,1)S(1)}, u32[]{:S(2)}, u32[]{:S(2)}) collective-permute-start(bf16[2,128,2048]{2,1,0:T(8,128)(2,1)S(1)} %slice_bitcast_fusion.4), channel_id=1, source_target_pairs={{0,8},{4,12},{8,0},{12,4},{16,24},{20,28},{24,16},{28,20},{1,9},{5... | collective-permute-start | bytes 3145736 | tf_op jit(solution)/shard_map/ppermute | solution.py:343
  856.8 56.1 %collective-permute-start.62 = (bf16[8,64,2048]{2,1,0:T(8,128)(2,1)S(1)}, bf16[8,64,2048]{2,1,0:T(8,128)(2,1)S(1)}, u32[]{:S(2)}, u32[]{:S(2)}) collective-permute-start(bf16[8,64,2048]{2,1,0:T(8,128)(2,1)S(1)} %pad_maximum_fusion.3), channel_id=1, source_target_pairs={{1,5},{2,10},{3,15},{4,20},{5,17},{6,30},{7,27},{9,13},{10,2},{11,... | collective-permute-start | bytes 6291464 | tf_op jit(solution)/shard_map/ppermute | solution.py:111
  977.8 46.7 %collective-permute-start.88 = (bf16[8,64,2048]{2,1,0:T(8,128)(2,1)S(1)}, bf16[8,64,2048]{2,1,0:T(8,128)(2,1)}, u32[]{:S(2)}, u32[]{:S(2)}) collective-permute-start(bf16[8,64,2048]{2,1,0:T(8,128)(2,1)S(1)} %broadcast_select_fusion.refs_1_), channel_id=1, source_target_pairs={{0,16},{4,20},{8,24},{12,28},{16,0},{20,4},{24,8},{28,12},{1,17},{... | collective-permute-start | bytes 6291464 | tf_op jit(solution)/shard_map/ppermute | solution.py:343
  979.5 46.3 %collective-permute-start.87 = (bf16[8,64,2048]{2,1,0:T(8,128)(2,1)S(1)}, bf16[8,64,2048]{2,1,0:T(8,128)(2,1)}, u32[]{:S(2)}, u32[]{:S(2)}) collective-permute-start(bf16[8,64,2048]{2,1,0:T(8,128)(2,1)S(1)} %broadcast_select_fusion.refs_1_), channel_id=1, source_target_pairs={{0,8},{4,12},{8,0},{12,4},{16,24},{20,28},{24,16},{28,20},{1,9},{5... | collective-permute-start | bytes 6291464 | tf_op jit(solution)/shard_map/ppermute | solution.py:343
  982.4 47.0 %collective-permute-start.78 = (bf16[128,2048]{1,0:T(8,128)(2,1)}, bf16[128,2048]{1,0:T(8,128)(2,1)}, u32[]{:S(2)}, u32[]{:S(2)}) collective-permute-start(bf16[128,2048]{1,0:T(8,128)(2,1)} %fusion.53), channel_id=1, source_target_pairs={{4,5},{8,10},{12,15},{16,17},{28,30},{24,27},{9,8},{1,2},{5,7},{29... | collective-permute-start | bytes 1572872 | tf_op jit(solution)/shard_map/ppermute | solution.py:111
  986.3 55.5 %collective-permute-start.80 = (bf16[256,2048]{1,0:T(8,128)(2,1)}, bf16[256,2048]{1,0:T(8,128)(2,1)}, u32[]{:S(2)}, u32[]{:S(2)}) collective-permute-start(bf16[256,2048]{1,0:T(8,128)(2,1)} %pad_maximum_fusion.8), channel_id=1, source_target_pairs={{4,5},{8,10},{12,15},{16,17},{28,30},{24,27},{9,8},{1,2},{5,7},{29... | collective-permute-start | bytes 3145736 | tf_op jit(solution)/shard_map/ppermute | solution.py:111
  989.1 93.2 %collective-permute-start.86 = (f32[3,2048]{1,0:T(4,128)S(1)}, f32[3,2048]{1,0:T(4,128)S(1)}, u32[]{:S(2)}, u32[]{:S(2)}) collective-permute-start(f32[3,2048]{1,0:T(4,128)S(1)} %add.396), channel_id=1, source_target_pairs={{0,16},{4,20},{8,24},{12,28},{16,0},{20,4},{24,8},{28,12},{1,17},{... | collective-permute-start | bytes 73736 | tf_op jit(solution)/shard_map/ppermute | solution.py:343
  1031.4 52.4 %collective-permute-start.79 = (bf16[128,2048]{1,0:T(8,128)(2,1)}, bf16[128,2048]{1,0:T(8,128)(2,1)}, u32[]{:S(2)}, u32[]{:S(2)}) collective-permute-start(bf16[128,2048]{1,0:T(8,128)(2,1)} %broadcast_select_fusion.8), channel_id=1, source_target_pairs={{5,1},{10,2},{15,3},{20,4},{17,5},{30,6},{27,7},{13,9},{2,10},{7,1... | collective-permute-start | bytes 1572872 | tf_op jit(solution)/shard_map/ppermute | solution.py:111
  1037.7 44.5 %collective-permute-start.94 = (bf16[8,32,2048]{2,1,0:T(8,128)(2,1)}, bf16[8,32,2048]{2,1,0:T(8,128)(2,1)}, u32[]{:S(2)}, u32[]{:S(2)}) collective-permute-start(bf16[8,32,2048]{2,1,0:T(8,128)(2,1)} %slice.391), channel_id=1, source_target_pairs={{0,16},{4,20},{8,24},{12,28},{16,0},{20,4},{24,8},{28,12},{1,17},{... | collective-permute-start | bytes 3145736 | tf_op jit(solution)/shard_map/ppermute | solution.py:343
  (198 other events, 3113.4 us)
Sparse Core Ops, SparseCore 0:
  46.0 61.7 all-gather.6
  145.1 44.4 all-gather.8
  223.2 53.9 all-gather.10
  282.3 26.9 all-gather.12
  316.0 43.6 all-gather.14
  388.0 46.5 all-gather.16
  454.0 42.7 reduce-scatter.5
  500.9 115.2 reduce-scatter.7
  619.0 77.1 reduce-scatter.11
  755.6 82.8 reduce-scatter.9
  945.0 74.0 reduce-scatter.13

commit v6 on v5

--- a/solution.py
+++ b/solution.py
@@ -568,7 +568,6 @@
     x = tokens_here.astype(jnp.float32)
     h1 = after(low(normed(x, gain[0])), info)
     rows_one = plane_gather(h1)
-    mlp_sides = side_pieces(after(mlp_shard, ws_q))
     ws_out, wc_q = narrow_full(after(jnp.stack([w_self_out, w_cross_q]), ws_q))
     wc_k, wc_v = narrow_full(after(w_cross_kv.swapaxes(0, 1), ws_out))
     (wc_out,) = narrow_full(after(w_cross_out[None], wc_k))
@@ -633,9 +632,7 @@
     sq, sk, sv = (project(rows_one, mat) for mat in (ws_q, ws_k, ws_v))
     self_result, self_lse = group_attend(sq, sk, sv, self_ok)
     self_heads = merge(self_result)
-    self_heads, mlp_sides, memory_here = lax.optimization_barrier(
-        (self_heads, mlp_sides, memory_here)
-    )
+    self_heads, memory_here = lax.optimization_barrier((self_heads, memory_here))
     x1 = x + spread_out([(self_heads, ws_out)])
     h2 = low(normed(x1, gain[1]))
     memory_all = plane_gather(after(memory_here, h2))
@@ -646,7 +643,7 @@
     cross_heads = merge(cross_result * valid_float[:, :, None, None])
     grad_y = cotangent_here.astype(jnp.float32) * local_weight[:, None]
     grad_mlp = row_gather(after(low(grad_y), wc_out))
-    mlp_chip = corner_pieces(lax.optimization_barrier((mlp_sides, memory_all[0]))[0])
+    mlp_chip = corner_pieces(side_pieces(after(mlp_shard, memory_all[0])))
     cross_heads, grad_mlp, mlp_chip = lax.optimization_barrier((cross_heads, grad_mlp, mlp_chip))
     x2 = x1 + spread_out([(cross_heads, wc_out)])
     h3 = low(normed(x2, gain[2]))
@@ -738,10 +735,9 @@
     grad_memory = unspread(memory_sums)
     mlp_pieces = core_pieces(mlp_chip)
     group_sides = side_pieces(group_here)
-    group_sides, mlp_pieces = lax.optimization_barrier((group_sides, mlp_pieces))
     mlp_totals = placed(mlp_pieces, spot_zero, ((0, 1), (2,)))
+    group_sides, mlp_totals = lax.optimization_barrier((group_sides, mlp_totals))
     group_chip = corner_pieces(group_sides)
-    group_chip, mlp_totals = lax.optimization_barrier((group_chip, mlp_totals))
     in_totals, *other_totals = placed(
         core_pieces(group_chip), spot_zero, ((0, 1, 2), (3,), (7,), (6, 5), (4,))
     )

time: 1150 us -> 1210 us (1.052)
  starting transfers between devices: 199 us -> 243 us
  waiting for transfers between devices: 454 us -> 486 us
    ppermute x2, starting transfers between devices: 0.18 us -> 32.3 us  [per_device(): gain_terms = gain_terms + lax.ppermute(gain_terms, 'narrow', pairs)]
    all_gather x4, waiting for transfers between devices: 1.61 us -> 30.2 us  [narrow_full(): lax.all_gather(stacked.reshape(kinds * rows, width), 'narrow', axis=0, ti...]
    ppermute x81, starting transfers between devices: 138 us -> 153 us  [flip(): return lax.ppermute(value, 'wide', [(i, i ^ bit) for i in range(PLANE)])]
    unnamed x275 -> x309, local copies, waits for them, and re-layouts: 35.4 us -> 38.7 us
  transfers between devices with their start and end apart: 112 -> 112, of which waited for: 57 -> 50; matrix products, arithmetic and copies ran while one was open for 31% -> 28% of each run, Pallas kernels for 4% -> 5%
where the time goes in v6:
time: 1210 us; the launch traced here: 1200 us
  waiting for transfers between devices  486 us (40%)
  starting transfers between devices  243 us (20%)
  matrix products  189 us (16%)
  local copies, waits for them, and re-layouts  130 us (11%)
  other arithmetic  68 us (6%)
  Pallas kernels  63.3 us (5%)
  between operations  18.3 us (2%)
    ppermute x81, waiting for transfers between devices, flip(): return lax.ppermute(value, 'wide', [(i, i ^ bit) for i in range(PLANE)])  323 us
    ppermute x81, starting transfers between devices, flip(): return lax.ppermute(value, 'wide', [(i, i ^ bit) for i in range(PLANE)])  153 us
    ppermute x18, waiting for transfers between devices, hop(): lax.ppermute(piece, ('wide', 'narrow'), [pair for pair in pairs if pair[0...  103 us
    dot_general x19, matrix products, matmul_nt(): lax.dot_general(a, b, (((1,), (1,)), ((), ())), preferred_element_type=jn...  68.3 us
    pallas_call x3, Pallas kernels, placed(): pl.pallas_call(body, grid_spec=pltpu.PrefetchScalarGridSpec(num_scalar_pr...  63.3 us
    ppermute x18, starting transfers between devices, hop(): lax.ppermute(piece, ('wide', 'narrow'), [pair for pair in pairs if pair[0...  55.5 us
    dot_general x19, matrix products, matmul_tn(): lax.dot_general(a, b, (((0,), (0,)), ((), ())), preferred_element_type=jn...  49.5 us
    unnamed x309, local copies, waits for them, and re-layouts  38.7 us
  transfers between devices with their start and end apart: 112, of which 50 were waited for; matrix products, arithmetic and copies ran while one was open for 28% of the time, Pallas kernels for 5%

profile of v6, /device:TPU:25, one launch (start us, length us, event | category | flops | bytes accessed | tf_op | source)
XLA Modules:
  0.0 1197.9 jit_solution(12715056864587041331)
XLA Ops:
  36.4 9.5 collective-permute-start.5
  47.6 10.2 collective-permute-start.8
  75.5 9.3 collective-permute-done.11
  85.7 21.6 %collective-permute-done.10 = bf16[256,2048]{1,0:T(8,128)(2,1)} collective-permute-done((bf16[256,2048]{1,0:T(8,128)(2,1)}, bf16[256,2048]{1,0:T(8,128)(2,1)}, u32[]{:S(2)}, u32[]{:S(2)}) %collective-permute-start.10) | collective-permute-done | bytes 1048608 | tf_op jit(solution)/shard_map/ppermute | solution.py:111
  113.3 12.1 %collective-permute-done.12 = bf16[256,2048]{1,0:T(8,128)(2,1)} collective-permute-done((bf16[256,2048]{1,0:T(8,128)(2,1)}, bf16[256,2048]{1,0:T(8,128)(2,1)}, u32[]{:S(2)}, u32[]{:S(2)}) %collective-permute-start.12) | collective-permute-done | bytes 1048608 | tf_op jit(solution)/shard_map/ppermute | solution.py:111
  157.4 30.1 %all-gather.9.cloned.1.call-done = bf16[4,128,2048]{2,1,0:T(8,128)(2,1)} async-done(((bf16[1,128,2048]{2,1,0:T(8,128)(2,1)}), bf16[4,128,2048]{2,1,0:T(8,128)(2,1)}) %all-gather.9.cloned.1.call-update) | async-done | bytes 2097168 | tf_op jit(solution)/shard_map/all_gather | solution.py:447
  201.5 8.0 collective-permute-done.14
  227.7 25.2 %collective-permute-done.24 = bf16[128,2048]{1,0:T(8,128)(2,1)S(1)} collective-permute-done((bf16[128,2048]{1,0:T(8,128)(2,1)}, bf16[128,2048]{1,0:T(8,128)(2,1)S(1)}, u32[]{:S(2)}, u32[]{:S(2)}) %collective-permute-start.24) | collective-permute-done | bytes 524320 | tf_op jit(solution)/shard_map/ppermute | solution.py:343
  313.2 11.2 collective-permute-done.30.refs_3_
  370.8 12.3 %collective-permute-done.34 = bf16[2,64,2048]{2,1,0:T(8,128)(2,1)S(1)} collective-permute-done((bf16[2,64,2048]{2,1,0:T(8,128)(2,1)S(1)}, bf16[2,64,2048]{2,1,0:T(8,128)(2,1)S(1)}, u32[]{:S(2)}, u32[]{:S(2)}) %collective-permute-start.34) | collective-permute-done | bytes 524320 | tf_op jit(solution)/shard_map/ppermute | solution.py:343
  396.8 9.3 collective-permute-done.41.refs_9_
  409.7 18.6 %place.3 = (bf16[1280,2048]{1,0:T(8,128)(2,1)}, bf16[1280,2048]{1,0:T(8,128)(2,1)}, bf16[1280,2048]{1,0:T(8,128)(2,1)}) custom-call(s32[8]{0:T(128)} %broadcast_xor_fusion.1.refs_0_, bf16[3,160,2048]{2,1,0:T(8,128)(2,1)} %pad_maximum_fusion.4.refs_1_, bf16[3,160,2048]{2,1,0:T(8,128)(2,1)} %collective-permute-done.29.refs_2_, ...), custom_call_target="tpu_custom_call" | custom-call | bytes 31457280 | tf_op jit(solution)/shard_map/place/pallas_call | solution.py:522
  428.3 7.5 fusion.146
  476.7 23.2 %reduce-scatter.6.cloned.1.call-done = bf16[128,2048]{1,0:T(8,128)(2,1)} async-done(((bf16[512,2048]{1,0:T(8,128)(2,1)}), bf16[128,2048]{1,0:T(8,128)(2,1)}) %reduce-scatter.6.cloned.1.call-update) | async-done | bytes 524304 | tf_op jit(solution)/shard_map/reduce_scatter | solution.py:160
  507.2 11.0 collective-permute-done.44
  610.9 12.9 %collective-permute-done.49 = bf16[2,64,2048]{2,1,0:T(8,128)(2,1)} collective-permute-done((bf16[2,64,2048]{2,1,0:T(8,128)(2,1)S(1)}, bf16[2,64,2048]{2,1,0:T(8,128)(2,1)}, u32[]{:S(2)}, u32[]{:S(2)}) %collective-permute-start.49) | collective-permute-done | bytes 524320 | tf_op jit(solution)/shard_map/ppermute | solution.py:343
  652.3 9.7 collective-permute-done.55
  662.8 35.0 %collective-permute-done.56 = bf16[64,2048]{1,0:T(8,128)(2,1)S(1)} collective-permute-done((bf16[64,2048]{1,0:T(8,128)(2,1)S(1)}, bf16[64,2048]{1,0:T(8,128)(2,1)S(1)}, u32[]{:S(2)}, u32[]{:S(2)}) %collective-permute-start.56) | collective-permute-done | bytes 262176 | tf_op jit(solution)/shard_map/ppermute | solution.py:343
  787.3 31.7 %collective-permute-done.67 = bf16[64,2048]{1,0:T(8,128)(2,1)S(1)} collective-permute-done((bf16[64,2048]{1,0:T(8,128)(2,1)S(1)}, bf16[64,2048]{1,0:T(8,128)(2,1)S(1)}, u32[]{:S(2)}, u32[]{:S(2)}) %collective-permute-start.67) | collective-permute-done | bytes 262176 | tf_op jit(solution)/shard_map/ppermute | solution.py:343
  819.1 9.5 collective-permute-start.71
  829.2 12.3 %collective-permute-done.69 = bf16[2,128,2048]{2,1,0:T(8,128)(2,1)S(1)} collective-permute-done((bf16[2,128,2048]{2,1,0:T(8,128)(2,1)S(1)}, bf16[2,128,2048]{2,1,0:T(8,128)(2,1)S(1)}, u32[]{:S(2)}, u32[]{:S(2)}) %collective-permute-start.69) | collective-permute-done | bytes 1048608 | tf_op jit(solution)/shard_map/ppermute | solution.py:343
  841.4 8.1 collective-permute-done.71
  865.1 20.5 %collective-permute-done.70 = bf16[128,2048]{1,0:T(8,128)(2,1)S(1)} collective-permute-done((bf16[128,2048]{1,0:T(8,128)(2,1)S(1)}, bf16[128,2048]{1,0:T(8,128)(2,1)S(1)}, u32[]{:S(2)}, u32[]{:S(2)}) %collective-permute-start.70) | collective-permute-done | bytes 524320 | tf_op jit(solution)/shard_map/ppermute | solution.py:343
  886.8 24.4 %collective-permute-done.62 = bf16[8,64,2048]{2,1,0:T(8,128)(2,1)S(1)} collective-permute-done((bf16[8,64,2048]{2,1,0:T(8,128)(2,1)S(1)}, bf16[8,64,2048]{2,1,0:T(8,128)(2,1)S(1)}, u32[]{:S(2)}, u32[]{:S(2)}) %collective-permute-start.62) | collective-permute-done | bytes 2097184 | tf_op jit(solution)/shard_map/ppermute | solution.py:111
  925.7 13.3 %collective-permute-done.75 = bf16[8,64,2048]{2,1,0:T(8,128)(2,1)} collective-permute-done((bf16[8,64,2048]{2,1,0:T(8,128)(2,1)S(1)}, bf16[8,64,2048]{2,1,0:T(8,128)(2,1)}, u32[]{:S(2)}, u32[]{:S(2)}) %collective-permute-start.75) | collective-permute-done | bytes 2097184 | tf_op jit(solution)/shard_map/ppermute | solution.py:111
  946.3 29.9 %collective-permute-start.82 = (f32[3,2048]{1,0:T(4,128)S(1)}, f32[3,2048]{1,0:T(4,128)S(1)}, u32[]{:S(2)}, u32[]{:S(2)}) collective-permute-start(f32[3,2048]{1,0:T(4,128)S(1)} %pad_maximum_fusion.15), channel_id=1, source_target_pairs={{0,1},{1,0},{2,3},{3,2},{4,5},{5,4},{6,7},{7,6},{8,9},{9,8},{10,11... | collective-permute-start | bytes 73736 | tf_op jit(solution)/shard_map/ppermute | solution.py:722
  981.9 48.5 %collective-permute-start.87 = (bf16[8,64,2048]{2,1,0:T(8,128)(2,1)S(1)}, bf16[8,64,2048]{2,1,0:T(8,128)(2,1)}, u32[]{:S(2)}, u32[]{:S(2)}) collective-permute-start(bf16[8,64,2048]{2,1,0:T(8,128)(2,1)S(1)} %broadcast_select_fusion.refs_1_), channel_id=1, source_target_pairs={{0,8},{4,12},{8,0},{12,4},{16,24},{20,28},{24,16},{28,20},{1,9},{5... | collective-permute-start | bytes 6291464 | tf_op jit(solution)/shard_map/ppermute | solution.py:343
  1039.7 22.1 %place.4 = (f32[1280,2,2048]{2,1,0:T(2,128)}, f32[1280,2048]{1,0:T(8,128)}) custom-call(s32[8]{0:T(128)} %broadcast_xor_fusion.refs_0_, bf16[3,160,2048]{2,1,0:T(8,128)(2,1)} %broadcast_select_fusion.3.refs_1_, bf16[3,160,2048]{2,1,0:T(8,128)(2,1)} %collective-permute-done.60.refs_2_, bf16[3,160,2048]{2,1,0:T(8,128)(2,1)} %collective-permute-done.61.refs_3_, ...), custom_call_target="tpu_custom_call" | custom-call | bytes 47185920 | tf_op jit(solution)/shard_map/place/pallas_call | solution.py:522
  1061.7 14.1 %collective-permute-done.87.refs_2_ = bf16[8,64,2048]{2,1,0:T(8,128)(2,1)} collective-permute-done((bf16[8,64,2048]{2,1,0:T(8,128)(2,1)S(1)}, bf16[8,64,2048]{2,1,0:T(8,128)(2,1)}, u32[]{:S(2)}, u32[]{:S(2)}) %collective-permute-start.87) | collective-permute-done | bytes 2097184 | tf_op jit(solution)/shard_map/ppermute | solution.py:343
  1090.1 42.2 %collective-permute-done.85 = f32[3,2048]{1,0:T(4,128)S(1)} collective-permute-done((f32[3,2048]{1,0:T(4,128)S(1)}, f32[3,2048]{1,0:T(4,128)S(1)}, u32[]{:S(2)}, u32[]{:S(2)}) %collective-permute-start.85) | collective-permute-done | bytes 24608 | tf_op jit(solution)/shard_map/ppermute | solution.py:343
  1144.4 13.5 %collective-permute-done.76 = bf16[128,2048]{1,0:T(8,128)(2,1)} collective-permute-done((bf16[128,2048]{1,0:T(8,128)(2,1)}, bf16[128,2048]{1,0:T(8,128)(2,1)}, u32[]{:S(2)}, u32[]{:S(2)}) %collective-permute-start.76) | collective-permute-done | bytes 524320 | tf_op jit(solution)/shard_map/ppermute | solution.py:111
  1167.6 22.7 %place.5 = (f32[3,512,2048]{2,1,0:T(8,128)}, f32[512,2048]{1,0:T(8,128)}, f32[512,2048]{1,0:T(8,128)}, f32[512,2,2048]{2,1,0:T(2,128)}, f32[512,2048]{1,0:T(8,128)}) custom-call(s32[8]{0:T(128)} %broadcast_xor_fusion.refs_0_, bf16[8,64,2048]{2,1,0:T(8,128)(2,1)} %copy-done.25, bf16[8,64,2048]{2,1,0:T(8,128)(2,1)} %collective-permute-done.87.refs_2_, ...), custom_call_target="tpu_custom_call" | custom-call | bytes 50331648 | tf_op jit(solution)/shard_map/place/pallas_call | solution.py:522
  (778 shorter events, 590.1 us)
Async XLA Ops:
  7.2 120.6 %all-gather.7.cloned.1.call-start = ((), (), s32[]{:S(2)}) async-start(), calls=%async_computation.5 | async-start | bytes 3932160 | tf_op jit(solution)/shard_map/all_gather | solution.py:447
  45.9 141.7 %all-gather.9.cloned.1.call-start = ((), (), s32[]{:S(2)}) async-start(), calls=%async_computation.6 | async-start | bytes 2621440 | tf_op jit(solution)/shard_map/all_gather | solution.py:447
  131.4 147.0 %all-gather.11.cloned.1.call-start = ((), (), s32[]{:S(2)}) async-start(), calls=%async_computation.7 | async-start | bytes 2621440 | tf_op jit(solution)/shard_map/all_gather | solution.py:447
  221.0 89.2 %all-gather.13.cloned.1.call-start = ((), (), s32[]{:S(2)}) async-start(), calls=%async_computation.8 | async-start | bytes 1310720 | tf_op jit(solution)/shard_map/all_gather | solution.py:447
  223.8 53.7 %collective-permute-start.28 = (bf16[128,2048]{1,0:T(8,128)(2,1)}, bf16[128,2048]{1,0:T(8,128)(2,1)S(1)}, u32[]{:S(2)}, u32[]{:S(2)}) collective-permute-start(bf16[128,2048]{1,0:T(8,128)(2,1)} %broadcast_select_fusion.13), channel_id=1, source_target_pairs={{5,4},{10,8},{15,12},{17,16},{30,28},{27,24},{8,9},{2,1},{7,5},{28... | collective-permute-start | bytes 1572872 | tf_op jit(solution)/shard_map/ppermute | solution.py:111
  272.0 59.1 %collective-permute-start.22 = (bf16[1024,2048]{1,0:T(8,128)(2,1)}, bf16[1024,2048]{1,0:T(8,128)(2,1)}, u32[]{:S(2)}, u32[]{:S(2)}) collective-permute-start(bf16[1024,2048]{1,0:T(8,128)(2,1)} %constant_dynamic-update-slice_fusion.5), channel_id=1, source_target_pairs={{0,4},{4,0},{8,12},{12,8},{16,20},{20,16},{24,28},{28,24},{1,5},{5... | collective-permute-start | bytes 12582920 | tf_op jit(solution)/shard_map/ppermute | solution.py:343
  280.1 82.5 %all-gather.15.cloned.1.call-start = ((), (), s32[]{:S(2)}) async-start(), calls=%async_computation.9 | async-start | bytes 2621440 | tf_op jit(solution)/shard_map/all_gather | solution.py:156
  310.3 127.5 %all-gather.17.cloned.1.call-start = ((), (), s32[]{:S(2)}) async-start(), calls=%async_computation.10 | async-start | bytes 2621440 | tf_op jit(solution)/shard_map/all_gather | solution.py:156
  392.3 107.5 %reduce-scatter.6.cloned.1.call-start = ((), (), s32[]{:S(2)}) async-start(), calls=%async_computation.11 | async-start | bytes 2621440 | tf_op jit(solution)/shard_map/reduce_scatter | solution.py:160
  456.9 177.5 %reduce-scatter.8.cloned.1.call-start = ((), (), s32[]{:S(2)}) async-start(), calls=%async_computation.12 | async-start | bytes 17694720 | tf_op jit(solution)/shard_map/reduce_scatter | solution.py:673
  502.0 351.6 %reduce-scatter.12.cloned.1.call-start = ((), (), s32[]{:S(2)}) async-start(), calls=%async_computation.14 | async-start | bytes 5242880 | tf_op jit(solution)/shard_map/reduce_scatter | solution.py:627
  605.2 248.4 %reduce-scatter.10.cloned.1.call-start = ((), (), s32[]{:S(2)}) async-start(), calls=%async_computation.13 | async-start | bytes 5242880 | tf_op jit(solution)/shard_map/reduce_scatter | solution.py:627
  643.5 62.1 %collective-permute-start.58 = (bf16[3,160,2048]{2,1,0:T(8,128)(2,1)}, bf16[3,160,2048]{2,1,0:T(8,128)(2,1)}, u32[]{:S(2)}, u32[]{:S(2)}) collective-permute-start(bf16[3,160,2048]{2,1,0:T(8,128)(2,1)} %bitcast.64), channel_id=1, source_target_pairs={{1,5},{2,10},{3,15},{4,20},{5,17},{6,30},{7,27},{9,13},{10,2},{11,... | collective-permute-start | bytes 5898248 | tf_op jit(solution)/shard_map/ppermute | solution.py:111
  649.0 48.8 %collective-permute-start.56 = (bf16[64,2048]{1,0:T(8,128)(2,1)S(1)}, bf16[64,2048]{1,0:T(8,128)(2,1)S(1)}, u32[]{:S(2)}, u32[]{:S(2)}) collective-permute-start(bf16[64,2048]{1,0:T(8,128)(2,1)S(1)} %slice.446), channel_id=1, source_target_pairs={{0,8},{4,12},{8,0},{12,4},{16,24},{20,28},{24,16},{28,20},{1,9},{5... | collective-permute-start | bytes 786440 | tf_op jit(solution)/shard_map/ppermute | solution.py:343
  731.9 50.9 %collective-permute-start.68 = (bf16[1024,2048]{1,0:T(8,128)(2,1)}, bf16[1024,2048]{1,0:T(8,128)(2,1)}, u32[]{:S(2)}, u32[]{:S(2)}) collective-permute-start(bf16[1024,2048]{1,0:T(8,128)(2,1)} %add_convert_fusion.1), channel_id=1, source_target_pairs={{0,4},{4,0},{8,12},{12,8},{16,20},{20,16},{24,28},{28,24},{1,5},{5... | collective-permute-start | bytes 12582920 | tf_op jit(solution)/shard_map/ppermute | solution.py:343
  752.6 387.0 %reduce-scatter.14.cloned.1.call-start = ((), (), s32[]{:S(2)}) async-start(), calls=%async_computation.15 | async-start | bytes 2621440 | tf_op jit(solution)/shard_map/reduce_scatter | solution.py:160
  768.2 143.3 %collective-permute-start.61 = (bf16[3,160,2048]{2,1,0:T(8,128)(2,1)}, bf16[3,160,2048]{2,1,0:T(8,128)(2,1)}, u32[]{:S(2)}, u32[]{:S(2)}) collective-permute-start(bf16[3,160,2048]{2,1,0:T(8,128)(2,1)} %broadcast_select_fusion.3.refs_1_), channel_id=1, source_target_pairs={{0,16},{4,20},{8,24},{12,28},{16,0},{20,4},{24,8},{28,12},{1,17},{... | collective-permute-start | bytes 5898248 | tf_op jit(solution)/shard_map/ppermute | solution.py:343
  768.2 143.3 %collective-permute-start.60 = (bf16[3,160,2048]{2,1,0:T(8,128)(2,1)}, bf16[3,160,2048]{2,1,0:T(8,128)(2,1)}, u32[]{:S(2)}, u32[]{:S(2)}) collective-permute-start(bf16[3,160,2048]{2,1,0:T(8,128)(2,1)} %broadcast_select_fusion.3.refs_1_), channel_id=1, source_target_pairs={{0,8},{4,12},{8,0},{12,4},{16,24},{20,28},{24,16},{28,20},{1,9},{5... | collective-permute-start | bytes 5898248 | tf_op jit(solution)/shard_map/ppermute | solution.py:343
  779.0 49.7 %collective-permute-start.65 = (bf16[64,2048]{1,0:T(8,128)(2,1)S(1)}, bf16[64,2048]{1,0:T(8,128)(2,1)S(1)}, u32[]{:S(2)}, u32[]{:S(2)}) collective-permute-start(bf16[64,2048]{1,0:T(8,128)(2,1)S(1)} %fusion.99), channel_id=1, source_target_pairs={{0,16},{4,20},{8,24},{12,28},{16,0},{20,4},{24,8},{28,12},{1,17},{... | collective-permute-start | bytes 786440 | tf_op jit(solution)/shard_map/ppermute | solution.py:343
  787.0 54.4 %collective-permute-start.69 = (bf16[2,128,2048]{2,1,0:T(8,128)(2,1)S(1)}, bf16[2,128,2048]{2,1,0:T(8,128)(2,1)S(1)}, u32[]{:S(2)}, u32[]{:S(2)}) collective-permute-start(bf16[2,128,2048]{2,1,0:T(8,128)(2,1)S(1)} %slice_bitcast_fusion.4), channel_id=1, source_target_pairs={{0,8},{4,12},{8,0},{12,4},{16,24},{20,28},{24,16},{28,20},{1,9},{5... | collective-permute-start | bytes 3145736 | tf_op jit(solution)/shard_map/ppermute | solution.py:343
  855.5 55.8 %collective-permute-start.62 = (bf16[8,64,2048]{2,1,0:T(8,128)(2,1)S(1)}, bf16[8,64,2048]{2,1,0:T(8,128)(2,1)S(1)}, u32[]{:S(2)}, u32[]{:S(2)}) collective-permute-start(bf16[8,64,2048]{2,1,0:T(8,128)(2,1)S(1)} %pad_maximum_fusion.3), channel_id=1, source_target_pairs={{1,5},{2,10},{3,15},{4,20},{5,17},{6,30},{7,27},{9,13},{10,2},{11,... | collective-permute-start | bytes 6291464 | tf_op jit(solution)/shard_map/ppermute | solution.py:111
  945.7 84.8 %collective-permute-start.93 = (bf16[3,80,2048]{2,1,0:T(8,128)(2,1)}, bf16[3,80,2048]{2,1,0:T(8,128)(2,1)}, u32[]{:S(2)}, u32[]{:S(2)}) collective-permute-start(bf16[3,80,2048]{2,1,0:T(8,128)(2,1)} %collective-permute-done.74.refs_5_), channel_id=1, source_target_pairs={{0,4},{4,0},{8,12},{12,8},{16,20},{20,16},{24,28},{28,24},{1,5},{5... | collective-permute-start | bytes 2949128 | tf_op jit(solution)/shard_map/ppermute | solution.py:343
  946.2 85.8 %collective-permute-start.89 = (bf16[3,160,2048]{2,1,0:T(8,128)(2,1)}, bf16[3,160,2048]{2,1,0:T(8,128)(2,1)}, u32[]{:S(2)}, u32[]{:S(2)}) collective-permute-start(bf16[3,160,2048]{2,1,0:T(8,128)(2,1)} %broadcast_select_fusion.3.refs_1_), channel_id=1, source_target_pairs={{0,4},{4,0},{8,12},{12,8},{16,20},{20,16},{24,28},{28,24},{1,5},{5... | collective-permute-start | bytes 5898248 | tf_op jit(solution)/shard_map/ppermute | solution.py:343
  979.9 55.4 %collective-permute-start.90 = (bf16[3,160,2048]{2,1,0:T(8,128)(2,1)}, bf16[3,160,2048]{2,1,0:T(8,128)(2,1)}, u32[]{:S(2)}, u32[]{:S(2)}) collective-permute-start(bf16[3,160,2048]{2,1,0:T(8,128)(2,1)} %collective-permute-done.60.refs_2_), channel_id=1, source_target_pairs={{0,4},{4,0},{8,12},{12,8},{16,20},{20,16},{24,28},{28,24},{1,5},{5... | collective-permute-start | bytes 5898248 | tf_op jit(solution)/shard_map/ppermute | solution.py:343
  980.0 81.7 %collective-permute-start.88 = (bf16[8,64,2048]{2,1,0:T(8,128)(2,1)S(1)}, bf16[8,64,2048]{2,1,0:T(8,128)(2,1)}, u32[]{:S(2)}, u32[]{:S(2)}) collective-permute-start(bf16[8,64,2048]{2,1,0:T(8,128)(2,1)S(1)} %broadcast_select_fusion.refs_1_), channel_id=1, source_target_pairs={{0,16},{4,20},{8,24},{12,28},{16,0},{20,4},{24,8},{28,12},{1,17},{... | collective-permute-start | bytes 6291464 | tf_op jit(solution)/shard_map/ppermute | solution.py:343
  981.9 93.9 %collective-permute-start.87 = (bf16[8,64,2048]{2,1,0:T(8,128)(2,1)S(1)}, bf16[8,64,2048]{2,1,0:T(8,128)(2,1)}, u32[]{:S(2)}, u32[]{:S(2)}) collective-permute-start(bf16[8,64,2048]{2,1,0:T(8,128)(2,1)S(1)} %broadcast_select_fusion.refs_1_), channel_id=1, source_target_pairs={{0,8},{4,12},{8,0},{12,4},{16,24},{20,28},{24,16},{28,20},{1,9},{5... | collective-permute-start | bytes 6291464 | tf_op jit(solution)/shard_map/ppermute | solution.py:343
  1032.0 47.4 %collective-permute-start.78 = (bf16[128,2048]{1,0:T(8,128)(2,1)}, bf16[128,2048]{1,0:T(8,128)(2,1)S(1)}, u32[]{:S(2)}, u32[]{:S(2)}) collective-permute-start(bf16[128,2048]{1,0:T(8,128)(2,1)} %fusion.53), channel_id=1, source_target_pairs={{4,5},{8,10},{12,15},{16,17},{28,30},{24,27},{9,8},{1,2},{5,7},{29... | collective-permute-start | bytes 1572872 | tf_op jit(solution)/shard_map/ppermute | solution.py:111
  1035.3 102.7 %collective-permute-start.81 = (bf16[256,2048]{1,0:T(8,128)(2,1)S(1)}, bf16[256,2048]{1,0:T(8,128)(2,1)S(1)}, u32[]{:S(2)}, u32[]{:S(2)}) collective-permute-start(bf16[256,2048]{1,0:T(8,128)(2,1)S(1)} %broadcast_select_fusion.4), channel_id=1, source_target_pairs={{5,1},{10,2},{15,3},{20,4},{17,5},{30,6},{27,7},{13,9},{2,10},{7,1... | collective-permute-start | bytes 3145736 | tf_op jit(solution)/shard_map/ppermute | solution.py:111
  1037.2 49.9 %collective-permute-start.83 = (f32[3,2048]{1,0:T(4,128)S(1)}, f32[3,2048]{1,0:T(4,128)S(1)}, u32[]{:S(2)}, u32[]{:S(2)}) collective-permute-start(f32[3,2048]{1,0:T(4,128)S(1)} %fusion.126), channel_id=1, source_target_pairs={{0,2},{1,3},{2,0},{3,1},{4,6},{5,7},{6,4},{7,5},{8,10},{9,11},{10,... | collective-permute-start | bytes 73736 | tf_op jit(solution)/shard_map/ppermute | solution.py:722
  1078.1 63.5 %collective-permute-start.95 = (bf16[8,32,2048]{2,1,0:T(8,128)(2,1)}, bf16[8,32,2048]{2,1,0:T(8,128)(2,1)}, u32[]{:S(2)}, u32[]{:S(2)}) collective-permute-start(bf16[8,32,2048]{2,1,0:T(8,128)(2,1)} %slice.392), channel_id=1, source_target_pairs={{0,8},{4,12},{8,0},{12,4},{16,24},{20,28},{24,16},{28,20},{1,9},{5... | collective-permute-start | bytes 3145736 | tf_op jit(solution)/shard_map/ppermute | solution.py:343
  1079.4 58.5 %collective-permute-start.79 = (bf16[128,2048]{1,0:T(8,128)(2,1)S(1)}, bf16[128,2048]{1,0:T(8,128)(2,1)S(1)}, u32[]{:S(2)}, u32[]{:S(2)}) collective-permute-start(bf16[128,2048]{1,0:T(8,128)(2,1)S(1)} %broadcast_select_fusion.8), channel_id=1, source_target_pairs={{5,1},{10,2},{15,3},{20,4},{17,5},{30,6},{27,7},{13,9},{2,10},{7,1... | collective-permute-start | bytes 1572872 | tf_op jit(solution)/shard_map/ppermute | solution.py:111
  1086.4 57.3 %collective-permute-start.94 = (bf16[8,32,2048]{2,1,0:T(8,128)(2,1)}, bf16[8,32,2048]{2,1,0:T(8,128)(2,1)}, u32[]{:S(2)}, u32[]{:S(2)}) collective-permute-start(bf16[8,32,2048]{2,1,0:T(8,128)(2,1)} %slice.391), channel_id=1, source_target_pairs={{0,16},{4,20},{8,24},{12,28},{16,0},{20,4},{24,8},{28,12},{1,17},{... | collective-permute-start | bytes 3145736 | tf_op jit(solution)/shard_map/ppermute | solution.py:343
  (215 other events, 3760.9 us)
Sparse Core Ops, SparseCore 0:
  46.0 61.7 all-gather.6
  131.5 56.0 all-gather.8
  221.2 54.2 all-gather.10
  280.2 26.8 all-gather.12
  310.4 43.5 all-gather.14
  392.5 45.2 all-gather.16
  457.0 42.7 reduce-scatter.5
  503.9 120.3 reduce-scatter.7
  627.2 77.0 reduce-scatter.11
  752.8 86.6 reduce-scatter.9
  943.6 67.2 reduce-scatter.13

commit v7 on v5

--- a/solution.py
+++ b/solution.py
@@ -741,7 +741,6 @@
     group_sides, mlp_pieces = lax.optimization_barrier((group_sides, mlp_pieces))
     mlp_totals = placed(mlp_pieces, spot_zero, ((0, 1), (2,)))
     group_chip = corner_pieces(group_sides)
-    group_chip, mlp_totals = lax.optimization_barrier((group_chip, mlp_totals))
     in_totals, *other_totals = placed(
         core_pieces(group_chip), spot_zero, ((0, 1, 2), (3,), (7,), (6, 5), (4,))
     )

time: 1150 us -> 1220 us (1.061)
  starting transfers between devices: 199 us -> 248 us
  waiting for transfers between devices: 454 us -> 480 us
    ppermute x2, starting transfers between devices: 0.18 us -> 33.7 us  [per_device(): gain_terms = gain_terms + lax.ppermute(gain_terms, 'narrow', pairs)]
    ppermute x81, waiting for transfers between devices: 312 us -> 339 us  [flip(): return lax.ppermute(value, 'wide', [(i, i ^ bit) for i in range(PLANE)])]
    unnamed x275 -> x293, local copies, waits for them, and re-layouts: 35.4 us -> 38 us
  transfers between devices with their start and end apart: 112 -> 112, of which waited for: 57 -> 53; matrix products, arithmetic and copies ran while one was open for 31% -> 29% of each run, Pallas kernels for 4% -> 5%
where the time goes in v7:
time: 1220 us; the launch traced here: 1210 us
  waiting for transfers between devices  480 us (39%)
  starting transfers between devices  248 us (20%)
  matrix products  197 us (16%)
  local copies, waits for them, and re-layouts  132 us (11%)
  other arithmetic  70.1 us (6%)
  Pallas kernels  63.3 us (5%)
  between operations  18.2 us (1%)
    ppermute x81, waiting for transfers between devices, flip(): return lax.ppermute(value, 'wide', [(i, i ^ bit) for i in range(PLANE)])  339 us
    ppermute x81, starting transfers between devices, flip(): return lax.ppermute(value, 'wide', [(i, i ^ bit) for i in range(PLANE)])  146 us
    ppermute x18, waiting for transfers between devices, hop(): lax.ppermute(piece, ('wide', 'narrow'), [pair for pair in pairs if pair[0...  102 us
    dot_general x19, matrix products, matmul_nt(): lax.dot_general(a, b, (((1,), (1,)), ((), ())), preferred_element_type=jn...  68.9 us
    ppermute x18, starting transfers between devices, hop(): lax.ppermute(piece, ('wide', 'narrow'), [pair for pair in pairs if pair[0...  66.9 us
    pallas_call x3, Pallas kernels, placed(): pl.pallas_call(body, grid_spec=pltpu.PrefetchScalarGridSpec(num_scalar_pr...  63.3 us
    dot_general x19, matrix products, matmul_tn(): lax.dot_general(a, b, (((0,), (0,)), ((), ())), preferred_element_type=jn...  50 us
    dot_general x19, matrix products, matmul_nn(): lax.dot_general(a, b, (((1,), (0,)), ((), ())), preferred_element_type=jn...  43.4 us
  transfers between devices with their start and end apart: 112, of which 53 were waited for; matrix products, arithmetic and copies ran while one was open for 29% of the time, Pallas kernels for 5%

profile of v7, /device:TPU:25, one launch (start us, length us, event | category | flops | bytes accessed | tf_op | source)
XLA Modules:
  0.0 1208.6 jit_solution(3867445311450747323)
XLA Ops:
  36.4 9.5 collective-permute-start.5
  47.6 10.2 collective-permute-start.8
  85.7 21.6 %collective-permute-done.10 = bf16[256,2048]{1,0:T(8,128)(2,1)} collective-permute-done((bf16[256,2048]{1,0:T(8,128)(2,1)}, bf16[256,2048]{1,0:T(8,128)(2,1)}, u32[]{:S(2)}, u32[]{:S(2)}) %collective-permute-start.10) | collective-permute-done | bytes 1048608 | tf_op jit(solution)/shard_map/ppermute | solution.py:111
  113.9 11.5 collective-permute-done.14
  131.4 13.5 %collective-permute-start.12 = (bf16[3,160,2048]{2,1,0:T(8,128)(2,1)}, bf16[3,160,2048]{2,1,0:T(8,128)(2,1)}, u32[]{:S(2)}, u32[]{:S(2)}) collective-permute-start(bf16[3,160,2048]{2,1,0:T(8,128)(2,1)} %pad_maximum_fusion.4.refs_1_), channel_id=1, source_target_pairs={{0,8},{4,12},{8,0},{12,4},{16,24},{20,28},{24,16},{28,20},{1,9},{5... | collective-permute-start | bytes 5898248 | tf_op jit(solution)/shard_map/ppermute | solution.py:343
  174.6 13.4 %collective-permute-done.12.refs_2_ = bf16[3,160,2048]{2,1,0:T(8,128)(2,1)} collective-permute-done((bf16[3,160,2048]{2,1,0:T(8,128)(2,1)}, bf16[3,160,2048]{2,1,0:T(8,128)(2,1)}, u32[]{:S(2)}, u32[]{:S(2)}) %collective-permute-start.12) | collective-permute-done | bytes 1966112 | tf_op jit(solution)/shard_map/ppermute | solution.py:343
  201.6 9.9 collective-permute-done.16
  230.0 25.0 %collective-permute-done.26 = bf16[128,2048]{1,0:T(8,128)(2,1)S(1)} collective-permute-done((bf16[128,2048]{1,0:T(8,128)(2,1)}, bf16[128,2048]{1,0:T(8,128)(2,1)S(1)}, u32[]{:S(2)}, u32[]{:S(2)}) %collective-permute-start.26) | collective-permute-done | bytes 524320 | tf_op jit(solution)/shard_map/ppermute | solution.py:343
  349.9 9.8 all-gather.15.cloned.1.call-done
  367.9 11.0 collective-permute-done.34
  392.4 9.3 collective-permute-done.41.refs_9_
  405.4 18.5 %place.3 = (bf16[1280,2048]{1,0:T(8,128)(2,1)}, bf16[1280,2048]{1,0:T(8,128)(2,1)}, bf16[1280,2048]{1,0:T(8,128)(2,1)}) custom-call(s32[8]{0:T(128)} %broadcast_xor_fusion.1.refs_0_, bf16[3,160,2048]{2,1,0:T(8,128)(2,1)} %pad_maximum_fusion.4.refs_1_, bf16[3,160,2048]{2,1,0:T(8,128)(2,1)} %collective-permute-done.12.refs_2_, ...), custom_call_target="tpu_custom_call" | custom-call | bytes 31457280 | tf_op jit(solution)/shard_map/place/pallas_call | solution.py:522
  473.7 23.2 %reduce-scatter.6.cloned.1.call-done = bf16[128,2048]{1,0:T(8,128)(2,1)} async-done(((bf16[512,2048]{1,0:T(8,128)(2,1)}), bf16[128,2048]{1,0:T(8,128)(2,1)}) %reduce-scatter.6.cloned.1.call-update) | async-done | bytes 524304 | tf_op jit(solution)/shard_map/reduce_scatter | solution.py:160
  504.2 11.0 collective-permute-done.44
  651.6 9.6 collective-permute-done.55
  662.0 34.7 %collective-permute-done.56 = bf16[64,2048]{1,0:T(8,128)(2,1)S(1)} collective-permute-done((bf16[64,2048]{1,0:T(8,128)(2,1)S(1)}, bf16[64,2048]{1,0:T(8,128)(2,1)S(1)}, u32[]{:S(2)}, u32[]{:S(2)}) %collective-permute-start.56) | collective-permute-done | bytes 262176 | tf_op jit(solution)/shard_map/ppermute | solution.py:343
  770.4 8.4 collective-permute-done.66
  787.6 31.8 %collective-permute-done.67 = bf16[64,2048]{1,0:T(8,128)(2,1)S(1)} collective-permute-done((bf16[64,2048]{1,0:T(8,128)(2,1)S(1)}, bf16[64,2048]{1,0:T(8,128)(2,1)S(1)}, u32[]{:S(2)}, u32[]{:S(2)}) %collective-permute-start.67) | collective-permute-done | bytes 262176 | tf_op jit(solution)/shard_map/ppermute | solution.py:343
  819.3 9.5 collective-permute-start.71
  829.4 12.3 %collective-permute-done.69 = bf16[2,128,2048]{2,1,0:T(8,128)(2,1)S(1)} collective-permute-done((bf16[2,128,2048]{2,1,0:T(8,128)(2,1)S(1)}, bf16[2,128,2048]{2,1,0:T(8,128)(2,1)S(1)}, u32[]{:S(2)}, u32[]{:S(2)}) %collective-permute-start.69) | collective-permute-done | bytes 1048608 | tf_op jit(solution)/shard_map/ppermute | solution.py:343
  841.7 9.0 collective-permute-done.71
  866.6 18.6 %collective-permute-done.70 = bf16[128,2048]{1,0:T(8,128)(2,1)S(1)} collective-permute-done((bf16[128,2048]{1,0:T(8,128)(2,1)S(1)}, bf16[128,2048]{1,0:T(8,128)(2,1)S(1)}, u32[]{:S(2)}, u32[]{:S(2)}) %collective-permute-start.70) | collective-permute-done | bytes 524320 | tf_op jit(solution)/shard_map/ppermute | solution.py:343
  886.4 26.5 %collective-permute-done.62 = bf16[8,64,2048]{2,1,0:T(8,128)(2,1)S(1)} collective-permute-done((bf16[8,64,2048]{2,1,0:T(8,128)(2,1)S(1)}, bf16[8,64,2048]{2,1,0:T(8,128)(2,1)S(1)}, u32[]{:S(2)}, u32[]{:S(2)}) %collective-permute-start.62) | collective-permute-done | bytes 2097184 | tf_op jit(solution)/shard_map/ppermute | solution.py:111
  926.8 13.9 %collective-permute-done.75 = bf16[8,64,2048]{2,1,0:T(8,128)(2,1)} collective-permute-done((bf16[8,64,2048]{2,1,0:T(8,128)(2,1)S(1)}, bf16[8,64,2048]{2,1,0:T(8,128)(2,1)}, u32[]{:S(2)}, u32[]{:S(2)}) %collective-permute-start.75) | collective-permute-done | bytes 2097184 | tf_op jit(solution)/shard_map/ppermute | solution.py:111
  947.8 33.1 %collective-permute-start.82 = (f32[3,2048]{1,0:T(4,128)S(1)}, f32[3,2048]{1,0:T(4,128)S(1)}, u32[]{:S(2)}, u32[]{:S(2)}) collective-permute-start(f32[3,2048]{1,0:T(4,128)S(1)} %pad_maximum_fusion.15), channel_id=1, source_target_pairs={{0,1},{1,0},{2,3},{3,2},{4,5},{5,4},{6,7},{7,6},{8,9},{9,8},{10,11... | collective-permute-start | bytes 73736 | tf_op jit(solution)/shard_map/ppermute | solution.py:725
  983.3 35.8 %collective-permute-start.87 = (bf16[8,64,2048]{2,1,0:T(8,128)(2,1)S(1)}, bf16[8,64,2048]{2,1,0:T(8,128)(2,1)}, u32[]{:S(2)}, u32[]{:S(2)}) collective-permute-start(bf16[8,64,2048]{2,1,0:T(8,128)(2,1)S(1)} %broadcast_select_fusion.refs_1_), channel_id=1, source_target_pairs={{0,8},{4,12},{8,0},{12,4},{16,24},{20,28},{24,16},{28,20},{1,9},{5... | collective-permute-start | bytes 6291464 | tf_op jit(solution)/shard_map/ppermute | solution.py:343
  1021.4 11.1 collective-permute-start.78
  1036.2 28.2 %collective-permute-done.87.refs_2_ = bf16[8,64,2048]{2,1,0:T(8,128)(2,1)} collective-permute-done((bf16[8,64,2048]{2,1,0:T(8,128)(2,1)S(1)}, bf16[8,64,2048]{2,1,0:T(8,128)(2,1)}, u32[]{:S(2)}, u32[]{:S(2)}) %collective-permute-start.87) | collective-permute-done | bytes 2097184 | tf_op jit(solution)/shard_map/ppermute | solution.py:343
  1078.4 42.5 %collective-permute-done.85 = f32[3,2048]{1,0:T(4,128)S(1)} collective-permute-done((f32[3,2048]{1,0:T(4,128)S(1)}, f32[3,2048]{1,0:T(4,128)S(1)}, u32[]{:S(2)}, u32[]{:S(2)}) %collective-permute-start.85) | collective-permute-done | bytes 24608 | tf_op jit(solution)/shard_map/ppermute | solution.py:343
  1133.5 12.2 %collective-permute-done.76 = bf16[128,2048]{1,0:T(8,128)(2,1)} collective-permute-done((bf16[128,2048]{1,0:T(8,128)(2,1)}, bf16[128,2048]{1,0:T(8,128)(2,1)}, u32[]{:S(2)}, u32[]{:S(2)}) %collective-permute-start.76) | collective-permute-done | bytes 524320 | tf_op jit(solution)/shard_map/ppermute | solution.py:111
  1155.3 22.1 %place.5 = (f32[1280,2,2048]{2,1,0:T(2,128)}, f32[1280,2048]{1,0:T(8,128)}) custom-call(s32[8]{0:T(128)} %broadcast_xor_fusion.refs_0_, bf16[3,160,2048]{2,1,0:T(8,128)(2,1)} %broadcast_select_fusion.3.refs_1_, bf16[3,160,2048]{2,1,0:T(8,128)(2,1)} %collective-permute-done.60.refs_2_, bf16[3,160,2048]{2,1,0:T(8,128)(2,1)} %collective-permute-done.61.refs_3_, ...), custom_call_target="tpu_custom_call" | custom-call | bytes 47185920 | tf_op jit(solution)/shard_map/place/pallas_call | solution.py:522
  1178.3 22.7 %place.4 = (f32[3,512,2048]{2,1,0:T(8,128)}, f32[512,2048]{1,0:T(8,128)}, f32[512,2048]{1,0:T(8,128)}, f32[512,2,2048]{2,1,0:T(2,128)}, f32[512,2048]{1,0:T(8,128)}) custom-call(s32[8]{0:T(128)} %broadcast_xor_fusion.refs_0_, bf16[8,64,2048]{2,1,0:T(8,128)(2,1)} %copy-done.23, bf16[8,64,2048]{2,1,0:T(8,128)(2,1)} %collective-permute-done.87.refs_2_, ...), custom_call_target="tpu_custom_call" | custom-call | bytes 50331648 | tf_op jit(solution)/shard_map/place/pallas_call | solution.py:522
  (762 shorter events, 611.1 us)
Async XLA Ops:
  7.2 120.6 %all-gather.7.cloned.1.call-start = ((), (), s32[]{:S(2)}) async-start(), calls=%async_computation.5 | async-start | bytes 3932160 | tf_op jit(solution)/shard_map/all_gather | solution.py:447
  45.9 143.8 %all-gather.9.cloned.1.call-start = ((), (), s32[]{:S(2)}) async-start(), calls=%async_computation.6 | async-start | bytes 2621440 | tf_op jit(solution)/shard_map/all_gather | solution.py:447
  131.4 56.6 %collective-permute-start.12 = (bf16[3,160,2048]{2,1,0:T(8,128)(2,1)}, bf16[3,160,2048]{2,1,0:T(8,128)(2,1)}, u32[]{:S(2)}, u32[]{:S(2)}) collective-permute-start(bf16[3,160,2048]{2,1,0:T(8,128)(2,1)} %pad_maximum_fusion.4.refs_1_), channel_id=1, source_target_pairs={{0,8},{4,12},{8,0},{12,4},{16,24},{20,28},{24,16},{28,20},{1,9},{5... | collective-permute-start | bytes 5898248 | tf_op jit(solution)/shard_map/ppermute | solution.py:343
  145.0 135.5 %all-gather.11.cloned.1.call-start = ((), (), s32[]{:S(2)}) async-start(), calls=%async_computation.7 | async-start | bytes 2621440 | tf_op jit(solution)/shard_map/all_gather | solution.py:447
  223.1 92.8 %all-gather.13.cloned.1.call-start = ((), (), s32[]{:S(2)}) async-start(), calls=%async_computation.8 | async-start | bytes 1310720 | tf_op jit(solution)/shard_map/all_gather | solution.py:447
  225.6 54.0 %collective-permute-start.30 = (bf16[128,2048]{1,0:T(8,128)(2,1)}, bf16[128,2048]{1,0:T(8,128)(2,1)S(1)}, u32[]{:S(2)}, u32[]{:S(2)}) collective-permute-start(bf16[128,2048]{1,0:T(8,128)(2,1)} %broadcast_select_fusion.13), channel_id=1, source_target_pairs={{5,4},{10,8},{15,12},{17,16},{30,28},{27,24},{8,9},{2,1},{7,5},{28... | collective-permute-start | bytes 1572872 | tf_op jit(solution)/shard_map/ppermute | solution.py:111
  282.2 77.5 %all-gather.15.cloned.1.call-start = ((), (), s32[]{:S(2)}) async-start(), calls=%async_computation.9 | async-start | bytes 2621440 | tf_op jit(solution)/shard_map/all_gather | solution.py:156
  316.0 118.8 %all-gather.17.cloned.1.call-start = ((), (), s32[]{:S(2)}) async-start(), calls=%async_computation.10 | async-start | bytes 2621440 | tf_op jit(solution)/shard_map/all_gather | solution.py:156
  388.0 108.9 %reduce-scatter.6.cloned.1.call-start = ((), (), s32[]{:S(2)}) async-start(), calls=%async_computation.11 | async-start | bytes 2621440 | tf_op jit(solution)/shard_map/reduce_scatter | solution.py:160
  453.9 178.4 %reduce-scatter.8.cloned.1.call-start = ((), (), s32[]{:S(2)}) async-start(), calls=%async_computation.12 | async-start | bytes 17694720 | tf_op jit(solution)/shard_map/reduce_scatter | solution.py:676
  499.0 355.9 %reduce-scatter.12.cloned.1.call-start = ((), (), s32[]{:S(2)}) async-start(), calls=%async_computation.14 | async-start | bytes 5242880 | tf_op jit(solution)/shard_map/reduce_scatter | solution.py:628
  606.8 248.1 %reduce-scatter.10.cloned.1.call-start = ((), (), s32[]{:S(2)}) async-start(), calls=%async_computation.13 | async-start | bytes 5242880 | tf_op jit(solution)/shard_map/reduce_scatter | solution.py:628
  642.9 61.6 %collective-permute-start.58 = (bf16[3,160,2048]{2,1,0:T(8,128)(2,1)}, bf16[3,160,2048]{2,1,0:T(8,128)(2,1)}, u32[]{:S(2)}, u32[]{:S(2)}) collective-permute-start(bf16[3,160,2048]{2,1,0:T(8,128)(2,1)} %bitcast.64), channel_id=1, source_target_pairs={{1,5},{2,10},{3,15},{4,20},{5,17},{6,30},{7,27},{9,13},{10,2},{11,... | collective-permute-start | bytes 5898248 | tf_op jit(solution)/shard_map/ppermute | solution.py:111
  755.3 373.0 %reduce-scatter.14.cloned.1.call-start = ((), (), s32[]{:S(2)}) async-start(), calls=%async_computation.15 | async-start | bytes 2621440 | tf_op jit(solution)/shard_map/reduce_scatter | solution.py:160
  768.5 144.7 %collective-permute-start.61 = (bf16[3,160,2048]{2,1,0:T(8,128)(2,1)}, bf16[3,160,2048]{2,1,0:T(8,128)(2,1)}, u32[]{:S(2)}, u32[]{:S(2)}) collective-permute-start(bf16[3,160,2048]{2,1,0:T(8,128)(2,1)} %broadcast_select_fusion.3.refs_1_), channel_id=1, source_target_pairs={{0,16},{4,20},{8,24},{12,28},{16,0},{20,4},{24,8},{28,12},{1,17},{... | collective-permute-start | bytes 5898248 | tf_op jit(solution)/shard_map/ppermute | solution.py:343
  768.6 144.7 %collective-permute-start.60 = (bf16[3,160,2048]{2,1,0:T(8,128)(2,1)}, bf16[3,160,2048]{2,1,0:T(8,128)(2,1)}, u32[]{:S(2)}, u32[]{:S(2)}) collective-permute-start(bf16[3,160,2048]{2,1,0:T(8,128)(2,1)} %broadcast_select_fusion.3.refs_1_), channel_id=1, source_target_pairs={{0,8},{4,12},{8,0},{12,4},{16,24},{20,28},{24,16},{28,20},{1,9},{5... | collective-permute-start | bytes 5898248 | tf_op jit(solution)/shard_map/ppermute | solution.py:343
  779.7 49.3 %collective-permute-start.65 = (bf16[64,2048]{1,0:T(8,128)(2,1)S(1)}, bf16[64,2048]{1,0:T(8,128)(2,1)S(1)}, u32[]{:S(2)}, u32[]{:S(2)}) collective-permute-start(bf16[64,2048]{1,0:T(8,128)(2,1)S(1)} %fusion.99), channel_id=1, source_target_pairs={{0,16},{4,20},{8,24},{12,28},{16,0},{20,4},{24,8},{28,12},{1,17},{... | collective-permute-start | bytes 786440 | tf_op jit(solution)/shard_map/ppermute | solution.py:343
  787.4 54.3 %collective-permute-start.69 = (bf16[2,128,2048]{2,1,0:T(8,128)(2,1)S(1)}, bf16[2,128,2048]{2,1,0:T(8,128)(2,1)S(1)}, u32[]{:S(2)}, u32[]{:S(2)}) collective-permute-start(bf16[2,128,2048]{2,1,0:T(8,128)(2,1)S(1)} %slice_bitcast_fusion.4), channel_id=1, source_target_pairs={{0,8},{4,12},{8,0},{12,4},{16,24},{20,28},{24,16},{28,20},{1,9},{5... | collective-permute-start | bytes 3145736 | tf_op jit(solution)/shard_map/ppermute | solution.py:343
  856.7 56.1 %collective-permute-start.62 = (bf16[8,64,2048]{2,1,0:T(8,128)(2,1)S(1)}, bf16[8,64,2048]{2,1,0:T(8,128)(2,1)S(1)}, u32[]{:S(2)}, u32[]{:S(2)}) collective-permute-start(bf16[8,64,2048]{2,1,0:T(8,128)(2,1)S(1)} %pad_maximum_fusion.3), channel_id=1, source_target_pairs={{1,5},{2,10},{3,15},{4,20},{5,17},{6,30},{7,27},{9,13},{10,2},{11,... | collective-permute-start | bytes 6291464 | tf_op jit(solution)/shard_map/ppermute | solution.py:111
  947.2 71.9 %collective-permute-start.93 = (bf16[3,80,2048]{2,1,0:T(8,128)(2,1)}, bf16[3,80,2048]{2,1,0:T(8,128)(2,1)}, u32[]{:S(2)}, u32[]{:S(2)}) collective-permute-start(bf16[3,80,2048]{2,1,0:T(8,128)(2,1)} %collective-permute-done.74.refs_5_), channel_id=1, source_target_pairs={{0,4},{4,0},{8,12},{12,8},{16,20},{20,16},{24,28},{28,24},{1,5},{5... | collective-permute-start | bytes 2949128 | tf_op jit(solution)/shard_map/ppermute | solution.py:343
  947.7 72.4 %collective-permute-start.89 = (bf16[3,160,2048]{2,1,0:T(8,128)(2,1)}, bf16[3,160,2048]{2,1,0:T(8,128)(2,1)S(1)}, u32[]{:S(2)}, u32[]{:S(2)}) collective-permute-start(bf16[3,160,2048]{2,1,0:T(8,128)(2,1)} %broadcast_select_fusion.3.refs_1_), channel_id=1, source_target_pairs={{0,4},{4,0},{8,12},{12,8},{16,20},{20,16},{24,28},{28,24},{1,5},{5... | collective-permute-start | bytes 5898248 | tf_op jit(solution)/shard_map/ppermute | solution.py:343
  982.6 50.1 %collective-permute-start.90 = (bf16[3,160,2048]{2,1,0:T(8,128)(2,1)}, bf16[3,160,2048]{2,1,0:T(8,128)(2,1)S(1)}, u32[]{:S(2)}, u32[]{:S(2)}) collective-permute-start(bf16[3,160,2048]{2,1,0:T(8,128)(2,1)} %collective-permute-done.60.refs_2_), channel_id=1, source_target_pairs={{0,4},{4,0},{8,12},{12,8},{16,20},{20,16},{24,28},{28,24},{1,5},{5... | collective-permute-start | bytes 5898248 | tf_op jit(solution)/shard_map/ppermute | solution.py:343
  983.3 52.9 %collective-permute-start.88 = (bf16[8,64,2048]{2,1,0:T(8,128)(2,1)S(1)}, bf16[8,64,2048]{2,1,0:T(8,128)(2,1)}, u32[]{:S(2)}, u32[]{:S(2)}) collective-permute-start(bf16[8,64,2048]{2,1,0:T(8,128)(2,1)S(1)} %broadcast_select_fusion.refs_1_), channel_id=1, source_target_pairs={{0,16},{4,20},{8,24},{12,28},{16,0},{20,4},{24,8},{28,12},{1,17},{... | collective-permute-start | bytes 6291464 | tf_op jit(solution)/shard_map/ppermute | solution.py:343
  983.3 81.1 %collective-permute-start.87 = (bf16[8,64,2048]{2,1,0:T(8,128)(2,1)S(1)}, bf16[8,64,2048]{2,1,0:T(8,128)(2,1)}, u32[]{:S(2)}, u32[]{:S(2)}) collective-permute-start(bf16[8,64,2048]{2,1,0:T(8,128)(2,1)S(1)} %broadcast_select_fusion.refs_1_), channel_id=1, source_target_pairs={{0,8},{4,12},{8,0},{12,4},{16,24},{20,28},{24,16},{28,20},{1,9},{5... | collective-permute-start | bytes 6291464 | tf_op jit(solution)/shard_map/ppermute | solution.py:343
  1032.7 93.9 %collective-permute-start.81 = (bf16[256,2048]{1,0:T(8,128)(2,1)S(1)}, bf16[256,2048]{1,0:T(8,128)(2,1)S(1)}, u32[]{:S(2)}, u32[]{:S(2)}) collective-permute-start(bf16[256,2048]{1,0:T(8,128)(2,1)S(1)} %broadcast_select_fusion.4), channel_id=1, source_target_pairs={{5,1},{10,2},{15,3},{20,4},{17,5},{30,6},{27,7},{13,9},{2,10},{7,1... | collective-permute-start | bytes 3145736 | tf_op jit(solution)/shard_map/ppermute | solution.py:111
  1066.7 63.5 %collective-permute-start.95 = (bf16[8,32,2048]{2,1,0:T(8,128)(2,1)}, bf16[8,32,2048]{2,1,0:T(8,128)(2,1)}, u32[]{:S(2)}, u32[]{:S(2)}) collective-permute-start(bf16[8,32,2048]{2,1,0:T(8,128)(2,1)} %slice.392), channel_id=1, source_target_pairs={{0,8},{4,12},{8,0},{12,4},{16,24},{20,28},{24,16},{28,20},{1,9},{5... | collective-permute-start | bytes 3145736 | tf_op jit(solution)/shard_map/ppermute | solution.py:343
  1068.0 58.6 %collective-permute-start.79 = (bf16[128,2048]{1,0:T(8,128)(2,1)S(1)}, bf16[128,2048]{1,0:T(8,128)(2,1)S(1)}, u32[]{:S(2)}, u32[]{:S(2)}) collective-permute-start(bf16[128,2048]{1,0:T(8,128)(2,1)S(1)} %broadcast_select_fusion.8), channel_id=1, source_target_pairs={{5,1},{10,2},{15,3},{20,4},{17,5},{30,6},{27,7},{13,9},{2,10},{7,1... | collective-permute-start | bytes 1572872 | tf_op jit(solution)/shard_map/ppermute | solution.py:111
  1075.1 57.8 %collective-permute-start.94 = (bf16[8,32,2048]{2,1,0:T(8,128)(2,1)}, bf16[8,32,2048]{2,1,0:T(8,128)(2,1)}, u32[]{:S(2)}, u32[]{:S(2)}) collective-permute-start(bf16[8,32,2048]{2,1,0:T(8,128)(2,1)} %slice.391), channel_id=1, source_target_pairs={{0,16},{4,20},{8,24},{12,28},{16,0},{20,4},{24,8},{28,12},{1,17},{... | collective-permute-start | bytes 3145736 | tf_op jit(solution)/shard_map/ppermute | solution.py:343
  1123.7 53.7 %collective-permute-start.97 = (bf16[8,64,2048]{2,1,0:T(8,128)(2,1)}, bf16[8,64,2048]{2,1,0:T(8,128)(2,1)}, u32[]{:S(2)}, u32[]{:S(2)}) collective-permute-start(bf16[8,64,2048]{2,1,0:T(8,128)(2,1)} %collective-permute-done.87.refs_2_), channel_id=1, source_target_pairs={{0,4},{4,0},{8,12},{12,8},{16,20},{20,16},{24,28},{28,24},{1,5},{5... | collective-permute-start | bytes 6291464 | tf_op jit(solution)/shard_map/ppermute | solution.py:343
  1126.5 50.9 %collective-permute-start.98 = (bf16[8,64,2048]{2,1,0:T(8,128)(2,1)}, bf16[8,64,2048]{2,1,0:T(8,128)(2,1)}, u32[]{:S(2)}, u32[]{:S(2)}) collective-permute-start(bf16[8,64,2048]{2,1,0:T(8,128)(2,1)} %collective-permute-done.88.refs_3_), channel_id=1, source_target_pairs={{0,4},{4,0},{8,12},{12,8},{16,20},{20,16},{24,28},{28,24},{1,5},{5... | collective-permute-start | bytes 6291464 | tf_op jit(solution)/shard_map/ppermute | solution.py:343
  1128.3 49.1 %collective-permute-start.96 = (bf16[8,64,2048]{2,1,0:T(8,128)(2,1)S(1)}, bf16[8,64,2048]{2,1,0:T(8,128)(2,1)}, u32[]{:S(2)}, u32[]{:S(2)}) collective-permute-start(bf16[8,64,2048]{2,1,0:T(8,128)(2,1)S(1)} %broadcast_select_fusion.refs_1_), channel_id=1, source_target_pairs={{0,4},{4,0},{8,12},{12,8},{16,20},{20,16},{24,28},{28,24},{1,5},{5... | collective-permute-start | bytes 6291464 | tf_op jit(solution)/shard_map/ppermute | solution.py:343
  1148.8 52.2 %collective-permute-start.77 = (bf16[128,2048]{1,0:T(8,128)(2,1)S(1)}, bf16[128,2048]{1,0:T(8,128)(2,1)S(1)}, u32[]{:S(2)}, u32[]{:S(2)}) collective-permute-start(bf16[128,2048]{1,0:T(8,128)(2,1)S(1)} %broadcast_select_fusion.11), channel_id=1, source_target_pairs={{5,1},{10,2},{15,3},{20,4},{17,5},{30,6},{27,7},{13,9},{2,10},{7,1... | collective-permute-start | bytes 1572872 | tf_op jit(solution)/shard_map/ppermute | solution.py:111
  (207 other events, 3852.4 us)
Sparse Core Ops, SparseCore 0:
  46.0 61.7 all-gather.6
  145.1 44.4 all-gather.8
  223.2 53.9 all-gather.10
  282.4 26.9 all-gather.12
  316.1 43.6 all-gather.14
  388.1 46.5 all-gather.16
  454.0 42.7 reduce-scatter.5
  500.9 114.5 reduce-scatter.7
  618.4 77.3 reduce-scatter.11
  755.5 82.8 reduce-scatter.9
  944.7 74.0 reduce-scatter.13
